TPU v7x, 32 devices: a whole 2x2x4 slice. The times are simulated.
32 devices in a mesh: tile: 8 (over y, x, core), crm: 4 (over z).
Axes of the slice: x: 2, y: 2, z: 4, core: 2. Of those that a mesh axis runs over, the one named last changes fastest.
Arguments:
- thermal_anomaly: float32 [72, 8192], P(None, ('tile', 'crm')), may hold values from -6 to 6
- vapour_anomaly: float32 [72, 8192], P(None, ('tile', 'crm')), may hold values from -6 to 6
- periodic_flow_velocity: float32 [72, 8192], P(None, ('tile', 'crm')), may hold values from -0.8 to 0.8
- processor_assignment: int32 [8192], P(('tile', 'crm')), may hold values from 0 to 31, as said below
- thermal_disturbance: float32 [50, 32, 8192], P(None, None, ('tile', 'crm')), may hold values from -8 to 8
- layer_index_downscale: float32 [50, 72], replicated, may hold values from -0.75 to 0.75
- layer_index_upscale: float32 [72, 50], replicated, may hold values from -0.875 to 0.875
Outputs:
- thermal_after_step: float32 [72, 8192], P(None, ('tile', 'crm'))
- vapour_after_step: float32 [72, 8192], P(None, ('tile', 'crm'))
- cloud_water: float32 [72, 8192], P(None, ('tile', 'crm'))
Inputs may be any that keep to these rules, and one draw needn't show every extreme that they name: `processor_assignment`: the 256 columns of each device go exactly 8 to each owner device; owners are numbered in the order of tile, then crm.
All inputs are finite; a program needn't handle non-finite values.
Results may differ from a plain program's by a relative error of at most 0.0003.
Values sent between devices are 32-bit elements; how exact they have to be, the bound alone decides.
No kernel may reach another device: no remote copies, remote signals or barrier semaphores. Data moves between devices by JAX's collectives and lax.ppermute only.
A program may use at most 64 MiB of HBM per device.

v0:
```python
import jax
import jax.numpy as jnp
from jax import lax
from jax.sharding import PartitionSpec as P

SUBSTEPS = 10


loop_diff = 0.35
mix_along = 0.35
mix_vertical = 0.1
cond_rate = 0.1
latent_heat = 1.5
max_speed = 0.8


def extended(block, sides, width):
    for axis, dim in sides:
        count = lax.axis_size(axis)
        forward = [(i, i + 1) for i in range(count - 1)]
        forward.append((count - 1, 0))
        backward = [(target, source) for source, target in forward]
        low = lax.ppermute(
            lax.slice_in_dim(block, block.shape[dim] - width, None, axis=dim), axis, forward
        )
        high = lax.ppermute(lax.slice_in_dim(block, 0, width, axis=dim), axis, backward)
        block = jnp.concatenate([low, block, high], axis=dim)
    return block


def transport(field_in, advect_speed):
    eastward = jnp.roll(field_in, -1, axis=1)
    westward = jnp.roll(field_in, 1, axis=1)
    level_above = jnp.concatenate([field_in[1:], field_in[-1:]], axis=0)
    level_below = jnp.concatenate([field_in[:1], field_in[:-1]], axis=0)
    return (
        field_in
        - advect_speed * (eastward - westward) * 0.5
        + mix_along * (eastward - 2.0 * field_in + westward)
        + mix_vertical * (level_above - 2.0 * field_in + level_below)
    )


def cloud_model(profiles, thermal_disturbance):
    temp_prof, water_prof, wind_prof, force_temp, force_water = (
        profiles[0],
        profiles[1],
        profiles[2],
        profiles[3],
        profiles[4],
    )
    advect_speed = (max_speed * jnp.tanh(wind_prof))[:, None, :]
    theta_state = temp_prof[:, None, :] + thermal_disturbance
    water_state = jnp.broadcast_to(water_prof[:, None, :], thermal_disturbance.shape)

    def substep(step_index, carry):
        theta_old, water_old = carry
        condense = cond_rate * jax.nn.softplus(water_old - 0.5 * theta_old)
        theta_new = (
            transport(theta_old, advect_speed)
            + force_temp[:, None, :] / SUBSTEPS
            + latent_heat * condense
        )
        water_new = (
            transport(water_old, advect_speed) + force_water[:, None, :] / SUBSTEPS - condense
        )
        return (theta_new, water_new)

    theta_state, water_state = lax.fori_loop(0, SUBSTEPS, substep, (theta_state, water_state))
    delta_temp = jnp.mean(theta_state, axis=1) - temp_prof
    delta_water = jnp.mean(water_state, axis=1) - water_prof
    cloud_mean = jnp.mean(jax.nn.softplus(water_state - 0.5 * theta_state), axis=1)
    return jnp.stack([delta_temp, delta_water, cloud_mean])


def local(
    thermal_anomaly,
    vapour_anomaly,
    periodic_flow_velocity,
    processor_assignment,
    thermal_disturbance,
    layer_index_downscale,
    layer_index_upscale,
):
    resident_verticals = thermal_anomaly.shape[1]
    tiles = lax.axis_size("tile")
    owners_tile = lax.axis_size("crm")
    devices = tiles * owners_tile
    per_peer = resident_verticals // devices
    coupled_soundings = jnp.stack([thermal_anomaly, vapour_anomaly])
    padded = extended(coupled_soundings, ((("tile", "crm"), 2),), 1)
    ahead = padded[:, :, 2:]
    behind = padded[:, :, :-2]
    shifted_quantities = -periodic_flow_velocity[None] * (ahead - behind) * 0.5 + loop_diff * (
        ahead - 2.0 * coupled_soundings + behind
    )
    prognostic_variables = jnp.stack(
        [
            thermal_anomaly,
            vapour_anomaly,
            periodic_flow_velocity,
            shifted_quantities[0],
            shifted_quantities[1],
        ]
    )
    onehot = (
        processor_assignment[:, None] == jnp.arange(devices, dtype=jnp.int32)[None, :]
    ).astype(jnp.int32)
    rank_here = jnp.sum((jnp.cumsum(onehot, axis=0) - 1) * onehot, axis=1)
    position = processor_assignment * per_peer + rank_here
    ordering = (
        jnp.zeros((resident_verticals,), jnp.int32)
        .at[position]
        .set(jnp.arange(resident_verticals, dtype=jnp.int32))
    )
    prognostic_variables = jnp.einsum(
        "zl,flc->fzc", layer_index_downscale, prognostic_variables, precision=lax.Precision.HIGHEST
    )
    depth = prognostic_variables.shape[1]
    outgoing = jnp.take(prognostic_variables, ordering, axis=2)
    outgoing = outgoing.reshape(5, depth, devices, per_peer)
    incoming = lax.all_to_all(outgoing, ("tile", "crm"), split_axis=2, concat_axis=2, tiled=True)
    incoming = incoming.reshape(5, depth, resident_verticals)
    result = cloud_model(incoming, thermal_disturbance)
    depth_back = result.shape[1]
    returning = result.reshape(3, depth_back, devices, per_peer)
    gathered_rate_changes = lax.all_to_all(
        returning, ("tile", "crm"), split_axis=2, concat_axis=2, tiled=True
    )
    gathered_rate_changes = gathered_rate_changes.reshape(3, depth_back, resident_verticals)
    gathered_rate_changes = jnp.take(gathered_rate_changes, position, axis=2)
    gathered_rate_changes = jnp.einsum(
        "lz,fzc->flc", layer_index_upscale, gathered_rate_changes, precision=lax.Precision.HIGHEST
    )
    thermal_after_step = thermal_anomaly + shifted_quantities[0] + gathered_rate_changes[0]
    vapour_after_step = vapour_anomaly + shifted_quantities[1] + gathered_rate_changes[1]
    return (thermal_after_step, vapour_after_step, gathered_rate_changes[2])


def solution(mesh):
    in_specs = (
        P(None, ("tile", "crm")),
        P(None, ("tile", "crm")),
        P(None, ("tile", "crm")),
        P(("tile", "crm")),
        P(None, None, ("tile", "crm")),
        P(),
        P(),
    )
    out_specs = (P(None, ("tile", "crm")), P(None, ("tile", "crm")), P(None, ("tile", "crm")))
    return jax.shard_map(local, mesh=mesh, in_specs=in_specs, out_specs=out_specs, check_vma=False)
```

profile of v0, /device:TPU:0, one launch (start us, length us, event | category | flops | bytes accessed | tf_op | source)
XLA Modules:
  0.0 124.3 jit_solution(10347198882309978848)
XLA Ops:
  0.6 0.9 fusion.27
  1.6 6.5 %collective-permute-start = (f32[2,72,1]{2,1,0:T(8,128)S(1)}, f32[2,72,1]{2,1,0:T(8,128)S(1)}, u32[]{:S(2)}, u32[]{:S(2)}) collective-permute-start(f32[2,72,1]{2,1,0:T(8,128)S(1)} %get-tuple-element.148), channel_id=1, source_target_pairs={{1,0},{2,1},{3,2},{4,3},{5,4},{6,5},{7,6},{8,7},{9,8},{10,9},{11,1... | collective-permute-start | bytes 1736 | tf_op jit(solution)/shard_map/ppermute | solution.py:26
  11.0 1.4 %scatter_custom_fusion = s32[256]{0:T(256)S(1)} fusion(s32[256]{0:T(256)S(1)} %get-tuple-element.111, s32[256]{0:T(256)S(1)} %iota.11, s32[]{:T(128)} %copy.59), kind=kCustom, calls=%fused_computation.92 | custom fusion | bytes 1028 | tf_op jit(solution)/shard_map/scatter | solution.py:114
  12.4 0.9 neg.14
  13.4 2.0 %collective-permute-done.1 = f32[2,72,1]{2,1,0:T(8,128)S(1)} collective-permute-done((f32[2,72,1]{2,1,0:T(8,128)S(1)}, f32[2,72,1]{2,1,0:T(8,128)S(1)}, u32[]{:S(2)}, u32[]{:S(2)}) %collective-permute-start.1) | collective-permute-done | bytes 608 | tf_op jit(solution)/shard_map/ppermute | solution.py:23
  15.4 1.2 fusion.23
  17.3 1.3 %convolution_bitcast_fusion = f32[5,50,256]{2,1,0:T(8,128)S(1)} fusion(f32[2,72,256]{2,1,0:T(8,128)S(1)} %fusion.23, f32[1,72,256]{2,1,0:T(8,128)} %bitcast.109, f32[1,72,256]{2,1,0:T(8,128)} %bitcast.104, f32[1,72,256]{2,1,0:T(8,128)} %bitcast.107, f32[50,72]{1,0:T(8,128)S(1)} %copy-done), kind=kOutput, calls=%fused_computation.24 | convolution fusion | flops 55572480 | bytes 639040 | tf_op jit(solution)/shard_map/zl,flc->fzc/dot_general | solution.py:116
  19.1 1.0 gather_fusion
  20.3 0.9 reshape.175
  21.3 13.8 %all_to_all.10 = f32[32,1,2000]{2,1,0:T(1,128)S(1)} all-to-all(f32[32,1,2000]{2,1,0:T(1,128)S(1)} %reshape.175), channel_id=1, replica_groups=mesh['tile'=8,'crm'=4] {'tile','crm'}, dimensions={0} | all-to-all | bytes 512000 | tf_op jit(solution)/shard_map/all_to_all | solution.py:122
  35.6 1.3 %reduce.2 = f32[32,2000]{1,0:T(8,128)S(1)} reduce(f32[32,1,2000]{2,1,0:T(1,128)S(1)} %all_to_all.10, f32[]{:T(128)} %broadcast.168), dimensions={1}, to_apply=%all_to_all.6.reduce_sub_computation | reduce | bytes 512004 | tf_op jit(solution)/shard_map/all_to_all | solution.py:122
  39.5 64.5 %while.14 = (s32[]{:T(128)}, f32[50,32,256]{2,1,0:T(8,128)S(1)}, f32[50,32,256]{2,1,0:T(8,128)S(1)}, f32[50,1,256]{2,0,1:T(8,128)S(1)}, f32[1,50,256]{2,1,0:T(8,128)S(1)}, /*index=5*/f32[1,50,256]{2,1,0:T(8,128)S(1)}, s32[]{:T(128)}) while((s32[]{:T(128)}, f32[50,32,256]{2,1,0:T(8,128)S(1)}, f32[50,32,256]{2,1,0:T(8,128)S(1)}, ...), condition=%wide.region_5.6_spmd, body=%wide.region_4.5_spmd.sunk | while | flops 22963200 | bytes 52838476 | solution.py:69
  39.5 0.8 fusion.58
  41.3 2.2 %fusion.61 = f32[50,32,256]{2,1,0:T(8,128)S(1)} fusion(f32[1,32,256]{2,1,0:T(8,128)S(1)} %get-tuple-element.215, f32[49,32,256]{2,1,0:T(8,128)S(1)} %get-tuple-element.216, f32[49,32,256]{2,1,0:T(8,128)S(1)} %get-tuple-element.217, f32[1,32,256]{2,1,0:T(8,128)S(1)} %get-tuple-element.218, f32[50,32,256]{2,1,0:T(8,128)S(1)} %get-tuple-element.233, ...), kind=kLoop, calls=%fused_computation.19.clone.1 | loop fusion | flops 11468800 | bytes 11571200 | tf_op jit(solution)/shard_map/while/body/eval_jaxpr/sub | solution.py:65
  43.5 2.3 %fusion.60 = f32[50,32,256]{2,1,0:T(8,128)S(1)} fusion(f32[1,32,256]{2,1,0:T(8,128)S(1)} %get-tuple-element.206, f32[49,32,256]{2,1,0:T(8,128)S(1)} %get-tuple-element.207, f32[49,32,256]{2,1,0:T(8,128)S(1)} %get-tuple-element.208, f32[1,32,256]{2,1,0:T(8,128)S(1)} %get-tuple-element.209, f32[50,32,256]{2,1,0:T(8,128)S(1)} %get-tuple-element.232, ...), kind=kLoop, calls=%fused_computation.11.clone.1 | loop fusion | flops 11468800 | bytes 11571200 | tf_op jit(solution)/shard_map/while/body/eval_jaxpr/add | solution.py:60
  45.9 0.8 fusion.58
  47.7 2.2 %fusion.61 = f32[50,32,256]{2,1,0:T(8,128)S(1)} fusion(f32[1,32,256]{2,1,0:T(8,128)S(1)} %get-tuple-element.215, f32[49,32,256]{2,1,0:T(8,128)S(1)} %get-tuple-element.216, f32[49,32,256]{2,1,0:T(8,128)S(1)} %get-tuple-element.217, f32[1,32,256]{2,1,0:T(8,128)S(1)} %get-tuple-element.218, f32[50,32,256]{2,1,0:T(8,128)S(1)} %get-tuple-element.233, ...), kind=kLoop, calls=%fused_computation.19.clone.1 | loop fusion | flops 11468800 | bytes 11571200 | tf_op jit(solution)/shard_map/while/body/eval_jaxpr/sub | solution.py:65
  50.0 2.3 %fusion.60 = f32[50,32,256]{2,1,0:T(8,128)S(1)} fusion(f32[1,32,256]{2,1,0:T(8,128)S(1)} %get-tuple-element.206, f32[49,32,256]{2,1,0:T(8,128)S(1)} %get-tuple-element.207, f32[49,32,256]{2,1,0:T(8,128)S(1)} %get-tuple-element.208, f32[1,32,256]{2,1,0:T(8,128)S(1)} %get-tuple-element.209, f32[50,32,256]{2,1,0:T(8,128)S(1)} %get-tuple-element.232, ...), kind=kLoop, calls=%fused_computation.11.clone.1 | loop fusion | flops 11468800 | bytes 11571200 | tf_op jit(solution)/shard_map/while/body/eval_jaxpr/add | solution.py:60
  52.4 0.8 fusion.58
  54.2 2.2 %fusion.61 = f32[50,32,256]{2,1,0:T(8,128)S(1)} fusion(f32[1,32,256]{2,1,0:T(8,128)S(1)} %get-tuple-element.215, f32[49,32,256]{2,1,0:T(8,128)S(1)} %get-tuple-element.216, f32[49,32,256]{2,1,0:T(8,128)S(1)} %get-tuple-element.217, f32[1,32,256]{2,1,0:T(8,128)S(1)} %get-tuple-element.218, f32[50,32,256]{2,1,0:T(8,128)S(1)} %get-tuple-element.233, ...), kind=kLoop, calls=%fused_computation.19.clone.1 | loop fusion | flops 11468800 | bytes 11571200 | tf_op jit(solution)/shard_map/while/body/eval_jaxpr/sub | solution.py:65
  56.4 2.3 %fusion.60 = f32[50,32,256]{2,1,0:T(8,128)S(1)} fusion(f32[1,32,256]{2,1,0:T(8,128)S(1)} %get-tuple-element.206, f32[49,32,256]{2,1,0:T(8,128)S(1)} %get-tuple-element.207, f32[49,32,256]{2,1,0:T(8,128)S(1)} %get-tuple-element.208, f32[1,32,256]{2,1,0:T(8,128)S(1)} %get-tuple-element.209, f32[50,32,256]{2,1,0:T(8,128)S(1)} %get-tuple-element.232, ...), kind=kLoop, calls=%fused_computation.11.clone.1 | loop fusion | flops 11468800 | bytes 11571200 | tf_op jit(solution)/shard_map/while/body/eval_jaxpr/add | solution.py:60
  58.8 0.8 fusion.58
  60.6 2.2 %fusion.61 = f32[50,32,256]{2,1,0:T(8,128)S(1)} fusion(f32[1,32,256]{2,1,0:T(8,128)S(1)} %get-tuple-element.215, f32[49,32,256]{2,1,0:T(8,128)S(1)} %get-tuple-element.216, f32[49,32,256]{2,1,0:T(8,128)S(1)} %get-tuple-element.217, f32[1,32,256]{2,1,0:T(8,128)S(1)} %get-tuple-element.218, f32[50,32,256]{2,1,0:T(8,128)S(1)} %get-tuple-element.233, ...), kind=kLoop, calls=%fused_computation.19.clone.1 | loop fusion | flops 11468800 | bytes 11571200 | tf_op jit(solution)/shard_map/while/body/eval_jaxpr/sub | solution.py:65
  62.9 2.3 %fusion.60 = f32[50,32,256]{2,1,0:T(8,128)S(1)} fusion(f32[1,32,256]{2,1,0:T(8,128)S(1)} %get-tuple-element.206, f32[49,32,256]{2,1,0:T(8,128)S(1)} %get-tuple-element.207, f32[49,32,256]{2,1,0:T(8,128)S(1)} %get-tuple-element.208, f32[1,32,256]{2,1,0:T(8,128)S(1)} %get-tuple-element.209, f32[50,32,256]{2,1,0:T(8,128)S(1)} %get-tuple-element.232, ...), kind=kLoop, calls=%fused_computation.11.clone.1 | loop fusion | flops 11468800 | bytes 11571200 | tf_op jit(solution)/shard_map/while/body/eval_jaxpr/add | solution.py:60
  65.3 0.8 fusion.58
  67.1 2.2 %fusion.61 = f32[50,32,256]{2,1,0:T(8,128)S(1)} fusion(f32[1,32,256]{2,1,0:T(8,128)S(1)} %get-tuple-element.215, f32[49,32,256]{2,1,0:T(8,128)S(1)} %get-tuple-element.216, f32[49,32,256]{2,1,0:T(8,128)S(1)} %get-tuple-element.217, f32[1,32,256]{2,1,0:T(8,128)S(1)} %get-tuple-element.218, f32[50,32,256]{2,1,0:T(8,128)S(1)} %get-tuple-element.233, ...), kind=kLoop, calls=%fused_computation.19.clone.1 | loop fusion | flops 11468800 | bytes 11571200 | tf_op jit(solution)/shard_map/while/body/eval_jaxpr/sub | solution.py:65
  69.3 2.3 %fusion.60 = f32[50,32,256]{2,1,0:T(8,128)S(1)} fusion(f32[1,32,256]{2,1,0:T(8,128)S(1)} %get-tuple-element.206, f32[49,32,256]{2,1,0:T(8,128)S(1)} %get-tuple-element.207, f32[49,32,256]{2,1,0:T(8,128)S(1)} %get-tuple-element.208, f32[1,32,256]{2,1,0:T(8,128)S(1)} %get-tuple-element.209, f32[50,32,256]{2,1,0:T(8,128)S(1)} %get-tuple-element.232, ...), kind=kLoop, calls=%fused_computation.11.clone.1 | loop fusion | flops 11468800 | bytes 11571200 | tf_op jit(solution)/shard_map/while/body/eval_jaxpr/add | solution.py:60
  71.7 0.8 fusion.58
  73.5 2.2 %fusion.61 = f32[50,32,256]{2,1,0:T(8,128)S(1)} fusion(f32[1,32,256]{2,1,0:T(8,128)S(1)} %get-tuple-element.215, f32[49,32,256]{2,1,0:T(8,128)S(1)} %get-tuple-element.216, f32[49,32,256]{2,1,0:T(8,128)S(1)} %get-tuple-element.217, f32[1,32,256]{2,1,0:T(8,128)S(1)} %get-tuple-element.218, f32[50,32,256]{2,1,0:T(8,128)S(1)} %get-tuple-element.233, ...), kind=kLoop, calls=%fused_computation.19.clone.1 | loop fusion | flops 11468800 | bytes 11571200 | tf_op jit(solution)/shard_map/while/body/eval_jaxpr/sub | solution.py:65
  75.8 2.3 %fusion.60 = f32[50,32,256]{2,1,0:T(8,128)S(1)} fusion(f32[1,32,256]{2,1,0:T(8,128)S(1)} %get-tuple-element.206, f32[49,32,256]{2,1,0:T(8,128)S(1)} %get-tuple-element.207, f32[49,32,256]{2,1,0:T(8,128)S(1)} %get-tuple-element.208, f32[1,32,256]{2,1,0:T(8,128)S(1)} %get-tuple-element.209, f32[50,32,256]{2,1,0:T(8,128)S(1)} %get-tuple-element.232, ...), kind=kLoop, calls=%fused_computation.11.clone.1 | loop fusion | flops 11468800 | bytes 11571200 | tf_op jit(solution)/shard_map/while/body/eval_jaxpr/add | solution.py:60
  78.2 0.8 fusion.58
  80.0 2.2 %fusion.61 = f32[50,32,256]{2,1,0:T(8,128)S(1)} fusion(f32[1,32,256]{2,1,0:T(8,128)S(1)} %get-tuple-element.215, f32[49,32,256]{2,1,0:T(8,128)S(1)} %get-tuple-element.216, f32[49,32,256]{2,1,0:T(8,128)S(1)} %get-tuple-element.217, f32[1,32,256]{2,1,0:T(8,128)S(1)} %get-tuple-element.218, f32[50,32,256]{2,1,0:T(8,128)S(1)} %get-tuple-element.233, ...), kind=kLoop, calls=%fused_computation.19.clone.1 | loop fusion | flops 11468800 | bytes 11571200 | tf_op jit(solution)/shard_map/while/body/eval_jaxpr/sub | solution.py:65
  82.2 2.3 %fusion.60 = f32[50,32,256]{2,1,0:T(8,128)S(1)} fusion(f32[1,32,256]{2,1,0:T(8,128)S(1)} %get-tuple-element.206, f32[49,32,256]{2,1,0:T(8,128)S(1)} %get-tuple-element.207, f32[49,32,256]{2,1,0:T(8,128)S(1)} %get-tuple-element.208, f32[1,32,256]{2,1,0:T(8,128)S(1)} %get-tuple-element.209, f32[50,32,256]{2,1,0:T(8,128)S(1)} %get-tuple-element.232, ...), kind=kLoop, calls=%fused_computation.11.clone.1 | loop fusion | flops 11468800 | bytes 11571200 | tf_op jit(solution)/shard_map/while/body/eval_jaxpr/add | solution.py:60
  84.6 0.8 fusion.58
  86.4 2.2 %fusion.61 = f32[50,32,256]{2,1,0:T(8,128)S(1)} fusion(f32[1,32,256]{2,1,0:T(8,128)S(1)} %get-tuple-element.215, f32[49,32,256]{2,1,0:T(8,128)S(1)} %get-tuple-element.216, f32[49,32,256]{2,1,0:T(8,128)S(1)} %get-tuple-element.217, f32[1,32,256]{2,1,0:T(8,128)S(1)} %get-tuple-element.218, f32[50,32,256]{2,1,0:T(8,128)S(1)} %get-tuple-element.233, ...), kind=kLoop, calls=%fused_computation.19.clone.1 | loop fusion | flops 11468800 | bytes 11571200 | tf_op jit(solution)/shard_map/while/body/eval_jaxpr/sub | solution.py:65
  88.7 2.3 %fusion.60 = f32[50,32,256]{2,1,0:T(8,128)S(1)} fusion(f32[1,32,256]{2,1,0:T(8,128)S(1)} %get-tuple-element.206, f32[49,32,256]{2,1,0:T(8,128)S(1)} %get-tuple-element.207, f32[49,32,256]{2,1,0:T(8,128)S(1)} %get-tuple-element.208, f32[1,32,256]{2,1,0:T(8,128)S(1)} %get-tuple-element.209, f32[50,32,256]{2,1,0:T(8,128)S(1)} %get-tuple-element.232, ...), kind=kLoop, calls=%fused_computation.11.clone.1 | loop fusion | flops 11468800 | bytes 11571200 | tf_op jit(solution)/shard_map/while/body/eval_jaxpr/add | solution.py:60
  92.9 2.2 %fusion.61 = f32[50,32,256]{2,1,0:T(8,128)S(1)} fusion(f32[1,32,256]{2,1,0:T(8,128)S(1)} %get-tuple-element.215, f32[49,32,256]{2,1,0:T(8,128)S(1)} %get-tuple-element.216, f32[49,32,256]{2,1,0:T(8,128)S(1)} %get-tuple-element.217, f32[1,32,256]{2,1,0:T(8,128)S(1)} %get-tuple-element.218, f32[50,32,256]{2,1,0:T(8,128)S(1)} %get-tuple-element.233, ...), kind=kLoop, calls=%fused_computation.19.clone.1 | loop fusion | flops 11468800 | bytes 11571200 | tf_op jit(solution)/shard_map/while/body/eval_jaxpr/sub | solution.py:65
  95.1 2.3 %fusion.60 = f32[50,32,256]{2,1,0:T(8,128)S(1)} fusion(f32[1,32,256]{2,1,0:T(8,128)S(1)} %get-tuple-element.206, f32[49,32,256]{2,1,0:T(8,128)S(1)} %get-tuple-element.207, f32[49,32,256]{2,1,0:T(8,128)S(1)} %get-tuple-element.208, f32[1,32,256]{2,1,0:T(8,128)S(1)} %get-tuple-element.209, f32[50,32,256]{2,1,0:T(8,128)S(1)} %get-tuple-element.232, ...), kind=kLoop, calls=%fused_computation.11.clone.1 | loop fusion | flops 11468800 | bytes 11571200 | tf_op jit(solution)/shard_map/while/body/eval_jaxpr/add | solution.py:60
  97.5 0.8 fusion.58
  99.4 2.2 %fusion.61 = f32[50,32,256]{2,1,0:T(8,128)S(1)} fusion(f32[1,32,256]{2,1,0:T(8,128)S(1)} %get-tuple-element.215, f32[49,32,256]{2,1,0:T(8,128)S(1)} %get-tuple-element.216, f32[49,32,256]{2,1,0:T(8,128)S(1)} %get-tuple-element.217, f32[1,32,256]{2,1,0:T(8,128)S(1)} %get-tuple-element.218, f32[50,32,256]{2,1,0:T(8,128)S(1)} %get-tuple-element.233, ...), kind=kLoop, calls=%fused_computation.19.clone.1 | loop fusion | flops 11468800 | bytes 11571200 | tf_op jit(solution)/shard_map/while/body/eval_jaxpr/sub | solution.py:65
  101.6 2.3 %fusion.60 = f32[50,32,256]{2,1,0:T(8,128)S(1)} fusion(f32[1,32,256]{2,1,0:T(8,128)S(1)} %get-tuple-element.206, f32[49,32,256]{2,1,0:T(8,128)S(1)} %get-tuple-element.207, f32[49,32,256]{2,1,0:T(8,128)S(1)} %get-tuple-element.208, f32[1,32,256]{2,1,0:T(8,128)S(1)} %get-tuple-element.209, f32[50,32,256]{2,1,0:T(8,128)S(1)} %get-tuple-element.232, ...), kind=kLoop, calls=%fused_computation.11.clone.1 | loop fusion | flops 11468800 | bytes 11571200 | tf_op jit(solution)/shard_map/while/body/eval_jaxpr/add | solution.py:60
  104.0 1.4 %fusion.40 = (f32[50,256]{1,0:T(8,128)S(1)}, f32[50,256]{1,0:T(8,128)S(1)}, f32[50,256]{1,0:T(8,128)S(1)}) fusion(f32[50,32,256]{2,1,0:T(8,128)S(1)} %get-tuple-element.81, f32[50,32,256]{2,1,0:T(8,128)S(1)} %get-tuple-element.82), kind=kLoop, calls=%fused_computation.95 | loop fusion | flops 4467200 | bytes 3430400 | tf_op jit(solution)/shard_map/reduce_sum | solution.py:70
  105.8 1.0 bitcast_subtract_fusion.1
  106.9 1.1 reshape.177
  107.9 2.7 %all-to-all-start.1 = ((f32[32,1,1200]{2,1,0:T(1,128)}), f32[32,1,1200]{2,1,0:T(1,128)S(1)}, u32[]{:S(2)}, u32[]{:S(2)}) async-start(f32[32,1,1200]{2,1,0:T(1,128)} %reshape.177), calls=%async_computation.1 | async-start | bytes 327680 | tf_op jit(solution)/shard_map/all_to_all | solution.py:127
  110.6 8.8 %all-to-all-done.1 = f32[32,1,1200]{2,1,0:T(1,128)S(1)} async-done(((f32[32,1,1200]{2,1,0:T(1,128)}), f32[32,1,1200]{2,1,0:T(1,128)S(1)}, u32[]{:S(2)}, u32[]{:S(2)}) %all-to-all-start.1) | async-done | bytes 153632 | tf_op jit(solution)/shard_map/all_to_all | solution.py:127
  119.4 1.0 reduce.3
  121.0 1.0 gather_fusion.1
  (109 shorter events, 22.2 us)
Async XLA Ops:
  0.6 16.7 %copy-start = (f32[50,72]{1,0:T(8,128)S(1)}, f32[50,72]{1,0:T(8,128)}, u32[]{:S(2)}) copy-start(f32[50,72]{1,0:T(8,128)} %param.14) | copy-start | bytes 43204
  1.6 11.8 %collective-permute-start = (f32[2,72,1]{2,1,0:T(8,128)S(1)}, f32[2,72,1]{2,1,0:T(8,128)S(1)}, u32[]{:S(2)}, u32[]{:S(2)}) collective-permute-start(f32[2,72,1]{2,1,0:T(8,128)S(1)} %get-tuple-element.148), channel_id=1, source_target_pairs={{1,0},{2,1},{3,2},{4,3},{5,4},{6,5},{7,6},{8,7},{9,8},{10,9},{11,1... | collective-permute-start | bytes 1736 | tf_op jit(solution)/shard_map/ppermute | solution.py:26
  8.0 7.4 %collective-permute-start.1 = (f32[2,72,1]{2,1,0:T(8,128)S(1)}, f32[2,72,1]{2,1,0:T(8,128)S(1)}, u32[]{:S(2)}, u32[]{:S(2)}) collective-permute-start(f32[2,72,1]{2,1,0:T(8,128)S(1)} %get-tuple-element.147), channel_id=1, source_target_pairs={{0,1},{1,2},{2,3},{3,4},{4,5},{5,6},{6,7},{7,8},{8,9},{9,10},{10,1... | collective-permute-start | bytes 1736 | tf_op jit(solution)/shard_map/ppermute | solution.py:23
  16.6 0.7 copy-start.3
  36.8 1.7 %copy-start.2 = (f32[50,32,256]{2,1,0:T(8,128)S(1)}, f32[50,32,256]{2,1,0:T(8,128)}, u32[]{:S(2)}) copy-start(f32[50,32,256]{2,1,0:T(8,128)} %param.13) | copy-start | bytes 4915204
  37.1 0.9 copy-start.1
  38.5 0.8 copy-start.7
  107.9 11.5 %all-to-all-start.1 = ((f32[32,1,1200]{2,1,0:T(1,128)}), f32[32,1,1200]{2,1,0:T(1,128)S(1)}, u32[]{:S(2)}, u32[]{:S(2)}) async-start(f32[32,1,1200]{2,1,0:T(1,128)} %reshape.177), calls=%async_computation.1 | async-start | bytes 327680 | tf_op jit(solution)/shard_map/all_to_all | solution.py:127
  120.7 1.7 %copy-start.8 = (f32[72,50]{0,1:T(8,128)S(1)}, f32[72,50]{0,1:T(8,128)}, u32[]{:S(2)}) copy-start(f32[72,50]{0,1:T(8,128)} %param.15) | copy-start | bytes 43204
  120.7 2.2 %copy-start.4 = (f32[2,72,256]{2,1,0:T(8,128)S(1)}, f32[2,72,256]{2,1,0:T(8,128)}, u32[]{:S(2)}) copy-start(f32[2,72,256]{2,1,0:T(8,128)} %copy-done.3) | copy-start | bytes 442372
  120.7 2.2 %copy-start.5 = (f32[72,256]{1,0:T(8,128)S(1)}, f32[72,256]{1,0:T(8,128)}, u32[]{:S(2)}) copy-start(f32[72,256]{1,0:T(8,128)} %param.10) | copy-start | bytes 221188
  120.7 2.2 %copy-start.6 = (f32[72,256]{1,0:T(8,128)S(1)}, f32[72,256]{1,0:T(8,128)}, u32[]{:S(2)}) copy-start(f32[72,256]{1,0:T(8,128)} %param.9) | copy-start | bytes 221188
where the time goes:
time: 125 us; the launch traced here: 124 us
  other arithmetic  57.4 us (46%)
  local copies, waits for them, and re-layouts  29.6 us (24%)
  blocking collectives  13.8 us (11%)
  waiting for transfers between devices  10.8 us (9%)
  starting transfers between devices  9.12 us (7%)
  matrix products  1.92 us (2%)
    add x10, other arithmetic, substep(): transport(theta_old, advect_speed) + force_temp[:, None, :] / SUBSTEPS  22.8 us
    sub x10, other arithmetic, substep(): transport(water_old, advect_speed) + force_water[:, None, :] / SUBSTEPS  22.1 us
    all_to_all x1, blocking collectives, local(): lax.all_to_all(outgoing, ('tile', 'crm'), split_axis=2, concat_axis=2, ti...  13.8 us
    slice x20, local copies, waits for them, and re-layouts, transport(): eastward = jnp.roll(field_in, -1, axis=1)  9.46 us
    all_to_all x1, waiting for transfers between devices, local(): lax.all_to_all(returning, ('tile', 'crm'), split_axis=2, concat_axis=2, t...  8.83 us
    slice x20, local copies, waits for them, and re-layouts, transport(): level_below = jnp.concatenate([field_in[:1], field_in[:-1]], axis=0)  8.11 us
    ppermute x1, starting transfers between devices, extended(): lax.ppermute(lax.slice_in_dim(block, 0, width, axis=dim), axis, backward)  6.46 us
    unnamed x22, local copies, waits for them, and re-layouts  3.87 us
  transfers between devices with their start and end apart: 3, of which 2 were waited for; matrix products, arithmetic and copies ran while one was open for 4% of the time, Pallas kernels for 0%

commit v1 on v0

v1 whole, which is shorter than its diff:
```python
import functools

import numpy as np

import jax
import jax.numpy as jnp
from jax import lax
from jax.experimental import pallas as pl
from jax.experimental.pallas import tpu as pltpu
from jax.sharding import PartitionSpec as P

SUBSTEPS = 10

loop_diff = 0.35
mix_along = 0.35
mix_vertical = 0.1
cond_rate = 0.1
latent_heat = 1.5
max_speed = 0.8

AXES = ("tile", "crm")
LOG2E = 1.4426950408889634
LN2 = 0.6931471805599453
SUB = 8
LANE = 128
HI = lax.Precision.HIGHEST
VMEM = pl.BlockSpec(memory_space=pltpu.VMEM)


def up_to(n, m):
    return -(-n // m) * m


def edges(block):
    count = lax.axis_size(AXES)
    forward = [(i, (i + 1) % count) for i in range(count)]
    backward = [(t, s) for s, t in forward]
    low = lax.ppermute(block[:, :, -1:], AXES, forward)
    high = lax.ppermute(block[:, :, :1], AXES, backward)
    return low, high


def ring_mean_operator(levels):
    f = np.eye(levels)
    east = west = f
    above = np.concatenate([f[1:], f[-1:]], axis=0)
    below = np.concatenate([f[:1], f[:-1]], axis=0)
    return (
        f
        + mix_along * (east - 2.0 * f + west)
        + mix_vertical * (above - 2.0 * f + below)
    )


def mean_operators(levels):
    v = ring_mean_operator(levels)
    power = np.eye(levels)
    total = np.zeros((levels, levels))
    for _ in range(SUBSTEPS):
        total = total + power
        power = v @ power
    return power, total / SUBSTEPS


def split3(x):
    a = x.astype(jnp.bfloat16)
    r = x - a.astype(jnp.float32)
    b = r.astype(jnp.bfloat16)
    c = (r - b.astype(jnp.float32)).astype(jnp.bfloat16)
    return a, b, c


def dot(a, b, ca, cb, precision=None):
    return lax.dot_general(
        a, b, (((ca,), (cb,)), ((), ())), precision=precision, preferred_element_type=jnp.float32
    )


def advection(f, v, low, high):
    cols = f.shape[1]
    lane = lax.broadcasted_iota(jnp.int32, f.shape, 1)
    ahead = jnp.where(lane == cols - 1, high, pltpu.roll(f, cols - 1, 1))
    behind = jnp.where(lane == 0, low, pltpu.roll(f, 1, 1))
    return -v * (ahead - behind) * 0.5 + loop_diff * (ahead - 2.0 * f + behind)


def onehot(pos_row, cols):
    place = lax.broadcasted_iota(jnp.int32, (cols, cols), 0)
    return jnp.where(place == pos_row, 1.0, 0.0).astype(jnp.bfloat16)


def pack_kernel(devices, t_ref, q_ref, v_ref, own_ref, low_ref, high_ref,
                out_ref, pos_ref, advt_ref, advq_ref, s_ref):
    nl, cols = t_ref.shape
    own = own_ref[...]
    who = lax.broadcasted_iota(jnp.int32, (devices, cols), 0)
    mine = jnp.where(who == own, 1.0, 0.0)
    before = lax.broadcasted_iota(jnp.int32, (cols, cols), 0) < lax.broadcasted_iota(
        jnp.int32, (cols, cols), 1
    )
    tri = jnp.where(before, 1.0, 0.0).astype(jnp.bfloat16)
    ranks = dot(mine.astype(jnp.bfloat16), tri, 1, 0)
    rank = jnp.sum(ranks * mine, axis=0, keepdims=True)
    pos = own * (cols // devices) + rank.astype(jnp.int32)
    pos_ref[...] = pos
    sel = onehot(pos, cols)

    t = t_ref[...]
    q = q_ref[...]
    v = v_ref[...]
    advt = advection(t, v, low_ref[0], high_ref[0])
    advq = advection(q, v, low_ref[1], high_ref[1])
    advt_ref[...] = advt
    advq_ref[...] = advq
    s_ref[0:nl, :] = q - 0.5 * t
    s_ref[nl:2 * nl, :] = v
    s_ref[2 * nl:3 * nl, :] = advq - 0.5 * advt
    rest = s_ref.shape[0] - 3 * nl
    if rest:
        s_ref[3 * nl:, :] = jnp.zeros((rest, cols), jnp.float32)
    a, b, c = split3(s_ref[...])
    out_ref[...] = dot(sel, a, 1, 1) + dot(sel, b, 1, 1) + dot(sel, c, 1, 1)


def softplus2(f):
    return jnp.maximum(f, jnp.log2(1.0 + jnp.exp2(jnp.minimum(f, 100.0))))


def cloud_kernel(zp, r_ref, td_ref, down_ref, mean_ref, out_ref,
                 d_ref, raw_ref, east_ref, west_ref, force_ref, val_ref):
    cz, cx, cols = td_ref.shape
    nl = down_ref.shape[1]
    width = r_ref.shape[1]
    groups = cx // SUB
    tiles = cols // LANE

    down = jnp.concatenate(
        [down_ref[...], jnp.zeros((cz, width - nl), jnp.float32)], axis=1
    )
    down = jnp.concatenate([down, jnp.zeros((zp - cz, width), jnp.float32)], axis=0)
    g = jnp.concatenate(
        [down, pltpu.roll(down, nl, 1), pltpu.roll(down, 2 * nl, 1)], axis=0
    )
    prof = dot(g, r_ref[...], 1, 1, HI)
    d0 = prof[0:zp]
    speed = max_speed * jnp.tanh(prof[zp:2 * zp])
    fd = prof[2 * zp:3 * zp]
    east_ref[...] = mix_along - 0.5 * speed
    west_ref[...] = mix_along + 0.5 * speed
    force_ref[...] = fd * (LOG2E / SUBSTEPS)
    val_ref[zp:2 * zp, :] = d0
    val_ref[2 * zp:3 * zp, :] = fd

    def lanes(k):
        return pl.ds(k * LANE, LANE)

    def row(ref, z, k):
        return jnp.broadcast_to(ref[pl.ds(z, 1), lanes(k)], (SUB, LANE))

    val_ref[0:zp, :] = jnp.zeros((zp, cols), jnp.float32)
    val_ref[3 * zp:, :] = jnp.zeros((val_ref.shape[0] - 3 * zp, cols), jnp.float32)

    for k in range(tiles):
        for z in range(cz):
            base = row(val_ref, zp + z, k) * LOG2E
            total = None
            raw = raw_ref.at[k * cz + z]
            raw[...] = td_ref[z, :, lanes(k)]
            for i in range(groups):
                td = raw[pl.ds(i, SUB, stride=groups), :]
                total = td if total is None else total + td
                d_ref[k, z, i] = base - (0.5 * LOG2E) * td
            val_ref[pl.ds(z, 1), lanes(k)] = jnp.sum(total, axis=0, keepdims=True) * (1.0 / cx)
    val_ref[zp:2 * zp, :] = d0 - 0.5 * val_ref[0:zp, :]

    drain = cond_rate * (1.0 + 0.5 * latent_heat)
    keep = 1.0 - 2.0 * mix_along - 2.0 * mix_vertical

    def step(_, carry):
        for k in range(tiles):
            prev = cur = [d_ref[k, 0, i] for i in range(groups)]
            for z in range(cz):
                nxt = [d_ref[k, z + 1, i] for i in range(groups)] if z + 1 < cz else cur
                ea = row(east_ref, z, k)
                we = row(west_ref, z, k)
                fo = row(force_ref, z, k)
                for i in range(groups):
                    f = cur[i]
                    east = cur[i + 1] if i + 1 < groups else pltpu.roll(cur[0], SUB - 1, 0)
                    west = cur[i - 1] if i else pltpu.roll(cur[-1], 1, 0)
                    new = (
                        keep * f
                        + mix_vertical * (prev[i] + nxt[i])
                        + ea * east
                        + we * west
                        + fo
                        - drain * softplus2(f)
                    )
                    d_ref[k, z, i] = new
                prev, cur = cur, nxt
        return carry

    lax.fori_loop(0, SUBSTEPS, step, 0)

    for k in range(tiles):
        for z in range(cz):
            total = cloud = None
            for i in range(groups):
                f = d_ref[k, z, i]
                c = softplus2(f)
                total = f if total is None else total + f
                cloud = c if cloud is None else cloud + c
            val_ref[pl.ds(3 * zp + z, 1), lanes(k)] = jnp.sum(
                total, axis=0, keepdims=True
            ) * (LN2 / cx)
            val_ref[pl.ds(4 * zp + z, 1), lanes(k)] = jnp.sum(
                cloud, axis=0, keepdims=True
            ) * (LN2 / cx)
    out_ref[...] = dot(val_ref[...], mean_ref[...], 0, 0, HI)


def finish_kernel(zp, r_ref, pos_ref, t_ref, q_ref, advt_ref, advq_ref, down_ref, up_ref,
                  lin_ref, to_ref, qo_ref, co_ref):
    nl, cols = t_ref.shape
    cz = down_ref.shape[0]
    width = r_ref.shape[1]
    down = down_ref[...]
    up = up_ref[...]
    tc = dot(down, t_ref[...], 1, 0, HI)
    qc = dot(down, q_ref[...], 1, 0, HI)
    ft = dot(down, advt_ref[...], 1, 0, HI)
    fq = dot(down, advq_ref[...], 1, 0, HI)
    lin = lin_ref[...]
    ls = dot(lin[0], tc, 1, 0, HI) + dot(lin[1], ft, 1, 0, HI)
    lq = dot(lin[0], qc, 1, 0, HI) + dot(lin[1], fq, 1, 0, HI)
    sel = onehot(pos_ref[...], cols)
    a, b, c = split3(r_ref[...])
    u = dot(a, sel, 0, 0) + dot(b, sel, 0, 0) + dot(c, sel, 0, 0)
    heat = dot(up, ls + u[0:cz], 1, 0, HI)
    moist = dot(up, lq - u[zp:zp + cz], 1, 0, HI)
    to_ref[...] = t_ref[...] + advt_ref[...] + heat
    qo_ref[...] = q_ref[...] + advq_ref[...] + moist
    co_ref[...] = dot(up, u[2 * zp:2 * zp + cz], 1, 0, HI)


def local(
    thermal_anomaly,
    vapour_anomaly,
    periodic_flow_velocity,
    processor_assignment,
    thermal_disturbance,
    layer_index_downscale,
    layer_index_upscale,
):
    nl, cols = thermal_anomaly.shape
    cz, cx, _ = thermal_disturbance.shape
    devices = lax.axis_size(AXES)
    per = cols // devices
    zp = up_to(cz, SUB)
    f32 = jnp.float32
    width = up_to(3 * nl, LANE)
    back = up_to(3 * zp, LANE)

    low, high = edges(jnp.stack([thermal_anomaly, vapour_anomaly]))
    field = jax.ShapeDtypeStruct((nl, cols), f32)
    out, pos, advt, advq = pl.pallas_call(
        functools.partial(pack_kernel, devices),
        out_shape=(
            jax.ShapeDtypeStruct((cols, width), f32),
            jax.ShapeDtypeStruct((1, cols), jnp.int32),
            field,
            field,
        ),
        in_specs=[VMEM] * 6,
        out_specs=(VMEM,) * 4,
        scratch_shapes=[pltpu.VMEM((width, cols), f32)],
        name="pack",
    )(
        thermal_anomaly,
        vapour_anomaly,
        periodic_flow_velocity,
        processor_assignment.reshape(1, cols),
        low,
        high,
    )
    r1 = lax.all_to_all(
        out.reshape(devices, per, width), AXES, split_axis=0, concat_axis=0, tiled=True
    ).reshape(cols, width)

    power, total = mean_operators(cz)
    release = cond_rate * (1.0 + 0.5 * latent_heat) / cond_rate
    mean = np.zeros((5 * zp, back))
    z_part = np.zeros((5 * zp, cz))
    z_part[zp:zp + cz] = power.T / release
    z_part[2 * zp:2 * zp + cz] = total.T / release
    z_part[3 * zp:3 * zp + cz] = -np.eye(cz) / release
    mean[0:cz, 0:cz] = power.T
    mean[:, 0:cz] += latent_heat * z_part
    mean[:, zp:zp + cz] = z_part
    mean[4 * zp:4 * zp + cz, 2 * zp:2 * zp + cz] = np.eye(cz)

    tiles = cols // LANE
    vals = pl.pallas_call(
        functools.partial(cloud_kernel, zp),
        out_shape=jax.ShapeDtypeStruct((cols, back), f32),
        in_specs=[VMEM] * 4,
        out_specs=VMEM,
        scratch_shapes=[
            pltpu.VMEM((tiles, cz, cx // SUB, SUB, LANE), f32),
            pltpu.VMEM((tiles * cz, cx, LANE), f32),
            pltpu.VMEM((zp, cols), f32),
            pltpu.VMEM((zp, cols), f32),
            pltpu.VMEM((zp, cols), f32),
            pltpu.VMEM((5 * zp, cols), f32),
        ],
        name="cloud",
    )(r1, thermal_disturbance, layer_index_downscale, jnp.asarray(mean, f32))
    r2 = lax.all_to_all(
        vals.reshape(devices, per, back), AXES, split_axis=0, concat_axis=0, tiled=True
    ).reshape(cols, back)

    lin = np.stack([power - np.eye(cz), total])
    return pl.pallas_call(
        functools.partial(finish_kernel, zp),
        out_shape=(field,) * 3,
        in_specs=[VMEM] * 9,
        out_specs=(VMEM,) * 3,
        name="finish",
    )(
        r2,
        pos,
        thermal_anomaly,
        vapour_anomaly,
        advt,
        advq,
        layer_index_downscale,
        layer_index_upscale,
        jnp.asarray(lin, f32),
    )


def solution(mesh):
    in_specs = (
        P(None, AXES),
        P(None, AXES),
        P(None, AXES),
        P(AXES),
        P(None, None, AXES),
        P(),
        P(),
    )
    out_specs = (P(None, AXES), P(None, AXES), P(None, AXES))
    return jax.shard_map(local, mesh=mesh, in_specs=in_specs, out_specs=out_specs, check_vma=False)
```

time: 125 us -> 59.6 us (0.48)
  other arithmetic: 57.4 us -> 0.91 us
  local copies, waits for them, and re-layouts: 29.6 us -> 2.02 us
  Pallas kernels: 0 us -> 18.3 us
  blocking collectives: 13.8 us -> 16 us
  matrix products: 1.92 us -> 0 us
    add x13 -> x0, other arithmetic: 25.1 us -> none  [the longest x10 22.8 us: substep(): transport(theta_old, advect_speed) + force_temp[:, None, :] / SUBSTEPS]
    sub x11 -> x0, other arithmetic: 23.2 us -> none  [the longest x10 22.1 us: substep(): transport(water_old, advect_speed) + force_water[:, None, :] / SUBSTEPS]
    pallas_call x0 -> x3, Pallas kernels: none -> 18.3 us  [the longest x1 13.2 us: local(): pl.pallas_call(functools.partial(cloud_kernel, zp), out_shape=jax.ShapeDt...]
    slice x40 -> x0, local copies, waits for them, and re-layouts: 17.6 us -> none  [the longest x20 9.46 us: transport(): eastward = jnp.roll(field_in, -1, axis=1)]
    all_to_all x2 -> x0, other arithmetic: 2.3 us -> none  [the longest x1 1.26 us: local(): lax.all_to_all(outgoing, ('tile', 'crm'), split_axis=2, concat_axis=2, ti...]
    reduce_sum x2 -> x0, other arithmetic: 2.22 us -> none  [the longest x1 1.44 us: cloud_model(): delta_temp = jnp.mean(theta_state, axis=1) - temp_prof]
    all_to_all x1, blocking collectives: 13.8 us -> 16 us  [local(): lax.all_to_all(out.reshape(devices, per, width), AXES, split_axis=0, conc...]
    gather x2 -> x0, local copies, waits for them, and re-layouts: 2.02 us -> none  [the longest x1 1.03 us: local(): outgoing = jnp.take(prognostic_variables, ordering, axis=2)]
  transfers between devices with their start and end apart: 3 -> 3, of which waited for: 2 -> 3; matrix products, arithmetic and copies ran while one was open for 4% -> 1% of each run, Pallas kernels for 0% -> 0%
where the time goes in v1:
time: 59.6 us; the launch traced here: 59.1 us
  Pallas kernels  18.3 us (31%)
  blocking collectives  16 us (27%)
  waiting for transfers between devices  12 us (20%)
  starting transfers between devices  9.19 us (15%)
  local copies, waits for them, and re-layouts  2.02 us (3%)
  other arithmetic  0.91 us (2%)
  between operations  0.66 us (1%)
    all_to_all x1, blocking collectives, local(): lax.all_to_all(out.reshape(devices, per, width), AXES, split_axis=0, conc...  16 us
    pallas_call x1, Pallas kernels, local(): pl.pallas_call(functools.partial(cloud_kernel, zp), out_shape=jax.ShapeDt...  13.2 us
    all_to_all x1, waiting for transfers between devices, local(): lax.all_to_all(vals.reshape(devices, per, back), AXES, split_axis=0, conc...  9.53 us
    ppermute x1, starting transfers between devices, edges(): high = lax.ppermute(block[:, :, :1], AXES, backward)  3.42 us
    ppermute x1, starting transfers between devices, edges(): low = lax.ppermute(block[:, :, -1:], AXES, forward)  3.11 us
    pallas_call x1, Pallas kernels, local(): pl.pallas_call(functools.partial(finish_kernel, zp), out_shape=(field,) *...  2.94 us
    all_to_all x1, starting transfers between devices, local(): lax.all_to_all(vals.reshape(devices, per, back), AXES, split_axis=0, conc...  2.66 us
    pallas_call x1, Pallas kernels, local(): pl.pallas_call(functools.partial(pack_kernel, devices), out_shape=(jax.Sh...  2.19 us
  transfers between devices with their start and end apart: 3, of which 3 were waited for; matrix products, arithmetic and copies ran while one was open for 1% of the time, Pallas kernels for 0%

profile of v1, /device:TPU:0, one launch (start us, length us, event | category | flops | bytes accessed | tf_op | source)
XLA Modules:
  0.0 59.1 jit_solution(13935530166369451497)
XLA Ops:
  0.6 0.9 %pad_maximum_fusion = (f32[2,72,1]{2,1,0:T(8,128)S(1)}, f32[2,72,1]{2,1,0:T(8,128)S(1)}) fusion(f32[1,72,256]{2,1,0:T(8,128)} %bitcast.11, f32[1,72,256]{2,1,0:T(8,128)} %bitcast.10), kind=kLoop, calls=%fused_computation.3 | loop fusion | flops 288 | bytes 148608 | tf_op jit(solution)/shard_map/stack | solution.py:264
  1.5 3.1 %collective-permute-start = (f32[2,72,1]{2,1,0:T(8,128)S(1)}, f32[2,72,1]{2,1,0:T(8,128)S(1)}, u32[]{:S(2)}, u32[]{:S(2)}) collective-permute-start(f32[2,72,1]{2,1,0:T(8,128)S(1)} %get-tuple-element.12), channel_id=1, source_target_pairs={{0,1},{1,2},{2,3},{3,4},{4,5},{5,6},{6,7},{7,8},{8,9},{9,10},{10,1... | collective-permute-start | bytes 1736 | tf_op jit(solution)/shard_map/ppermute | solution.py:38
  4.7 3.4 %collective-permute-start.1 = (f32[2,72,1]{2,1,0:T(8,128)S(1)}, f32[2,72,1]{2,1,0:T(8,128)S(1)}, u32[]{:S(2)}, u32[]{:S(2)}) collective-permute-start(f32[2,72,1]{2,1,0:T(8,128)S(1)} %get-tuple-element.11), channel_id=1, source_target_pairs={{1,0},{2,1},{3,2},{4,3},{5,4},{6,5},{7,6},{8,7},{9,8},{10,9},{11,1... | collective-permute-start | bytes 1736 | tf_op jit(solution)/shard_map/ppermute | solution.py:39
  8.1 2.1 %collective-permute-done.low_ref = f32[2,72,1]{2,1,0:T(8,128)S(1)} collective-permute-done((f32[2,72,1]{2,1,0:T(8,128)S(1)}, f32[2,72,1]{2,1,0:T(8,128)S(1)}, u32[]{:S(2)}, u32[]{:S(2)}) %collective-permute-start) | collective-permute-done | bytes 608 | tf_op jit(solution)/shard_map/ppermute | solution.py:38
  10.1 0.0 copy-start.1
  10.1 0.4 collective-permute-done.1.high_ref
  10.6 0.0 copy-start.2
  10.6 0.2 copy-done.1
  10.8 0.4 copy-done.2
  11.2 2.2 %pack.1 = (f32[256,256]{1,0:T(8,128)}, s32[1,256]{1,0:T(1,128)}, f32[72,256]{1,0:T(8,128)}, f32[72,256]{1,0:T(8,128)}) custom-call(f32[72,256]{1,0:T(8,128)} %t_ref.3, f32[72,256]{1,0:T(8,128)} %q_ref.3, f32[72,256]{1,0:T(8,128)} %v_ref.1, s32[1,256]{1,0:T(1,128)} %bitcast.13, f32[2,72,1]{2,1,0:T(8,128)} %copy-done.1, f32[2,72,1]{2,1,0:T(8,128)} %copy-done.2), custom_call_target="tpu_custom_call" | custom-call | tf_op jit(solution)/shard_map/pack/pallas_call | solution.py:266
  13.4 0.0 copy-start.3
  13.4 16.0 %all_to_all.10 = f32[32,8,256]{2,1,0:T(8,128)} all-to-all(f32[32,8,256]{2,1,0:T(8,128)} %bitcast.12), channel_id=1, replica_groups=mesh['tile'=8,'crm'=4] {'tile','crm'}, dimensions={0} | all-to-all | bytes 524288 | tf_op jit(solution)/shard_map/all_to_all | solution.py:286
  29.4 13.2 %cloud.1 = f32[256,256]{1,0:T(8,128)} custom-call(f32[256,256]{1,0:T(8,128)} %bitcast.8, f32[50,32,256]{2,1,0:T(8,128)} %td_ref.1, f32[50,72]{1,0:T(8,128)} %down_ref.3, f32[280,256]{1,0:T(8,128)} %constant.4.clone.mean_ref), custom_call_target="tpu_custom_call" | custom-call | tf_op jit(solution)/shard_map/cloud/pallas_call | solution.py:303
  42.6 2.7 %all-to-all-start.1 = ((f32[32,8,256]{2,1,0:T(8,128)}), f32[32,8,256]{2,1,0:T(8,128)S(1)}, u32[]{:S(2)}, u32[]{:S(2)}) async-start(f32[32,8,256]{2,1,0:T(8,128)} %bitcast.7), calls=%async_computation.1 | async-start | bytes 524288 | tf_op jit(solution)/shard_map/all_to_all | solution.py:318
  45.3 0.0 copy-done.3
  45.3 0.7 %copy.12.up_ref = f32[72,50]{1,0:T(8,128)} copy(f32[72,50]{0,1:T(8,128)S(1)} %copy-done.3) | data formatting | bytes 28800 | tf_op args[6]
  46.0 9.5 %all-to-all-done.1 = f32[32,8,256]{2,1,0:T(8,128)S(1)} async-done(((f32[32,8,256]{2,1,0:T(8,128)}), f32[32,8,256]{2,1,0:T(8,128)S(1)}, u32[]{:S(2)}, u32[]{:S(2)}) %all-to-all-start.1) | async-done | bytes 262176 | tf_op jit(solution)/shard_map/all_to_all | solution.py:318
  55.5 0.0 copy-start
  55.5 0.7 %copy-done = f32[32,8,256]{2,1,0:T(8,128)} copy-done((f32[32,8,256]{2,1,0:T(8,128)}, f32[32,8,256]{2,1,0:T(8,128)S(1)}, u32[]{:S(2)}) %copy-start) | copy-done | bytes 262168
  56.2 2.9 %finish.1 = (f32[72,256]{1,0:T(8,128)}, f32[72,256]{1,0:T(8,128)}, f32[72,256]{1,0:T(8,128)}) custom-call(f32[256,256]{1,0:T(8,128)} %bitcast.9, s32[1,256]{1,0:T(1,128)} %get-tuple-element.8.pos_ref, f32[72,256]{1,0:T(8,128)} %t_ref.3, f32[72,256]{1,0:T(8,128)} %q_ref.3, f32[72,256]{1,0:T(8,128)} %get-tuple-element.9.advt_ref, ...), custom_call_target="tpu_custom_call" | custom-call | tf_op jit(solution)/shard_map/finish/pallas_call | solution.py:323
Async XLA Ops:
  1.5 8.6 %collective-permute-start = (f32[2,72,1]{2,1,0:T(8,128)S(1)}, f32[2,72,1]{2,1,0:T(8,128)S(1)}, u32[]{:S(2)}, u32[]{:S(2)}) collective-permute-start(f32[2,72,1]{2,1,0:T(8,128)S(1)} %get-tuple-element.12), channel_id=1, source_target_pairs={{0,1},{1,2},{2,3},{3,4},{4,5},{5,6},{6,7},{7,8},{8,9},{9,10},{10,1... | collective-permute-start | bytes 1736 | tf_op jit(solution)/shard_map/ppermute | solution.py:38
  4.7 5.9 %collective-permute-start.1 = (f32[2,72,1]{2,1,0:T(8,128)S(1)}, f32[2,72,1]{2,1,0:T(8,128)S(1)}, u32[]{:S(2)}, u32[]{:S(2)}) collective-permute-start(f32[2,72,1]{2,1,0:T(8,128)S(1)} %get-tuple-element.11), channel_id=1, source_target_pairs={{1,0},{2,1},{3,2},{4,3},{5,4},{6,5},{7,6},{8,7},{9,8},{10,9},{11,1... | collective-permute-start | bytes 1736 | tf_op jit(solution)/shard_map/ppermute | solution.py:39
  10.1 0.6 %copy-start.1 = (f32[2,72,1]{2,1,0:T(8,128)}, f32[2,72,1]{2,1,0:T(8,128)S(1)}, u32[]{:S(2)}) copy-start(f32[2,72,1]{2,1,0:T(8,128)S(1)} %collective-permute-done.low_ref) | copy-start | bytes 1732
  10.6 0.6 %copy-start.2 = (f32[2,72,1]{2,1,0:T(8,128)}, f32[2,72,1]{2,1,0:T(8,128)S(1)}, u32[]{:S(2)}) copy-start(f32[2,72,1]{2,1,0:T(8,128)S(1)} %collective-permute-done.1.high_ref) | copy-start | bytes 1732
  13.4 31.9 %copy-start.3 = (f32[72,50]{0,1:T(8,128)S(1)}, f32[72,50]{0,1:T(8,128)}, u32[]{:S(2)}) copy-start(f32[72,50]{0,1:T(8,128)} %param.15) | copy-start | bytes 43204
  42.6 12.9 %all-to-all-start.1 = ((f32[32,8,256]{2,1,0:T(8,128)}), f32[32,8,256]{2,1,0:T(8,128)S(1)}, u32[]{:S(2)}, u32[]{:S(2)}) async-start(f32[32,8,256]{2,1,0:T(8,128)} %bitcast.7), calls=%async_computation.1 | async-start | bytes 524288 | tf_op jit(solution)/shard_map/all_to_all | solution.py:318
  55.5 0.7 %copy-start = (f32[32,8,256]{2,1,0:T(8,128)}, f32[32,8,256]{2,1,0:T(8,128)S(1)}, u32[]{:S(2)}) copy-start(f32[32,8,256]{2,1,0:T(8,128)S(1)} %all-to-all-done.1) | copy-start | bytes 786436

commit v2 on v1

v2 whole, which is shorter than its diff:
```python
import functools

import numpy as np

import jax
import jax.numpy as jnp
from jax import lax
from jax.experimental import pallas as pl
from jax.experimental.pallas import tpu as pltpu
from jax.sharding import PartitionSpec as P

SUBSTEPS = 10

loop_diff = 0.35
mix_along = 0.35
mix_vertical = 0.1
cond_rate = 0.1
latent_heat = 1.5
max_speed = 0.8

AXES = ("tile", "crm")
LOG2E = 1.4426950408889634
LN2 = 0.6931471805599453
SUB = 8
LANE = 128
HI = lax.Precision.HIGH
VMEM = pl.BlockSpec(memory_space=pltpu.VMEM)
ANY = pl.BlockSpec(memory_space=pl.ANY)


def up_to(n, m):
    return -(-n // m) * m


def edges(block):
    count = lax.axis_size(AXES)
    forward = [(i, (i + 1) % count) for i in range(count)]
    backward = [(t, s) for s, t in forward]
    low = lax.ppermute(block[:, :, -1:], AXES, forward)
    high = lax.ppermute(block[:, :, :1], AXES, backward)
    return low, high


def ring_mean_operator(levels):
    f = np.eye(levels)
    east = west = f
    above = np.concatenate([f[1:], f[-1:]], axis=0)
    below = np.concatenate([f[:1], f[:-1]], axis=0)
    return (
        f
        + mix_along * (east - 2.0 * f + west)
        + mix_vertical * (above - 2.0 * f + below)
    )


def mean_operators(levels):
    v = ring_mean_operator(levels)
    power = np.eye(levels)
    total = np.zeros((levels, levels))
    for _ in range(SUBSTEPS):
        total = total + power
        power = v @ power
    return power, total / SUBSTEPS


def split(x):
    a = x.astype(jnp.bfloat16)
    return a, (x - a.astype(jnp.float32)).astype(jnp.bfloat16)


def dot(a, b, ca, cb, precision=None):
    return lax.dot_general(
        a, b, (((ca,), (cb,)), ((), ())), precision=precision, preferred_element_type=jnp.float32
    )


def advection(f, v, low, high):
    cols = f.shape[1]
    lane = lax.broadcasted_iota(jnp.int32, f.shape, 1)
    ahead = jnp.where(lane == cols - 1, high, pltpu.roll(f, cols - 1, 1))
    behind = jnp.where(lane == 0, low, pltpu.roll(f, 1, 1))
    return -v * (ahead - behind) * 0.5 + loop_diff * (ahead - 2.0 * f + behind)


def onehot(pos_row, cols):
    place = lax.broadcasted_iota(jnp.int32, (cols, cols), 0)
    return jnp.where(place == pos_row, 1.0, 0.0).astype(jnp.bfloat16)


CARRIED = (
    (0, 1, 0), (0, 0, 0), (0, 0, 1), (0, 1, 1),
    (1, 0, 0), (1, 1, 0), (1, 0, 1), (1, 1, 1),
)


def row_of(field, half, end):
    return CARRIED.index((field, half, end))


def halves(levels):
    first = up_to(-(-levels // 2), SUB)
    return first, levels - first


def carries(levels, per, width):
    first, second = halves(levels)
    return per >= len(CARRIED) and 3 * levels + first <= width and second < first


def pack_kernel(devices, carry, *refs):
    t_ref, q_ref, v_ref, own_ref = refs[:4]
    low_ref, high_ref = (None, None) if carry else refs[4:6]
    out_ref, pos_ref, s_ref = refs[-3:]
    nl, cols = t_ref.shape
    width = s_ref.shape[0]
    per = cols // devices
    own = own_ref[...]
    who = lax.broadcasted_iota(jnp.int32, (devices, cols), 0)
    mine = jnp.where(who == own, 1.0, 0.0)
    before = lax.broadcasted_iota(jnp.int32, (cols, cols), 0) < lax.broadcasted_iota(
        jnp.int32, (cols, cols), 1
    )
    tri = jnp.where(before, 1.0, 0.0).astype(jnp.bfloat16)
    ranks = dot(mine.astype(jnp.bfloat16), tri, 1, 0)
    rank = jnp.sum(ranks * mine, axis=0, keepdims=True)
    pos = own * per + rank.astype(jnp.int32)
    pos_ref[...] = pos
    sel = onehot(pos, cols)

    t = t_ref[...]
    x = q_ref[...] - 0.5 * t
    v = v_ref[...]
    if carry:
        low = high = jnp.zeros((nl, 1), jnp.float32)
    else:
        low = low_ref[1] - 0.5 * low_ref[0]
        high = high_ref[1] - 0.5 * high_ref[0]
    s_ref[0:nl, :] = x
    s_ref[nl:2 * nl, :] = v
    s_ref[2 * nl:3 * nl, :] = advection(x, v, low, high)
    rest = width - 3 * nl
    if rest:
        s_ref[3 * nl:, :] = jnp.zeros((rest, cols), jnp.float32)
    if carry:
        first, second = halves(nl)
        lane = lax.broadcasted_iota(jnp.int32, (1, cols), 1)
        s_ref[3 * nl + second:3 * nl + second + 1, :] = jnp.where(
            (lane == 0) | (lane == cols - 1), 1.0, 0.0
        )
    a, b = split(s_ref[...])
    out = dot(sel, a, 1, 1) + dot(sel, b, 1, 1)
    if carry:
        fill = jnp.zeros((first - second, cols), jnp.float32)
        parts = []
        for f in (x, t):
            parts += [f[:first], jnp.concatenate([f[first:], fill], axis=0)]
        parts = jnp.concatenate(parts, axis=1)
        shape = (SUB, parts.shape[1])
        want = jnp.full(shape, -1, jnp.int32)
        row = lax.broadcasted_iota(jnp.int32, shape, 0)
        for r, (field, half, end) in enumerate(CARRIED):
            want = jnp.where(row == r, (2 * field + half) * cols + end * (cols - 1), want)
        pick = jnp.where(lax.broadcasted_iota(jnp.int32, shape, 1) == want, 1.0, 0.0).astype(
            jnp.bfloat16
        )
        a, b = split(parts)
        ends = dot(pick, a, 1, 1) + dot(pick, b, 1, 1)
        ends = jnp.concatenate([ends, jnp.zeros((SUB, width - first), jnp.float32)], axis=1)
        ends = pltpu.roll(ends, 3 * nl, 1)
        out = (out.reshape(devices, per, width) + ends[None]).reshape(cols, width)
    out_ref[...] = out


def softplus2(f):
    return jnp.maximum(f, jnp.log2(1.0 + jnp.exp2(jnp.minimum(f, 100.0))))


def cloud_kernel(devices, carry, r_ref, td_ref, down_ref, mean_ref, out_ref,
                 d_ref, raw_ref, east_ref, west_ref, force_ref, val_ref, part_ref, mean_buf,
                 td_sem, mean_sem):
    cz, cx, cols = td_ref.shape
    nl = down_ref.shape[1]
    zp = east_ref.shape[0]
    width = r_ref.shape[1]
    per = cols // devices
    groups = cx // SUB
    tiles = cols // LANE
    chunk = -(-cz // td_sem.shape[1])

    def lanes(k):
        return pl.ds(k * LANE, LANE)

    def td_copy(k, c):
        levels = pl.ds(c * chunk, min(chunk, cz - c * chunk))
        return pltpu.make_async_copy(
            td_ref.at[levels, :, lanes(k)], raw_ref.at[k, levels], td_sem.at[k, c]
        )

    for k in range(tiles):
        for c in range(td_sem.shape[1]):
            td_copy(k, c).start()
    mean_copy = pltpu.make_async_copy(mean_ref, mean_buf, mean_sem)
    mean_copy.start()

    down = jnp.concatenate(
        [down_ref[...], jnp.zeros((cz, width - nl), jnp.float32)], axis=1
    )
    down = jnp.concatenate([down, jnp.zeros((zp - cz, width), jnp.float32)], axis=0)
    g = [down, pltpu.roll(down, nl, 1), pltpu.roll(down, 2 * nl, 1)]
    if carry:
        first, second = halves(nl)
        shape = (nl + first, width)
        row = lax.broadcasted_iota(jnp.int32, shape, 0)
        to = jnp.where(row < nl, row + nl, row + 2 * nl)
        g.append(jnp.where(lax.broadcasted_iota(jnp.int32, shape, 1) == to, 1.0, 0.0))
    prof = dot(jnp.concatenate(g, axis=0), r_ref[...], 1, 1, HI)
    d0 = prof[0:zp]
    speed = max_speed * jnp.tanh(prof[zp:2 * zp])
    fd = prof[2 * zp:3 * zp]
    if carry:
        v = prof[3 * zp:3 * zp + nl]
        ends = prof[3 * zp + nl:3 * zp + nl + first]
        flag = ends[second:second + 1] > 0.5
        place = lax.rem(lax.broadcasted_iota(jnp.int32, (1, cols), 1), per)

        def neighbour(end, at):
            step = per if at == 0 else -per
            shift = lambda half: (step + at - row_of(0, half, end)) % cols
            return jnp.concatenate(
                [pltpu.roll(ends, shift(0), 1), pltpu.roll(ends, shift(1), 1)[:second]], axis=0
            )

        behind = neighbour(1, 0) * (loop_diff + 0.5 * v)
        ahead = neighbour(0, per - 1) * (loop_diff - 0.5 * v)
        halo = jnp.where(flag & (place == 0), behind, 0.0) + jnp.where(
            flag & (place == per - 1), ahead, 0.0
        )
        fd = fd + dot(down[:, :nl], halo, 1, 0, HI)
    east_ref[...] = mix_along - 0.5 * speed
    west_ref[...] = mix_along + 0.5 * speed
    force_ref[...] = fd * (LOG2E / SUBSTEPS)
    val_ref[zp:2 * zp, :] = d0
    val_ref[2 * zp:3 * zp, :] = fd

    def row_at(ref, z, k):
        return jnp.broadcast_to(ref[pl.ds(z, 1), lanes(k)], (SUB, LANE))

    zeros = jnp.zeros((SUB, LANE), jnp.float32)
    for n in range(part_ref.shape[0]):
        for z in range(cz, zp):
            part_ref[n, pl.ds(z * SUB, SUB), :] = zeros

    def fold(n, k, base, scale):
        total = part_ref[n, pl.ds(0, zp, stride=SUB), :]
        for s in range(1, SUB):
            total = total + part_ref[n, pl.ds(s, zp, stride=SUB), :]
        val_ref[pl.ds(base, zp), lanes(k)] = total * scale

    slot = [0] + [SUB * (i + 1) for i in range(1, groups)]
    last = slot[-1]

    def put(k, z, i, new):
        d_ref[k, z, pl.ds(slot[i], SUB), :] = new
        if i == 0:
            d_ref[k, z, pl.ds(SUB, SUB), :] = new
        if i == groups - 1:
            d_ref[k, z, pl.ds(last + SUB, SUB), :] = new

    for k in range(tiles):
        for z in range(cz):
            if z % chunk == 0:
                td_copy(k, z // chunk).wait()
            base = row_at(val_ref, zp + z, k) * LOG2E
            total = None
            for i in range(groups):
                td = raw_ref[k, z, pl.ds(i, SUB, stride=groups), :]
                total = td if total is None else total + td
                put(k, z, i, base - (0.5 * LOG2E) * td)
            part_ref[k, pl.ds(z * SUB, SUB), :] = total
        fold(k, k, 0, 1.0 / cx)

    drain = cond_rate * (1.0 + 0.5 * latent_heat)

    def step(_, carry):
        for k in range(tiles):
            prev = cur = [d_ref[k, 0, pl.ds(slot[i], SUB), :] for i in range(groups)]
            for z in range(cz):
                nxt = cur
                if z + 1 < cz:
                    nxt = [d_ref[k, z + 1, pl.ds(slot[i], SUB), :] for i in range(groups)]
                ea = row_at(east_ref, z, k)
                we = row_at(west_ref, z, k)
                fo = row_at(force_ref, z, k)
                ring = [d_ref[k, z, pl.ds(last + SUB - 1, SUB), :]] + cur
                ring = ring + [d_ref[k, z, pl.ds(1, SUB), :]]
                for i in range(groups):
                    f = cur[i]
                    new = (
                        mix_vertical * ((prev[i] + f) + nxt[i])
                        + ea * ring[i + 2]
                        + we * ring[i]
                        + fo
                        - drain * softplus2(f)
                    )
                    put(k, z, i, new)
                prev, cur = cur, nxt
        return carry

    lax.fori_loop(0, SUBSTEPS, step, 0)

    for k in range(tiles):
        for z in range(cz):
            total = cloud = None
            for i in range(groups):
                f = d_ref[k, z, pl.ds(slot[i], SUB), :]
                c = softplus2(f)
                total = f if total is None else total + f
                cloud = c if cloud is None else cloud + c
            part_ref[2 * k, pl.ds(z * SUB, SUB), :] = total
            part_ref[2 * k + 1, pl.ds(z * SUB, SUB), :] = cloud
        fold(2 * k, k, 3 * zp, LN2 / cx)
        fold(2 * k + 1, k, 4 * zp, LN2 / cx)
    val_ref[zp:2 * zp, :] = val_ref[zp:2 * zp, :] - 0.5 * val_ref[0:zp, :]
    mean_copy.wait()
    out_ref[...] = dot(val_ref[...], mean_buf[...], 0, 0, HI)


def base_kernel(devices, carry, *refs):
    t_ref, q_ref, v_ref, down_ref, up_ref, lin_ref, after_ref, r_ref = refs[:8]
    high_ref = None if carry else refs[8]
    to_ref, qo_ref = refs[-2:]
    del after_ref
    nl, cols = t_ref.shape
    per = cols // devices
    if carry:
        first, second = halves(nl)
        me = lax.axis_index(AXES)

        def ends(device, end):
            start = pl.multiple_of(device * per, SUB)
            block = r_ref[pl.ds(start, SUB), :]
            block = pltpu.roll(block, block.shape[1] - 3 * nl, 1)[:, :LANE].T
            x, t = [
                jnp.concatenate(
                    [
                        block[:first, row_of(field, 0, end):row_of(field, 0, end) + 1],
                        block[:second, row_of(field, 1, end):row_of(field, 1, end) + 1],
                    ],
                    axis=0,
                )
                for field in (0, 1)
            ]
            return t, x + 0.5 * t

        low = ends(lax.rem(me + devices - 1, devices), 1)
        high = ends(lax.rem(me + 1, devices), 0)
    else:
        low = (r_ref[0], r_ref[1])
        high = (high_ref[0], high_ref[1])
    v = v_ref[...]
    t = t_ref[...]
    q = q_ref[...]
    advt = advection(t, v, low[0], high[0])
    advq = advection(q, v, low[1], high[1])
    prof = dot(down_ref[...], jnp.concatenate([t, q, advt, advq], axis=1), 1, 0, HI)
    lin = lin_ref[...]
    gain = dot(lin[0], prof[:, :2 * cols], 1, 0, HI) + dot(lin[1], prof[:, 2 * cols:], 1, 0, HI)
    gain = dot(up_ref[...], gain, 1, 0, HI)
    to_ref[...] = t + advt + gain[:, :cols]
    qo_ref[...] = q + advq + gain[:, cols:]


def finish_kernel(zp, r_ref, pos_ref, up_ref, tb_ref, qb_ref, to_ref, qo_ref, co_ref):
    nl, cols = tb_ref.shape
    cz = up_ref.shape[1]
    width = r_ref.shape[1]
    up = jnp.concatenate([up_ref[...], jnp.zeros((nl, width - cz), jnp.float32)], axis=1)
    up = jnp.concatenate([up, -pltpu.roll(up, zp, 1), pltpu.roll(up, 2 * zp, 1)], axis=0)
    sel = onehot(pos_ref[...], cols)
    a, b = split(dot(up, r_ref[...], 1, 1, HI))
    out = dot(a, sel, 1, 0) + dot(b, sel, 1, 0)
    to_ref[...] = tb_ref[...] + out[0:nl]
    qo_ref[...] = qb_ref[...] + out[nl:2 * nl]
    co_ref[...] = out[2 * nl:3 * nl]


def local(
    thermal_anomaly,
    vapour_anomaly,
    periodic_flow_velocity,
    processor_assignment,
    thermal_disturbance,
    layer_index_downscale,
    layer_index_upscale,
):
    nl, cols = thermal_anomaly.shape
    cz, cx, _ = thermal_disturbance.shape
    devices = lax.axis_size(AXES)
    per = cols // devices
    zp = up_to(cz, SUB)
    f32 = jnp.float32
    width = up_to(3 * nl, LANE)
    back = up_to(3 * zp, LANE)
    field = jax.ShapeDtypeStruct((nl, cols), f32)
    carry = carries(nl, per, width)

    fields = (thermal_anomaly, vapour_anomaly, periodic_flow_velocity)
    ends = () if carry else edges(jnp.stack(fields[:2]))
    out, pos = pl.pallas_call(
        functools.partial(pack_kernel, devices, carry),
        out_shape=(
            jax.ShapeDtypeStruct((cols, width), f32),
            jax.ShapeDtypeStruct((1, cols), jnp.int32),
        ),
        in_specs=[VMEM] * (4 + len(ends)),
        out_specs=(VMEM,) * 2,
        scratch_shapes=[pltpu.VMEM((width, cols), f32)],
        compiler_params=pltpu.CompilerParams(vmem_limit_bytes=VMEM_PACK),
        name="pack",
    )(*fields, processor_assignment.reshape(1, cols), *ends)

    def exchange(blocks):
        shape = blocks.shape
        blocks = blocks.reshape(devices, per, shape[1])
        return lax.all_to_all(blocks, AXES, split_axis=0, concat_axis=0, tiled=True).reshape(shape)

    r1 = exchange(out)

    power, total = mean_operators(cz)
    release = 1.0 + 0.5 * latent_heat
    mean = np.zeros((5 * zp, back))
    z_part = np.zeros((5 * zp, cz))
    z_part[zp:zp + cz] = power.T / release
    z_part[2 * zp:2 * zp + cz] = total.T / release
    z_part[3 * zp:3 * zp + cz] = -np.eye(cz) / release
    mean[0:cz, 0:cz] = power.T
    mean[:, 0:cz] += latent_heat * z_part
    mean[:, zp:zp + cz] = z_part
    mean[4 * zp:4 * zp + cz, 2 * zp:2 * zp + cz] = np.eye(cz)

    tiles = cols // LANE
    groups = cx // SUB
    vals = pl.pallas_call(
        functools.partial(cloud_kernel, devices, carry),
        out_shape=jax.ShapeDtypeStruct((cols, back), f32),
        in_specs=[VMEM, ANY, VMEM, ANY],
        out_specs=VMEM,
        scratch_shapes=[
            pltpu.VMEM((tiles, cz, SUB * (groups + 2), LANE), f32),
            pltpu.VMEM((tiles, cz, cx, LANE), f32),
            pltpu.VMEM((zp, cols), f32),
            pltpu.VMEM((zp, cols), f32),
            pltpu.VMEM((zp, cols), f32),
            pltpu.VMEM((5 * zp, cols), f32),
            pltpu.VMEM((2 * tiles, zp * SUB, LANE), f32),
            pltpu.VMEM((5 * zp, back), f32),
            pltpu.SemaphoreType.DMA((tiles, 5)),
            pltpu.SemaphoreType.DMA,
        ],
        compiler_params=pltpu.CompilerParams(vmem_limit_bytes=VMEM_CLOUD),
        name="cloud",
    )(r1, thermal_disturbance, layer_index_downscale, jnp.asarray(mean, f32))
    r2 = exchange(vals)

    lin = np.stack([power - np.eye(cz), total])
    halo = (r1,) if carry else ends
    base = pl.pallas_call(
        functools.partial(base_kernel, devices, carry),
        out_shape=(field,) * 2,
        in_specs=[VMEM] * 6 + [ANY] + [VMEM] * len(halo),
        out_specs=(VMEM,) * 2,
        compiler_params=pltpu.CompilerParams(vmem_limit_bytes=VMEM_PACK),
        cost_estimate=pl.CostEstimate(flops=10**8, bytes_accessed=10**6, transcendentals=0),
        name="base",
    )(*fields, layer_index_downscale, layer_index_upscale, jnp.asarray(lin, f32), vals, *halo)
    return pl.pallas_call(
        functools.partial(finish_kernel, zp),
        out_shape=(field,) * 3,
        in_specs=[VMEM] * 5,
        out_specs=(VMEM,) * 3,
        compiler_params=pltpu.CompilerParams(vmem_limit_bytes=VMEM_PACK),
        name="finish",
    )(r2, pos, layer_index_upscale, *base)


VMEM_PACK = 16 * 2**20
VMEM_CLOUD = 24 * 2**20


def solution(mesh):
    in_specs = (
        P(None, AXES),
        P(None, AXES),
        P(None, AXES),
        P(AXES),
        P(None, None, AXES),
        P(),
        P(),
    )
    out_specs = (P(None, AXES), P(None, AXES), P(None, AXES))
    return jax.shard_map(local, mesh=mesh, in_specs=in_specs, out_specs=out_specs, check_vma=False)
```

time: 59.6 us -> 50.6 us (0.85)
  starting transfers between devices: 9.19 us -> 2.67 us
  Pallas kernels: 18.3 us -> 13.6 us
  local copies, waits for them, and re-layouts: 2.02 us -> 6.58 us
  waiting for transfers between devices: 12 us -> 9.08 us
  blocking collectives: 16 us -> 17.4 us
  other arithmetic: 0.91 us -> 0 us
    ppermute x2 -> x0, starting transfers between devices: 6.53 us -> none  [the longest x1 3.42 us: edges(): high = lax.ppermute(block[:, :, :1], AXES, backward)]
    unnamed x9 -> x27, local copies, waits for them, and re-layouts: 2.02 us -> 6.58 us
    pallas_call x2 -> x3, Pallas kernels: 15.4 us -> 12.4 us  [the longest x1 11 us: local(): pl.pallas_call(functools.partial(cloud_kernel, devices, carry), out_shape...]
    ppermute x2 -> x0, waiting for transfers between devices: 2.51 us -> none  [the longest x1 2.07 us: edges(): low = lax.ppermute(block[:, :, -1:], AXES, forward)]
    pallas_call x1, Pallas kernels: 2.94 us -> 1.22 us  [local(): pl.pallas_call(functools.partial(finish_kernel, zp), out_shape=(field,) *...]
    all_to_all x1, blocking collectives: 16 us -> 17.4 us  [exchange(): lax.all_to_all(blocks, AXES, split_axis=0, concat_axis=0, tiled=True)]
    another operation x1 -> x0, other arithmetic: 0.91 us -> none  [local(): low, high = edges(jnp.stack([thermal_anomaly, vapour_anomaly]))]
  transfers between devices with their start and end apart: 3 -> 1, of which waited for: 3 -> 1; matrix products, arithmetic and copies ran while one was open for 1% -> 0% of each run, Pallas kernels for 0% -> 2%
where the time goes in v2:
time: 50.6 us; the launch traced here: 50.1 us
  blocking collectives  17.4 us (34%)
  Pallas kernels  13.6 us (27%)
  waiting for transfers between devices  9.08 us (18%)
  local copies, waits for them, and re-layouts  6.58 us (13%)
  starting transfers between devices  2.67 us (5%)
  between operations  0.74 us (1%)
    all_to_all x1, blocking collectives, exchange(): lax.all_to_all(blocks, AXES, split_axis=0, concat_axis=0, tiled=True)  17.4 us
    pallas_call x1, Pallas kernels, local(): pl.pallas_call(functools.partial(cloud_kernel, devices, carry), out_shape...  11 us
    all_to_all x1, waiting for transfers between devices, exchange(): lax.all_to_all(blocks, AXES, split_axis=0, concat_axis=0, tiled=True)  9.08 us
    unnamed x27, local copies, waits for them, and re-layouts  6.58 us
    all_to_all x1, starting transfers between devices, exchange(): lax.all_to_all(blocks, AXES, split_axis=0, concat_axis=0, tiled=True)  2.67 us
    pallas_call x1, Pallas kernels, local(): pl.pallas_call(functools.partial(finish_kernel, zp), out_shape=(field,) *...  1.22 us
  transfers between devices with their start and end apart: 1, of which 1 were waited for; matrix products, arithmetic and copies ran while one was open for 0% of the time, Pallas kernels for 2%

profile of v2, /device:TPU:0, one launch (start us, length us, event | category | flops | bytes accessed | tf_op | source)
XLA Modules:
  0.0 50.1 jit_solution(12208887485593443853)
XLA Ops:
  0.6 0.0 copy-start.1
  0.6 0.9 %copy-done.1 = f32[72,256]{1,0:T(8,128)S(1)} copy-done((f32[72,256]{1,0:T(8,128)S(1)}, f32[72,256]{1,0:T(8,128)}, u32[]{:S(2)}) %copy-start.1) | copy-done | bytes 73752
  1.5 0.0 copy-start.3
  1.5 0.9 %copy-done.3 = f32[72,256]{1,0:T(8,128)S(1)} copy-done((f32[72,256]{1,0:T(8,128)S(1)}, f32[72,256]{1,0:T(8,128)}, u32[]{:S(2)}) %copy-start.3) | copy-done | bytes 73752
  2.4 0.0 copy-start.5
  2.4 0.9 %copy-done.5 = f32[72,256]{1,0:T(8,128)S(1)} copy-done((f32[72,256]{1,0:T(8,128)S(1)}, f32[72,256]{1,0:T(8,128)}, u32[]{:S(2)}) %copy-start.5) | copy-done | bytes 73752
  3.3 0.0 copy-start.11
  3.3 0.7 %copy-done.11 = s32[256]{0:T(256)S(1)} copy-done((s32[256]{0:T(256)S(1)}, s32[256]{0:T(256)}, u32[]{:S(2)}) %copy-start.11) | copy-done | bytes 1048
  4.0 0.4 pack.1
  4.4 0.0 copy-start.12
  4.4 17.4 %all_to_all.10 = f32[32,8,256]{2,1,0:T(8,128)S(1)} all-to-all(f32[32,8,256]{2,1,0:T(8,128)S(1)} %bitcast.8), channel_id=1, replica_groups=mesh['tile'=8,'crm'=4] {'tile','crm'}, dimensions={0} | all-to-all | bytes 524288 | tf_op jit(solution)/shard_map/all_to_all | solution.py:425
  21.8 0.0 copy-start
  21.8 1.4 %copy-done = f32[50,32,256]{2,1,0:T(8,128)S(1)} copy-done((f32[50,32,256]{2,1,0:T(8,128)S(1)}, f32[50,32,256]{2,1,0:T(8,128)}, u32[]{:S(2)}) %copy-start) | copy-done | bytes 1638424
  23.2 0.0 copy-start.7
  23.2 1.0 %copy-done.7 = f32[280,256]{1,0:T(8,128)S(1)} copy-done((f32[280,256]{1,0:T(8,128)S(1)}, f32[280,256]{1,0:T(8,128)}, u32[]{:S(2)}) %copy-start.7) | copy-done | bytes 286744
  24.2 0.0 copy-start.8
  24.2 0.7 %copy-done.8 = f32[50,72]{1,0:T(8,128)S(1)} copy-done((f32[50,72]{1,0:T(8,128)S(1)}, f32[50,72]{1,0:T(8,128)}, u32[]{:S(2)}) %copy-start.8) | copy-done | bytes 14424
  24.9 0.0 copy-start.2
  24.9 0.0 copy-start.4
  24.9 0.0 copy-start.6
  24.9 0.0 copy-start.9
  24.9 0.0 copy-start.10
  24.9 11.0 %cloud.1.refs_6_ = f32[256,256]{1,0:T(8,128)} custom-call(f32[256,256]{1,0:T(8,128)S(1)} %bitcast.5, f32[50,32,256]{2,1,0:T(8,128)S(1)} %copy-done, f32[50,72]{1,0:T(8,128)S(1)} %copy-done.8, f32[280,256]{1,0:T(8,128)S(1)} %copy-done.7), custom_call_target="tpu_custom_call" | custom-call | tf_op jit(solution)/shard_map/cloud/pallas_call | solution.py:443
  35.9 2.7 %all-to-all-start.1 = ((f32[32,8,256]{2,1,0:T(8,128)}), f32[32,8,256]{2,1,0:T(8,128)S(1)}, u32[]{:S(2)}, u32[]{:S(2)}) async-start(f32[32,8,256]{2,1,0:T(8,128)} %bitcast.3), calls=%async_computation.1 | async-start | bytes 524288 | tf_op jit(solution)/shard_map/all_to_all | solution.py:425
  38.6 0.0 copy-done.12
  38.6 0.1 copy.13.refs_4_.up_ref
  38.7 0.0 copy-done.2
  38.7 0.0 copy-done.4
  38.7 0.0 copy-done.6
  38.7 0.0 copy-done.9
  38.7 0.0 copy-done.10
  38.7 1.0 %base.1 = (f32[72,256]{1,0:T(8,128)S(1)}, f32[72,256]{1,0:T(8,128)S(1)}) custom-call(f32[72,256]{1,0:T(8,128)S(1)} %copy-done.2, f32[72,256]{1,0:T(8,128)S(1)} %copy-done.4, f32[72,256]{1,0:T(8,128)S(1)} %copy-done.6, f32[50,72]{1,0:T(8,128)S(1)} %copy-done.9, f32[72,50]{1,0:T(8,128)S(1)} %copy.13.refs_4_.up_ref, f32[2,50,50]{2,1,0:T(8,128)S(1)} %copy-done.10, ...), custom_call_target="tpu_custom_call" | custom-call | flops 100000000 | bytes 1000000 | tf_op jit(solution)/shard_map/base/pallas_call | solution.py:467
  39.7 9.1 %all-to-all-done.1 = f32[32,8,256]{2,1,0:T(8,128)S(1)} async-done(((f32[32,8,256]{2,1,0:T(8,128)}), f32[32,8,256]{2,1,0:T(8,128)S(1)}, u32[]{:S(2)}, u32[]{:S(2)}) %all-to-all-start.1) | async-done | bytes 262176 | tf_op jit(solution)/shard_map/all_to_all | solution.py:425
  48.8 1.2 %finish.1 = (f32[72,256]{1,0:T(8,128)}, f32[72,256]{1,0:T(8,128)}, f32[72,256]{1,0:T(8,128)}) custom-call(f32[256,256]{1,0:T(8,128)S(1)} %bitcast.7, s32[1,256]{1,0:T(1,128)S(1)} %get-tuple-element.8.pos_ref, f32[72,50]{1,0:T(8,128)S(1)} %copy.13.refs_4_.up_ref, f32[72,256]{1,0:T(8,128)S(1)} %get-tuple-element.9.tb_ref, f32[72,256]{1,0:T(8,128)S(1)} %get-tuple-element.10.qb_ref), custom_call_target="tpu_custom_call" | custom-call | tf_op jit(solution)/shard_map/finish/pallas_call | solution.py:476
Async XLA Ops:
  0.6 0.9 %copy-start.1 = (f32[72,256]{1,0:T(8,128)S(1)}, f32[72,256]{1,0:T(8,128)}, u32[]{:S(2)}) copy-start(f32[72,256]{1,0:T(8,128)} %refs_0_.3) | copy-start | bytes 221188
  1.5 0.9 %copy-start.3 = (f32[72,256]{1,0:T(8,128)S(1)}, f32[72,256]{1,0:T(8,128)}, u32[]{:S(2)}) copy-start(f32[72,256]{1,0:T(8,128)} %refs_1_.3) | copy-start | bytes 221188
  2.4 0.9 %copy-start.5 = (f32[72,256]{1,0:T(8,128)S(1)}, f32[72,256]{1,0:T(8,128)}, u32[]{:S(2)}) copy-start(f32[72,256]{1,0:T(8,128)} %refs_2_.3) | copy-start | bytes 221188
  3.3 0.7 %copy-start.11 = (s32[256]{0:T(256)S(1)}, s32[256]{0:T(256)}, u32[]{:S(2)}) copy-start(s32[256]{0:T(256)} %param.12) | copy-start | bytes 3076
  4.4 34.2 %copy-start.12 = (f32[72,50]{0,1:T(8,128)S(1)}, f32[72,50]{0,1:T(8,128)}, u32[]{:S(2)}) copy-start(f32[72,50]{0,1:T(8,128)} %param.15) | copy-start | bytes 43204
  21.8 1.4 %copy-start = (f32[50,32,256]{2,1,0:T(8,128)S(1)}, f32[50,32,256]{2,1,0:T(8,128)}, u32[]{:S(2)}) copy-start(f32[50,32,256]{2,1,0:T(8,128)} %td_ref.1) | copy-start | bytes 4915204
  23.2 1.0 %copy-start.7 = (f32[280,256]{1,0:T(8,128)S(1)}, f32[280,256]{1,0:T(8,128)}, u32[]{:S(2)}) copy-start(f32[280,256]{1,0:T(8,128)} %constant.4.clone.mean_ref) | copy-start | bytes 860164
  24.2 0.7 %copy-start.8 = (f32[50,72]{1,0:T(8,128)S(1)}, f32[50,72]{1,0:T(8,128)}, u32[]{:S(2)}) copy-start(f32[50,72]{1,0:T(8,128)} %refs_3_.1) | copy-start | bytes 43204
  24.9 13.8 %copy-start.2 = (f32[72,256]{1,0:T(8,128)S(1)}, f32[72,256]{1,0:T(8,128)}, u32[]{:S(2)}) copy-start(f32[72,256]{1,0:T(8,128)} %refs_0_.3) | copy-start | bytes 221188
  24.9 13.8 %copy-start.4 = (f32[72,256]{1,0:T(8,128)S(1)}, f32[72,256]{1,0:T(8,128)}, u32[]{:S(2)}) copy-start(f32[72,256]{1,0:T(8,128)} %refs_1_.3) | copy-start | bytes 221188
  24.9 13.8 %copy-start.6 = (f32[72,256]{1,0:T(8,128)S(1)}, f32[72,256]{1,0:T(8,128)}, u32[]{:S(2)}) copy-start(f32[72,256]{1,0:T(8,128)} %refs_2_.3) | copy-start | bytes 221188
  24.9 13.8 %copy-start.9 = (f32[50,72]{1,0:T(8,128)S(1)}, f32[50,72]{1,0:T(8,128)}, u32[]{:S(2)}) copy-start(f32[50,72]{1,0:T(8,128)} %refs_3_.1) | copy-start | bytes 43204
  24.9 13.8 %copy-start.10 = (f32[2,50,50]{2,1,0:T(8,128)S(1)}, f32[2,50,50]{2,1,0:T(8,128)}, u32[]{:S(2)}) copy-start(f32[2,50,50]{2,1,0:T(8,128)} %constant.5.clone.refs_5_) | copy-start | bytes 60004
  35.9 12.9 %all-to-all-start.1 = ((f32[32,8,256]{2,1,0:T(8,128)}), f32[32,8,256]{2,1,0:T(8,128)S(1)}, u32[]{:S(2)}, u32[]{:S(2)}) async-start(f32[32,8,256]{2,1,0:T(8,128)} %bitcast.3), calls=%async_computation.1 | async-start | bytes 524288 | tf_op jit(solution)/shard_map/all_to_all | solution.py:425

commit v3 on v2

--- a/solution.py
+++ b/solution.py
@@ -26,6 +26,7 @@
 HI = lax.Precision.HIGH
 VMEM = pl.BlockSpec(memory_space=pltpu.VMEM)
 ANY = pl.BlockSpec(memory_space=pl.ANY)
+HBM = pl.BlockSpec(memory_space=pltpu.HBM)
 
 
 def up_to(n, m):
@@ -108,12 +109,18 @@
 
 
 def pack_kernel(devices, carry, *refs):
-    t_ref, q_ref, v_ref, own_ref = refs[:4]
     low_ref, high_ref = (None, None) if carry else refs[4:6]
-    out_ref, pos_ref, s_ref = refs[-3:]
+    out_ref, pos_ref, s_ref, t_ref, q_ref, v_ref, own_ref, sem = refs[-8:]
+    copies = [
+        pltpu.make_async_copy(source, target, sem.at[n])
+        for n, (source, target) in enumerate(zip(refs[:4], (t_ref, q_ref, v_ref, own_ref)))
+    ]
+    for n in (3, 0, 1, 2):
+        copies[n].start()
     nl, cols = t_ref.shape
     width = s_ref.shape[0]
     per = cols // devices
+    copies[3].wait()
     own = own_ref[...]
     who = lax.broadcasted_iota(jnp.int32, (devices, cols), 0)
     mine = jnp.where(who == own, 1.0, 0.0)
@@ -127,6 +134,8 @@
     pos_ref[...] = pos
     sel = onehot(pos, cols)
 
+    for n in range(3):
+        copies[n].wait()
     t = t_ref[...]
     x = q_ref[...] - 0.5 * t
     v = v_ref[...]
@@ -175,20 +184,34 @@
     return jnp.maximum(f, jnp.log2(1.0 + jnp.exp2(jnp.minimum(f, 100.0))))
 
 
-def cloud_kernel(devices, carry, r_ref, td_ref, down_ref, mean_ref, out_ref,
-                 d_ref, raw_ref, east_ref, west_ref, force_ref, val_ref, part_ref, mean_buf,
-                 td_sem, mean_sem):
+def lanes(k):
+    return pl.ds(k * LANE, LANE)
+
+
+def fold(part_ref, out_ref, k, scale):
+    levels = out_ref.shape[0]
+    total = part_ref[pl.ds(0, levels, stride=SUB), :]
+    for s in range(1, SUB):
+        total = total + part_ref[pl.ds(s, levels, stride=SUB), :]
+    out_ref[:, lanes(k)] = total * scale
+
+
+def clear_tail(part_ref, cz):
+    for n in range(part_ref.shape[0]):
+        for z in range(cz * SUB, part_ref.shape[1], SUB):
+            part_ref[n, pl.ds(z, SUB), :] = jnp.zeros((SUB, LANE), jnp.float32)
+
+
+def prep_kernel(carry, td_ref, down_ref, after_ref, start_ref, mean_ref, g_ref,
+                raw_ref, part_ref, td_sem):
+    del after_ref
     cz, cx, cols = td_ref.shape
     nl = down_ref.shape[1]
-    zp = east_ref.shape[0]
-    width = r_ref.shape[1]
-    per = cols // devices
+    zp = mean_ref.shape[0]
+    width = g_ref.shape[1]
     groups = cx // SUB
     tiles = cols // LANE
     chunk = -(-cz // td_sem.shape[1])
-
-    def lanes(k):
-        return pl.ds(k * LANE, LANE)
 
     def td_copy(k, c):
         levels = pl.ds(c * chunk, min(chunk, cz - c * chunk))
@@ -199,25 +222,51 @@
     for k in range(tiles):
         for c in range(td_sem.shape[1]):
             td_copy(k, c).start()
-    mean_copy = pltpu.make_async_copy(mean_ref, mean_buf, mean_sem)
-    mean_copy.start()
 
     down = jnp.concatenate(
         [down_ref[...], jnp.zeros((cz, width - nl), jnp.float32)], axis=1
     )
     down = jnp.concatenate([down, jnp.zeros((zp - cz, width), jnp.float32)], axis=0)
-    g = [down, pltpu.roll(down, nl, 1), pltpu.roll(down, 2 * nl, 1)]
+    for n in range(3):
+        g_ref[n * zp:(n + 1) * zp, :] = down if n == 0 else pltpu.roll(down, n * nl, 1)
     if carry:
-        first, second = halves(nl)
-        shape = (nl + first, width)
+        shape = (g_ref.shape[0] - 3 * zp, width)
         row = lax.broadcasted_iota(jnp.int32, shape, 0)
         to = jnp.where(row < nl, row + nl, row + 2 * nl)
-        g.append(jnp.where(lax.broadcasted_iota(jnp.int32, shape, 1) == to, 1.0, 0.0))
-    prof = dot(jnp.concatenate(g, axis=0), r_ref[...], 1, 1, HI)
+        g_ref[3 * zp:, :] = jnp.where(
+            lax.broadcasted_iota(jnp.int32, shape, 1) == to, 1.0, 0.0
+        )
+
+    clear_tail(part_ref, cz)
+    for k in range(tiles):
+        for z in range(cz):
+            if z % chunk == 0:
+                td_copy(k, z // chunk).wait()
+            total = None
+            for i in range(groups):
+                td = raw_ref[k, z, pl.ds(i, SUB, stride=groups), :]
+                total = td if total is None else total + td
+                start_ref[k, z, pl.ds(SUB * i, SUB), :] = (-0.5 * LOG2E) * td
+            part_ref[k, pl.ds(z * SUB, SUB), :] = total
+        fold(part_ref.at[k], mean_ref, k, 1.0 / cx)
+
+
+def cloud_kernel(devices, carry, nl, r_ref, start_ref, td_mean_ref, g_ref, mean_ref, out_ref,
+                 d_ref, east_ref, west_ref, force_ref, val_ref, part_ref, mean_buf, mean_sem):
+    tiles, cz, cx, _ = start_ref.shape
+    zp, cols = td_mean_ref.shape
+    per = cols // devices
+    groups = cx // SUB
+
+    mean_copy = pltpu.make_async_copy(mean_ref, mean_buf, mean_sem)
+    mean_copy.start()
+
+    prof = dot(g_ref[...], r_ref[...], 1, 1, HI)
     d0 = prof[0:zp]
     speed = max_speed * jnp.tanh(prof[zp:2 * zp])
     fd = prof[2 * zp:3 * zp]
     if carry:
+        first, second = halves(nl)
         v = prof[3 * zp:3 * zp + nl]
         ends = prof[3 * zp + nl:3 * zp + nl + first]
         flag = ends[second:second + 1] > 0.5
@@ -235,29 +284,23 @@
         halo = jnp.where(flag & (place == 0), behind, 0.0) + jnp.where(
             flag & (place == per - 1), ahead, 0.0
         )
-        fd = fd + dot(down[:, :nl], halo, 1, 0, HI)
+        fd = fd + dot(g_ref[0:zp, 0:nl], halo, 1, 0, HI)
     east_ref[...] = mix_along - 0.5 * speed
     west_ref[...] = mix_along + 0.5 * speed
     force_ref[...] = fd * (LOG2E / SUBSTEPS)
+    val_ref[0:zp, :] = td_mean_ref[...]
     val_ref[zp:2 * zp, :] = d0
     val_ref[2 * zp:3 * zp, :] = fd
+    clear_tail(part_ref, cz)
 
     def row_at(ref, z, k):
         return jnp.broadcast_to(ref[pl.ds(z, 1), lanes(k)], (SUB, LANE))
 
-    zeros = jnp.zeros((SUB, LANE), jnp.float32)
-    for n in range(part_ref.shape[0]):
-        for z in range(cz, zp):
-            part_ref[n, pl.ds(z * SUB, SUB), :] = zeros
-
-    def fold(n, k, base, scale):
-        total = part_ref[n, pl.ds(0, zp, stride=SUB), :]
-        for s in range(1, SUB):
-            total = total + part_ref[n, pl.ds(s, zp, stride=SUB), :]
-        val_ref[pl.ds(base, zp), lanes(k)] = total * scale
-
     slot = [0] + [SUB * (i + 1) for i in range(1, groups)]
     last = slot[-1]
+
+    def get(k, z):
+        return [d_ref[k, z, pl.ds(slot[i], SUB), :] for i in range(groups)]
 
     def put(k, z, i, new):
         d_ref[k, z, pl.ds(slot[i], SUB), :] = new
@@ -268,42 +311,39 @@
 
     for k in range(tiles):
         for z in range(cz):
-            if z % chunk == 0:
-                td_copy(k, z // chunk).wait()
             base = row_at(val_ref, zp + z, k) * LOG2E
-            total = None
             for i in range(groups):
-                td = raw_ref[k, z, pl.ds(i, SUB, stride=groups), :]
-                total = td if total is None else total + td
-                put(k, z, i, base - (0.5 * LOG2E) * td)
-            part_ref[k, pl.ds(z * SUB, SUB), :] = total
-        fold(k, k, 0, 1.0 / cx)
+                put(k, z, i, base + start_ref[k, z, pl.ds(SUB * i, SUB), :])
 
     drain = cond_rate * (1.0 + 0.5 * latent_heat)
 
     def step(_, carry):
         for k in range(tiles):
-            prev = cur = [d_ref[k, 0, pl.ds(slot[i], SUB), :] for i in range(groups)]
+            below = cur = get(k, 0)
+            pair = None
             for z in range(cz):
-                nxt = cur
-                if z + 1 < cz:
-                    nxt = [d_ref[k, z + 1, pl.ds(slot[i], SUB), :] for i in range(groups)]
+                above = get(k, z + 1) if z + 1 < cz else cur
+                if pair is None:
+                    pair = [c + a for c, a in zip(cur, above)]
+                    column = [p + b for p, b in zip(pair, below)]
+                else:
+                    column = [p + a for p, a in zip(pair, above)]
+                    pair = None
                 ea = row_at(east_ref, z, k)
                 we = row_at(west_ref, z, k)
                 fo = row_at(force_ref, z, k)
                 ring = [d_ref[k, z, pl.ds(last + SUB - 1, SUB), :]] + cur
                 ring = ring + [d_ref[k, z, pl.ds(1, SUB), :]]
                 for i in range(groups):
-                    f = cur[i]
                     new = (
-                        mix_vertical * ((prev[i] + f) + nxt[i])
+                        mix_vertical * column[i]
                         + ea * ring[i + 2]
                         + we * ring[i]
                         + fo
-                        - drain * softplus2(f)
+                        - drain * softplus2(cur[i])
                     )
                     put(k, z, i, new)
-                prev, cur = cur, nxt
+                below, cur = cur, above
         return carry
 
     lax.fori_loop(0, SUBSTEPS, step, 0)
@@ -311,15 +351,14 @@
     for k in range(tiles):
         for z in range(cz):
             total = cloud = None
-            for i in range(groups):
-                f = d_ref[k, z, pl.ds(slot[i], SUB), :]
+            for f in get(k, z):
                 c = softplus2(f)
                 total = f if total is None else total + f
                 cloud = c if cloud is None else cloud + c
             part_ref[2 * k, pl.ds(z * SUB, SUB), :] = total
             part_ref[2 * k + 1, pl.ds(z * SUB, SUB), :] = cloud
-        fold(2 * k, k, 3 * zp, LN2 / cx)
-        fold(2 * k + 1, k, 4 * zp, LN2 / cx)
+        fold(part_ref.at[2 * k], val_ref.at[pl.ds(3 * zp, zp)], k, LN2 / cx)
+        fold(part_ref.at[2 * k + 1], val_ref.at[pl.ds(4 * zp, zp)], k, LN2 / cx)
     val_ref[zp:2 * zp, :] = val_ref[zp:2 * zp, :] - 0.5 * val_ref[0:zp, :]
     mean_copy.wait()
     out_ref[...] = dot(val_ref[...], mean_buf[...], 0, 0, HI)
@@ -412,10 +451,17 @@
             jax.ShapeDtypeStruct((cols, width), f32),
             jax.ShapeDtypeStruct((1, cols), jnp.int32),
         ),
-        in_specs=[VMEM] * (4 + len(ends)),
+        in_specs=[HBM] * 4 + [VMEM] * len(ends),
         out_specs=(VMEM,) * 2,
-        scratch_shapes=[pltpu.VMEM((width, cols), f32)],
-        compiler_params=pltpu.CompilerParams(vmem_limit_bytes=VMEM_PACK),
+        scratch_shapes=[
+            pltpu.VMEM((width, cols), f32),
+            pltpu.VMEM((nl, cols), f32),
+            pltpu.VMEM((nl, cols), f32),
+            pltpu.VMEM((nl, cols), f32),
+            pltpu.VMEM((1, cols), jnp.int32),
+            pltpu.SemaphoreType.DMA((4,)),
+        ],
+        compiler_params=pltpu.CompilerParams(vmem_limit_bytes=VMEM_ALL),
         name="pack",
     )(*fields, processor_assignment.reshape(1, cols), *ends)
 
@@ -440,26 +486,43 @@
 
     tiles = cols // LANE
     groups = cx // SUB
+    level_rows = 3 * zp + (nl + halves(nl)[0] if carry else 0)
+    prep = pl.pallas_call(
+        functools.partial(prep_kernel, carry),
+        out_shape=(
+            jax.ShapeDtypeStruct((tiles, cz, cx, LANE), f32),
+            jax.ShapeDtypeStruct((zp, cols), f32),
+            jax.ShapeDtypeStruct((level_rows, width), f32),
+        ),
+        in_specs=[HBM, VMEM, ANY],
+        out_specs=(VMEM,) * 3,
+        scratch_shapes=[
+            pltpu.VMEM((tiles, cz, cx, LANE), f32),
+            pltpu.VMEM((tiles, zp * SUB, LANE), f32),
+            pltpu.SemaphoreType.DMA((tiles, 5)),
+        ],
+        compiler_params=pltpu.CompilerParams(vmem_limit_bytes=VMEM_PACK),
+        cost_estimate=pl.CostEstimate(flops=10**8, bytes_accessed=4 * 10**6, transcendentals=0),
+        name="prep",
+    )(thermal_disturbance, layer_index_downscale, out)
     vals = pl.pallas_call(
-        functools.partial(cloud_kernel, devices, carry),
+        functools.partial(cloud_kernel, devices, carry, nl),
         out_shape=jax.ShapeDtypeStruct((cols, back), f32),
-        in_specs=[VMEM, ANY, VMEM, ANY],
+        in_specs=[VMEM] * 4 + [HBM],
         out_specs=VMEM,
         scratch_shapes=[
             pltpu.VMEM((tiles, cz, SUB * (groups + 2), LANE), f32),
-            pltpu.VMEM((tiles, cz, cx, LANE), f32),
             pltpu.VMEM((zp, cols), f32),
             pltpu.VMEM((zp, cols), f32),
             pltpu.VMEM((zp, cols), f32),
             pltpu.VMEM((5 * zp, cols), f32),
             pltpu.VMEM((2 * tiles, zp * SUB, LANE), f32),
             pltpu.VMEM((5 * zp, back), f32),
-            pltpu.SemaphoreType.DMA((tiles, 5)),
             pltpu.SemaphoreType.DMA,
         ],
         compiler_params=pltpu.CompilerParams(vmem_limit_bytes=VMEM_CLOUD),
         name="cloud",
-    )(r1, thermal_disturbance, layer_index_downscale, jnp.asarray(mean, f32))
+    )(r1, *prep, jnp.asarray(mean, f32))
     r2 = exchange(vals)
 
     lin = np.stack([power - np.eye(cz), total])
@@ -483,6 +546,7 @@
     )(r2, pos, layer_index_upscale, *base)
 
 
+VMEM_ALL = 60 * 1024 * 2**10
 VMEM_PACK = 16 * 2**20
 VMEM_CLOUD = 24 * 2**20
 

time: 50.6 us -> 45.2 us (0.89)
  blocking collectives: 17.4 us -> 0 us
  starting transfers between devices: 2.67 us -> 10 us
  waiting for transfers between devices: 9.08 us -> 15.6 us
  local copies, waits for them, and re-layouts: 6.58 us -> 3.25 us
  Pallas kernels: 13.6 us -> 15.2 us
    all_to_all x1 -> x0, blocking collectives: 17.4 us -> none  [exchange(): lax.all_to_all(blocks, AXES, split_axis=0, concat_axis=0, tiled=True)]
    all_to_all x1 -> x2, starting transfers between devices: 2.67 us -> 10 us  [exchange(): lax.all_to_all(blocks, AXES, split_axis=0, concat_axis=0, tiled=True)]
    all_to_all x1 -> x2, waiting for transfers between devices: 9.08 us -> 15.6 us  [exchange(): lax.all_to_all(blocks, AXES, split_axis=0, concat_axis=0, tiled=True)]
    unnamed x27 -> x23, local copies, waits for them, and re-layouts: 6.58 us -> 3.25 us
    pallas_call x1, Pallas kernels: 0.43 us -> 2.12 us  [local(): pl.pallas_call(functools.partial(pack_kernel, devices, carry), out_shape=...]
    pallas_call x1 -> x2, Pallas kernels: 11 us -> 10.9 us  [the longest x1 10.3 us: local(): pl.pallas_call(functools.partial(cloud_kernel, devices, carry, nl), out_s...]
  transfers between devices with their start and end apart: 1 -> 2, of which waited for: 1 -> 2; matrix products, arithmetic and copies ran while one was open for 0% -> 0% of each run, Pallas kernels for 2% -> 4%
where the time goes in v3:
time: 45.2 us; the launch traced here: 44.8 us
  waiting for transfers between devices  15.6 us (35%)
  Pallas kernels  15.2 us (34%)
  starting transfers between devices  10 us (22%)
  local copies, waits for them, and re-layouts  3.25 us (7%)
  between operations  0.78 us (2%)
    all_to_all x2, waiting for transfers between devices, exchange(): lax.all_to_all(blocks, AXES, split_axis=0, concat_axis=0, tiled=True)  15.6 us
    pallas_call x1, Pallas kernels, local(): pl.pallas_call(functools.partial(cloud_kernel, devices, carry, nl), out_s...  10.3 us
    all_to_all x2, starting transfers between devices, exchange(): lax.all_to_all(blocks, AXES, split_axis=0, concat_axis=0, tiled=True)  10 us
    unnamed x23, local copies, waits for them, and re-layouts  3.25 us
    pallas_call x1, Pallas kernels, local(): pl.pallas_call(functools.partial(pack_kernel, devices, carry), out_shape=...  2.12 us
    pallas_call x1, Pallas kernels, local(): pl.pallas_call(functools.partial(finish_kernel, zp), out_shape=(field,) *...  1.22 us
    pallas_call x1, Pallas kernels, local(): pl.pallas_call(functools.partial(base_kernel, devices, carry), out_shape=...  1 us
  transfers between devices with their start and end apart: 2, of which 2 were waited for; matrix products, arithmetic and copies ran while one was open for 0% of the time, Pallas kernels for 4%

profile of v3, /device:TPU:0, one launch (start us, length us, event | category | flops | bytes accessed | tf_op | source)
XLA Modules:
  0.0 44.8 jit_solution(3198790525293532243)
XLA Ops:
  0.6 0.0 copy-start.5
  0.6 2.1 %pack.1 = (f32[256,256]{1,0:T(8,128)}, s32[1,256]{1,0:T(1,128)}) custom-call(f32[72,256]{1,0:T(8,128)} %refs_0_.3, f32[72,256]{1,0:T(8,128)} %refs_1_.3, f32[72,256]{1,0:T(8,128)} %refs_2_.3, s32[1,256]{1,0:T(1,128)} %bitcast.9), custom_call_target="tpu_custom_call" | custom-call | tf_op jit(solution)/shard_map/pack/pallas_call | solution.py:448
  2.8 7.3 %all-to-all-start = ((f32[32,8,256]{2,1,0:T(8,128)}), f32[32,8,256]{2,1,0:T(8,128)S(1)}, u32[]{:S(2)}, u32[]{:S(2)}) async-start(f32[32,8,256]{2,1,0:T(8,128)} %bitcast.8), calls=%async_computation | async-start | bytes 524288 | tf_op jit(solution)/shard_map/all_to_all | solution.py:471
  10.1 0.0 copy-start
  10.1 1.4 %copy-done = f32[50,32,256]{2,1,0:T(8,128)S(1)} copy-done((f32[50,32,256]{2,1,0:T(8,128)S(1)}, f32[50,32,256]{2,1,0:T(8,128)}, u32[]{:S(2)}) %copy-start) | copy-done | bytes 1638424
  11.5 0.0 copy-start.1
  11.5 0.9 %copy-done.1 = f32[256,256]{1,0:T(8,128)S(1)} copy-done((f32[256,256]{1,0:T(8,128)S(1)}, f32[256,256]{1,0:T(8,128)}, u32[]{:S(2)}) %copy-start.1) | copy-done | bytes 262168
  12.5 0.0 copy-start.6
  12.5 0.7 %copy-done.6 = f32[50,72]{1,0:T(8,128)S(1)} copy-done((f32[50,72]{1,0:T(8,128)S(1)}, f32[50,72]{1,0:T(8,128)}, u32[]{:S(2)}) %copy-start.6) | copy-done | bytes 14424
  13.2 0.6 %prep.1 = (f32[2,50,32,128]{3,2,1,0:T(8,128)S(1)}, f32[56,256]{1,0:T(8,128)S(1)}, f32[280,256]{1,0:T(8,128)S(1)}) custom-call(f32[50,32,256]{2,1,0:T(8,128)S(1)} %copy-done, f32[50,72]{1,0:T(8,128)S(1)} %copy-done.6, f32[256,256]{1,0:T(8,128)S(1)} %copy-done.1), custom_call_target="tpu_custom_call" | custom-call | flops 100000000 | bytes 4000000 | tf_op jit(solution)/shard_map/prep/pallas_call | solution.py:490
  13.8 6.5 %all-to-all-done = f32[32,8,256]{2,1,0:T(8,128)S(1)} async-done(((f32[32,8,256]{2,1,0:T(8,128)}), f32[32,8,256]{2,1,0:T(8,128)S(1)}, u32[]{:S(2)}, u32[]{:S(2)}) %all-to-all-start) | async-done | bytes 262176 | tf_op jit(solution)/shard_map/all_to_all | solution.py:471
  20.3 0.0 copy-done.5
  20.3 0.0 copy-start.10
  20.3 0.0 copy-start.2
  20.3 0.0 copy-start.3
  20.4 0.0 copy-start.4
  20.4 0.0 copy-start.7
  20.4 0.0 copy-start.8
  20.4 0.0 copy-start.9
  20.4 10.3 %cloud.1.refs_6_ = f32[256,256]{1,0:T(8,128)} custom-call(f32[256,256]{1,0:T(8,128)S(1)} %bitcast.5, f32[2,50,32,128]{3,2,1,0:T(8,128)S(1)} %get-tuple-element.11.start_ref, f32[56,256]{1,0:T(8,128)S(1)} %get-tuple-element.12.td_mean_ref, f32[280,256]{1,0:T(8,128)S(1)} %get-tuple-element.13.g_ref, f32[280,256]{1,0:T(8,128)S(1)} %copy-done.5), custom_call_target="tpu_custom_call" | custom-call | tf_op jit(solution)/shard_map/cloud/pallas_call | solution.py:508
  30.7 2.7 %all-to-all-start.1 = ((f32[32,8,256]{2,1,0:T(8,128)}), f32[32,8,256]{2,1,0:T(8,128)S(1)}, u32[]{:S(2)}, u32[]{:S(2)}) async-start(f32[32,8,256]{2,1,0:T(8,128)} %bitcast.3), calls=%async_computation.1 | async-start | bytes 524288 | tf_op jit(solution)/shard_map/all_to_all | solution.py:471
  33.4 0.0 copy-done.10
  33.4 0.1 copy.13.refs_4_.up_ref
  33.5 0.0 copy-done.2
  33.5 0.0 copy-done.3
  33.5 0.0 copy-done.4
  33.5 0.0 copy-done.7
  33.5 0.0 copy-done.8
  33.5 1.0 %base.1 = (f32[72,256]{1,0:T(8,128)S(1)}, f32[72,256]{1,0:T(8,128)S(1)}) custom-call(f32[72,256]{1,0:T(8,128)S(1)} %copy-done.2, f32[72,256]{1,0:T(8,128)S(1)} %copy-done.3, f32[72,256]{1,0:T(8,128)S(1)} %copy-done.4, f32[50,72]{1,0:T(8,128)S(1)} %copy-done.7, f32[72,50]{1,0:T(8,128)S(1)} %copy.13.refs_4_.up_ref, f32[2,50,50]{2,1,0:T(8,128)S(1)} %copy-done.8, ...), custom_call_target="tpu_custom_call" | custom-call | flops 100000000 | bytes 1000000 | tf_op jit(solution)/shard_map/base/pallas_call | solution.py:530
  34.5 9.1 %all-to-all-done.1 = f32[32,8,256]{2,1,0:T(8,128)S(1)} async-done(((f32[32,8,256]{2,1,0:T(8,128)}), f32[32,8,256]{2,1,0:T(8,128)S(1)}, u32[]{:S(2)}, u32[]{:S(2)}) %all-to-all-start.1) | async-done | bytes 262176 | tf_op jit(solution)/shard_map/all_to_all | solution.py:471
  43.6 0.0 copy-done.9
  43.6 1.2 %finish.1 = (f32[72,256]{1,0:T(8,128)}, f32[72,256]{1,0:T(8,128)}, f32[72,256]{1,0:T(8,128)}) custom-call(f32[256,256]{1,0:T(8,128)S(1)} %bitcast.7, s32[1,256]{1,0:T(1,128)S(1)} %copy-done.9, f32[72,50]{1,0:T(8,128)S(1)} %copy.13.refs_4_.up_ref, f32[72,256]{1,0:T(8,128)S(1)} %get-tuple-element.15.tb_ref, f32[72,256]{1,0:T(8,128)S(1)} %get-tuple-element.16.qb_ref), custom_call_target="tpu_custom_call" | custom-call | tf_op jit(solution)/shard_map/finish/pallas_call | solution.py:539
Async XLA Ops:
  0.6 19.7 %copy-start.5 = (f32[280,256]{1,0:T(8,128)S(1)}, f32[280,256]{1,0:T(8,128)}, u32[]{:S(2)}) copy-start(f32[280,256]{1,0:T(8,128)} %constant.4.clone.mean_ref) | copy-start | bytes 860164
  2.8 17.6 %all-to-all-start = ((f32[32,8,256]{2,1,0:T(8,128)}), f32[32,8,256]{2,1,0:T(8,128)S(1)}, u32[]{:S(2)}, u32[]{:S(2)}) async-start(f32[32,8,256]{2,1,0:T(8,128)} %bitcast.8), calls=%async_computation | async-start | bytes 524288 | tf_op jit(solution)/shard_map/all_to_all | solution.py:471
  10.1 1.4 %copy-start = (f32[50,32,256]{2,1,0:T(8,128)S(1)}, f32[50,32,256]{2,1,0:T(8,128)}, u32[]{:S(2)}) copy-start(f32[50,32,256]{2,1,0:T(8,128)} %td_ref.1) | copy-start | bytes 4915204
  11.5 0.9 %copy-start.1 = (f32[256,256]{1,0:T(8,128)S(1)}, f32[256,256]{1,0:T(8,128)}, u32[]{:S(2)}) copy-start(f32[256,256]{1,0:T(8,128)} %get-tuple-element.10.after_ref) | copy-start | bytes 786436
  12.5 0.7 %copy-start.6 = (f32[50,72]{1,0:T(8,128)S(1)}, f32[50,72]{1,0:T(8,128)}, u32[]{:S(2)}) copy-start(f32[50,72]{1,0:T(8,128)} %refs_3_.1) | copy-start | bytes 43204
  20.3 13.0 %copy-start.10 = (f32[72,50]{0,1:T(8,128)S(1)}, f32[72,50]{0,1:T(8,128)}, u32[]{:S(2)}) copy-start(f32[72,50]{0,1:T(8,128)} %param.15) | copy-start | bytes 43204
  20.3 13.1 %copy-start.2 = (f32[72,256]{1,0:T(8,128)S(1)}, f32[72,256]{1,0:T(8,128)}, u32[]{:S(2)}) copy-start(f32[72,256]{1,0:T(8,128)} %refs_0_.3) | copy-start | bytes 221188
  20.3 13.1 %copy-start.3 = (f32[72,256]{1,0:T(8,128)S(1)}, f32[72,256]{1,0:T(8,128)}, u32[]{:S(2)}) copy-start(f32[72,256]{1,0:T(8,128)} %refs_1_.3) | copy-start | bytes 221188
  20.4 13.1 %copy-start.4 = (f32[72,256]{1,0:T(8,128)S(1)}, f32[72,256]{1,0:T(8,128)}, u32[]{:S(2)}) copy-start(f32[72,256]{1,0:T(8,128)} %refs_2_.3) | copy-start | bytes 221188
  20.4 13.1 %copy-start.7 = (f32[50,72]{1,0:T(8,128)S(1)}, f32[50,72]{1,0:T(8,128)}, u32[]{:S(2)}) copy-start(f32[50,72]{1,0:T(8,128)} %refs_3_.1) | copy-start | bytes 43204
  20.4 13.1 %copy-start.8 = (f32[2,50,50]{2,1,0:T(8,128)S(1)}, f32[2,50,50]{2,1,0:T(8,128)}, u32[]{:S(2)}) copy-start(f32[2,50,50]{2,1,0:T(8,128)} %constant.5.clone.refs_5_) | copy-start | bytes 60004
  20.4 23.2 %copy-start.9 = (s32[1,256]{1,0:T(1,128)S(1)}, s32[1,256]{1,0:T(1,128)}, u32[]{:S(2)}) copy-start(s32[1,256]{1,0:T(1,128)} %get-tuple-element.14.pos_ref) | copy-start | bytes 3076
  30.7 12.9 %all-to-all-start.1 = ((f32[32,8,256]{2,1,0:T(8,128)}), f32[32,8,256]{2,1,0:T(8,128)S(1)}, u32[]{:S(2)}, u32[]{:S(2)}) async-start(f32[32,8,256]{2,1,0:T(8,128)} %bitcast.3), calls=%async_computation.1 | async-start | bytes 524288 | tf_op jit(solution)/shard_map/all_to_all | solution.py:471

commit v4 on v3

--- a/solution.py
+++ b/solution.py
@@ -25,8 +25,11 @@
 LANE = 128
 HI = lax.Precision.HIGH
 VMEM = pl.BlockSpec(memory_space=pltpu.VMEM)
-ANY = pl.BlockSpec(memory_space=pl.ANY)
 HBM = pl.BlockSpec(memory_space=pltpu.HBM)
+
+
+def in_hbm(x):
+    return pltpu.with_memory_space_constraint(x, pltpu.HBM)
 
 
 def up_to(n, m):
@@ -86,6 +89,24 @@
 def onehot(pos_row, cols):
     place = lax.broadcasted_iota(jnp.int32, (cols, cols), 0)
     return jnp.where(place == pos_row, 1.0, 0.0).astype(jnp.bfloat16)
+
+
+SLOT = 32
+SLOTS = LANE // SLOT
+
+
+def return_shape(cz, per):
+    head = (LANE - 2 * cz) // SUB * SUB
+    assert 0 <= head <= cz and cz - head <= SLOT
+    return head, per + -(-per // SLOTS)
+
+
+def slot_onehot(place_row, devices, per, cols):
+    row = place_row % per // SLOTS * devices + place_row // per
+    rows = -(-per // SLOTS) * devices
+    return jnp.where(
+        lax.broadcasted_iota(jnp.int32, (rows, cols), 0) == row, 1.0, 0.0
+    ).astype(jnp.bfloat16)
 
 
 CARRIED = (
@@ -180,6 +201,13 @@
     out_ref[...] = out
 
 
+LARGEST = 120.0
+
+
+def small_softplus2(f):
+    return jnp.log2(1.0 + jnp.exp2(f))
+
+
 def softplus2(f):
     return jnp.maximum(f, jnp.log2(1.0 + jnp.exp2(jnp.minimum(f, 100.0))))
 
@@ -202,7 +230,7 @@
             part_ref[n, pl.ds(z, SUB), :] = jnp.zeros((SUB, LANE), jnp.float32)
 
 
-def prep_kernel(carry, td_ref, down_ref, after_ref, start_ref, mean_ref, g_ref,
+def prep_kernel(carry, td_ref, down_ref, after_ref, start_ref, mean_ref, g_ref, most_ref,
                 raw_ref, part_ref, td_sem):
     del after_ref
     cz, cx, cols = td_ref.shape
@@ -238,6 +266,7 @@
         )
 
     clear_tail(part_ref, cz)
+    most = [jnp.zeros((SUB, LANE), jnp.float32)] * groups
     for k in range(tiles):
         for z in range(cz):
             if z % chunk == 0:
@@ -246,20 +275,20 @@
             for i in range(groups):
                 td = raw_ref[k, z, pl.ds(i, SUB, stride=groups), :]
                 total = td if total is None else total + td
-                start_ref[k, z, pl.ds(SUB * i, SUB), :] = (-0.5 * LOG2E) * td
+                first = (-0.5 * LOG2E) * td
+                start_ref[k, z, pl.ds(SUB * i, SUB), :] = first
+                most[i] = jnp.maximum(most[i], jnp.abs(first))
             part_ref[k, pl.ds(z * SUB, SUB), :] = total
         fold(part_ref.at[k], mean_ref, k, 1.0 / cx)
-
-
-def cloud_kernel(devices, carry, nl, r_ref, start_ref, td_mean_ref, g_ref, mean_ref, out_ref,
-                 d_ref, east_ref, west_ref, force_ref, val_ref, part_ref, mean_buf, mean_sem):
+    most_ref[...] = functools.reduce(jnp.maximum, most)
+
+
+def cloud_kernel(devices, carry, nl, r_ref, start_ref, td_mean_ref, g_ref, most_ref, mean_ref,
+                 out_ref, d_ref, base_ref, east_ref, west_ref, force_ref, val_ref, part_ref):
     tiles, cz, cx, _ = start_ref.shape
     zp, cols = td_mean_ref.shape
     per = cols // devices
     groups = cx // SUB
-
-    mean_copy = pltpu.make_async_copy(mean_ref, mean_buf, mean_sem)
-    mean_copy.start()
 
     prof = dot(g_ref[...], r_ref[...], 1, 1, HI)
     d0 = prof[0:zp]
@@ -285,11 +314,20 @@
             flag & (place == per - 1), ahead, 0.0
         )
         fd = fd + dot(g_ref[0:zp, 0:nl], halo, 1, 0, HI)
+    base_ref[...] = d0 * LOG2E
     east_ref[...] = mix_along - 0.5 * speed
     west_ref[...] = mix_along + 0.5 * speed
-    force_ref[...] = fd * (LOG2E / SUBSTEPS)
+    force = fd * (LOG2E / SUBSTEPS)
+    force_ref[...] = force
+    drain = cond_rate * (1.0 + 0.5 * latent_heat)
+    rate = 1.0 - 2.0 * mix_along + max(2.0 * mix_along, max_speed)
+    growth = rate**SUBSTEPS
+    series = sum(rate**n for n in range(SUBSTEPS))
+    bound = growth * (jnp.max(jnp.abs(d0)) * LOG2E + jnp.max(most_ref[...])) + series * (
+        jnp.max(jnp.abs(force)) + drain
+    )
     val_ref[0:zp, :] = td_mean_ref[...]
-    val_ref[zp:2 * zp, :] = d0
+    val_ref[zp:2 * zp, :] = d0 - 0.5 * td_mean_ref[...]
     val_ref[2 * zp:3 * zp, :] = fd
     clear_tail(part_ref, cz)
 
@@ -311,13 +349,11 @@
 
     for k in range(tiles):
         for z in range(cz):
-            base = row_at(val_ref, zp + z, k) * LOG2E
+            base = row_at(base_ref, z, k)
             for i in range(groups):
                 put(k, z, i, base + start_ref[k, z, pl.ds(SUB * i, SUB), :])
 
-    drain = cond_rate * (1.0 + 0.5 * latent_heat)
-
-    def step(_, carry):
+    def step(softplus, _, carry):
         for k in range(tiles):
             below = cur = get(k, 0)
             pair = None
@@ -340,14 +376,22 @@
                         + ea * ring[i + 2]
                         + we * ring[i]
                         + fo
-                        - drain * softplus2(cur[i])
+                        - drain * softplus(cur[i])
                     )
                     put(k, z, i, new)
                 below, cur = cur, above
         return carry
 
-    lax.fori_loop(0, SUBSTEPS, step, 0)
-
+    @pl.when(bound < LARGEST)
+    def _():
+        lax.fori_loop(0, SUBSTEPS, functools.partial(step, small_softplus2), 0)
+
+    @pl.when(jnp.logical_not(bound < LARGEST))
+    def _():
+        lax.fori_loop(0, SUBSTEPS, functools.partial(step, softplus2), 0)
+
+    head, rows = return_shape(cz, per)
+    cloud_ref = east_ref
     for k in range(tiles):
         for z in range(cz):
             total = cloud = None
@@ -358,19 +402,44 @@
             part_ref[2 * k, pl.ds(z * SUB, SUB), :] = total
             part_ref[2 * k + 1, pl.ds(z * SUB, SUB), :] = cloud
         fold(part_ref.at[2 * k], val_ref.at[pl.ds(3 * zp, zp)], k, LN2 / cx)
-        fold(part_ref.at[2 * k + 1], val_ref.at[pl.ds(4 * zp, zp)], k, LN2 / cx)
-    val_ref[zp:2 * zp, :] = val_ref[zp:2 * zp, :] - 0.5 * val_ref[0:zp, :]
-    mean_copy.wait()
-    out_ref[...] = dot(val_ref[...], mean_buf[...], 0, 0, HI)
+        fold(part_ref.at[2 * k + 1], cloud_ref, k, LN2 / cx)
+        val_ref[4 * zp:, lanes(k)] = cloud_ref[0:head, lanes(k)]
+        main = dot(val_ref[:, lanes(k)], mean_ref[...], 0, 0, HI)
+        for h in range(LANE // per):
+            out_ref[pl.ds((k * (LANE // per) + h) * rows, per), :] = main[h * per:(h + 1) * per]
+    left = cloud_ref[head:, :]
+    left = jnp.concatenate([left, jnp.zeros((SLOT - left.shape[0], cols), jnp.float32)], axis=0) \
+        if left.shape[0] < SLOT else left
+    place = lax.broadcasted_iota(jnp.int32, (1, cols), 1)
+    part = place % SLOTS
+    spread = jnp.concatenate(
+        [jnp.where(part == j, left, 0.0) for j in range(SLOTS)], axis=0
+    )
+    pick = slot_onehot(place, devices, per, cols)
+    a, b = split(spread)
+    extra = dot(pick, a, 1, 1) + dot(pick, b, 1, 1)
+    for i in range(rows - per):
+        out_ref[pl.ds(per + i, devices, stride=rows), :] = extra[i * devices:(i + 1) * devices]
 
 
 def base_kernel(devices, carry, *refs):
-    t_ref, q_ref, v_ref, down_ref, up_ref, lin_ref, after_ref, r_ref = refs[:8]
-    high_ref = None if carry else refs[8]
-    to_ref, qo_ref = refs[-2:]
+    t_ref, q_ref, v_ref, down_ref, up_ref, lin_ref, pos_ref, after_ref, r_ref = refs[:9]
+    high_ref = None if carry else refs[9]
+    to_ref, qo_ref, level_ref, rest_ref, sel_ref, pick_ref = refs[-6:]
     del after_ref
     nl, cols = t_ref.shape
+    cz = up_ref.shape[1]
     per = cols // devices
+    head, _ = return_shape(cz, per)
+    up = up_ref[...]
+    wide = jnp.concatenate([up, jnp.zeros((nl, LANE - cz), jnp.float32)], axis=1)
+    lane = lax.broadcasted_iota(jnp.int32, wide.shape, 1)
+    level_ref[0:nl, :] = wide
+    level_ref[nl:2 * nl, :] = -pltpu.roll(wide, cz, 1)
+    level_ref[2 * nl:3 * nl, :] = pltpu.roll(jnp.where(lane < head, wide, 0.0), 2 * cz, 1)
+    rest_ref[...] = jnp.where(lane < SLOT, pltpu.roll(wide, LANE - head, 1), 0.0)
+    sel_ref[...] = onehot(pos_ref[...], cols)
+    pick_ref[...] = slot_onehot(pos_ref[...], devices, per, cols)
     if carry:
         first, second = halves(nl)
         me = lax.axis_index(AXES)
@@ -404,23 +473,32 @@
     prof = dot(down_ref[...], jnp.concatenate([t, q, advt, advq], axis=1), 1, 0, HI)
     lin = lin_ref[...]
     gain = dot(lin[0], prof[:, :2 * cols], 1, 0, HI) + dot(lin[1], prof[:, 2 * cols:], 1, 0, HI)
-    gain = dot(up_ref[...], gain, 1, 0, HI)
+    gain = dot(up, gain, 1, 0, HI)
     to_ref[...] = t + advt + gain[:, :cols]
     qo_ref[...] = q + advq + gain[:, cols:]
 
 
-def finish_kernel(zp, r_ref, pos_ref, up_ref, tb_ref, qb_ref, to_ref, qo_ref, co_ref):
+def finish_kernel(devices, r_ref, pos_ref, tb_ref, qb_ref, level_ref, rest_ref, sel_ref, pick_ref,
+                  to_ref, qo_ref, co_ref):
     nl, cols = tb_ref.shape
-    cz = up_ref.shape[1]
-    width = r_ref.shape[1]
-    up = jnp.concatenate([up_ref[...], jnp.zeros((nl, width - cz), jnp.float32)], axis=1)
-    up = jnp.concatenate([up, -pltpu.roll(up, zp, 1), pltpu.roll(up, 2 * zp, 1)], axis=0)
-    sel = onehot(pos_ref[...], cols)
-    a, b = split(dot(up, r_ref[...], 1, 1, HI))
-    out = dot(a, sel, 1, 0) + dot(b, sel, 1, 0)
+    per = cols // devices
+    rows = r_ref.shape[0] // devices
+    main = jnp.concatenate([r_ref[pl.ds(h * rows, per), :] for h in range(devices)], axis=0)
+    extra = jnp.concatenate(
+        [r_ref[pl.ds(per + i, devices, stride=rows), :] for i in range(rows - per)], axis=0
+    )
+    a, b = split(extra)
+    extra = dot(a, pick_ref[...], 0, 0) + dot(b, pick_ref[...], 0, 0)
+    part = pos_ref[...] % per % SLOTS
+    left = jnp.where(part == 0, extra[:SLOT], 0.0)
+    for j in range(1, SLOTS):
+        left = left + jnp.where(part == j, extra[j * SLOT:(j + 1) * SLOT], 0.0)
+    rest = dot(rest_ref[:, 0:SLOT], left, 1, 0, HI)
+    a, b = split(dot(level_ref[...], main, 1, 1, HI))
+    out = dot(a, sel_ref[...], 1, 0) + dot(b, sel_ref[...], 1, 0)
     to_ref[...] = tb_ref[...] + out[0:nl]
     qo_ref[...] = qb_ref[...] + out[nl:2 * nl]
-    co_ref[...] = out[2 * nl:3 * nl]
+    co_ref[...] = out[2 * nl:3 * nl] + rest
 
 
 def local(
@@ -439,7 +517,7 @@
     zp = up_to(cz, SUB)
     f32 = jnp.float32
     width = up_to(3 * nl, LANE)
-    back = up_to(3 * zp, LANE)
+    head, rows = return_shape(cz, per)
     field = jax.ShapeDtypeStruct((nl, cols), f32)
     carry = carries(nl, per, width)
 
@@ -461,28 +539,28 @@
             pltpu.VMEM((1, cols), jnp.int32),
             pltpu.SemaphoreType.DMA((4,)),
         ],
-        compiler_params=pltpu.CompilerParams(vmem_limit_bytes=VMEM_ALL),
+        compiler_params=pltpu.CompilerParams(vmem_limit_bytes=VMEM_PACK),
         name="pack",
-    )(*fields, processor_assignment.reshape(1, cols), *ends)
-
-    def exchange(blocks):
+    )(*[in_hbm(f) for f in (*fields, processor_assignment.reshape(1, cols))], *ends)
+
+    def exchange(blocks, *inner):
         shape = blocks.shape
-        blocks = blocks.reshape(devices, per, shape[1])
+        blocks = blocks.reshape(devices, *inner)
         return lax.all_to_all(blocks, AXES, split_axis=0, concat_axis=0, tiled=True).reshape(shape)
 
-    r1 = exchange(out)
+    r1 = exchange(out, per, width)
 
     power, total = mean_operators(cz)
     release = 1.0 + 0.5 * latent_heat
-    mean = np.zeros((5 * zp, back))
-    z_part = np.zeros((5 * zp, cz))
+    mean = np.zeros((4 * zp + head, LANE))
+    z_part = np.zeros((4 * zp + head, cz))
     z_part[zp:zp + cz] = power.T / release
     z_part[2 * zp:2 * zp + cz] = total.T / release
     z_part[3 * zp:3 * zp + cz] = -np.eye(cz) / release
     mean[0:cz, 0:cz] = power.T
     mean[:, 0:cz] += latent_heat * z_part
-    mean[:, zp:zp + cz] = z_part
-    mean[4 * zp:4 * zp + cz, 2 * zp:2 * zp + cz] = np.eye(cz)
+    mean[:, cz:2 * cz] = z_part
+    mean[4 * zp:, 2 * cz:2 * cz + head] = np.eye(head)
 
     tiles = cols // LANE
     groups = cx // SUB
@@ -493,9 +571,10 @@
             jax.ShapeDtypeStruct((tiles, cz, cx, LANE), f32),
             jax.ShapeDtypeStruct((zp, cols), f32),
             jax.ShapeDtypeStruct((level_rows, width), f32),
+            jax.ShapeDtypeStruct((SUB, LANE), f32),
         ),
-        in_specs=[HBM, VMEM, ANY],
-        out_specs=(VMEM,) * 3,
+        in_specs=[HBM, VMEM, HBM],
+        out_specs=(VMEM,) * 4,
         scratch_shapes=[
             pltpu.VMEM((tiles, cz, cx, LANE), f32),
             pltpu.VMEM((tiles, zp * SUB, LANE), f32),
@@ -504,49 +583,54 @@
         compiler_params=pltpu.CompilerParams(vmem_limit_bytes=VMEM_PACK),
         cost_estimate=pl.CostEstimate(flops=10**8, bytes_accessed=4 * 10**6, transcendentals=0),
         name="prep",
-    )(thermal_disturbance, layer_index_downscale, out)
+    )(in_hbm(thermal_disturbance), layer_index_downscale, in_hbm(out))
     vals = pl.pallas_call(
         functools.partial(cloud_kernel, devices, carry, nl),
-        out_shape=jax.ShapeDtypeStruct((cols, back), f32),
-        in_specs=[VMEM] * 4 + [HBM],
+        out_shape=jax.ShapeDtypeStruct((devices * rows, LANE), f32),
+        in_specs=[VMEM] * 6,
         out_specs=VMEM,
         scratch_shapes=[
             pltpu.VMEM((tiles, cz, SUB * (groups + 2), LANE), f32),
             pltpu.VMEM((zp, cols), f32),
             pltpu.VMEM((zp, cols), f32),
             pltpu.VMEM((zp, cols), f32),
-            pltpu.VMEM((5 * zp, cols), f32),
+            pltpu.VMEM((zp, cols), f32),
+            pltpu.VMEM((4 * zp + head, cols), f32),
             pltpu.VMEM((2 * tiles, zp * SUB, LANE), f32),
-            pltpu.VMEM((5 * zp, back), f32),
-            pltpu.SemaphoreType.DMA,
         ],
         compiler_params=pltpu.CompilerParams(vmem_limit_bytes=VMEM_CLOUD),
         name="cloud",
     )(r1, *prep, jnp.asarray(mean, f32))
-    r2 = exchange(vals)
+    r2 = exchange(vals, 1, rows * LANE)
 
     lin = np.stack([power - np.eye(cz), total])
     halo = (r1,) if carry else ends
     base = pl.pallas_call(
         functools.partial(base_kernel, devices, carry),
-        out_shape=(field,) * 2,
-        in_specs=[VMEM] * 6 + [ANY] + [VMEM] * len(halo),
-        out_specs=(VMEM,) * 2,
+        out_shape=(
+            field,
+            field,
+            jax.ShapeDtypeStruct((3 * nl, LANE), f32),
+            jax.ShapeDtypeStruct((nl, LANE), f32),
+            jax.ShapeDtypeStruct((cols, cols), jnp.bfloat16),
+            jax.ShapeDtypeStruct((devices * (rows - per), cols), jnp.bfloat16),
+        ),
+        in_specs=[VMEM] * 7 + [HBM] + [VMEM] * len(halo),
+        out_specs=(VMEM,) * 6,
         compiler_params=pltpu.CompilerParams(vmem_limit_bytes=VMEM_PACK),
         cost_estimate=pl.CostEstimate(flops=10**8, bytes_accessed=10**6, transcendentals=0),
         name="base",
-    )(*fields, layer_index_downscale, layer_index_upscale, jnp.asarray(lin, f32), vals, *halo)
+    )(*fields, layer_index_downscale, layer_index_upscale, jnp.asarray(lin, f32), pos, in_hbm(vals), *halo)
     return pl.pallas_call(
-        functools.partial(finish_kernel, zp),
+        functools.partial(finish_kernel, devices),
         out_shape=(field,) * 3,
-        in_specs=[VMEM] * 5,
+        in_specs=[VMEM] * 8,
         out_specs=(VMEM,) * 3,
         compiler_params=pltpu.CompilerParams(vmem_limit_bytes=VMEM_PACK),
         name="finish",
-    )(r2, pos, layer_index_upscale, *base)
-
-
-VMEM_ALL = 60 * 1024 * 2**10
+    )(r2, pos, *base)
+
+
 VMEM_PACK = 16 * 2**20
 VMEM_CLOUD = 24 * 2**20
 

time: 45.2 us -> 42.4 us (0.938)
  local copies, waits for them, and re-layouts: 3.25 us -> 0.88 us
    unnamed x23 -> x17, local copies, waits for them, and re-layouts: 3.25 us -> 0.88 us
    pallas_call x1, Pallas kernels: 10.3 us -> 8.99 us  [local(): pl.pallas_call(functools.partial(cloud_kernel, devices, carry, nl), out_s...]
    pallas_call x1, Pallas kernels: 0.59 us -> 1.64 us  [local(): pl.pallas_call(functools.partial(prep_kernel, carry), out_shape=(jax.Shap...]
  transfers between devices with their start and end apart: 2 -> 2, of which waited for: 2 -> 2; matrix products, arithmetic and copies ran while one was open for 0% -> 0% of each run, Pallas kernels for 4% -> 6%
where the time goes in v4:
time: 42.4 us; the launch traced here: 42.1 us
  waiting for transfers between devices  15.4 us (36%)
  Pallas kernels  15 us (35%)
  starting transfers between devices  9.99 us (24%)
  local copies, waits for them, and re-layouts  0.88 us (2%)
  between operations  0.77 us (2%)
    all_to_all x2, waiting for transfers between devices, exchange(): lax.all_to_all(blocks, AXES, split_axis=0, concat_axis=0, tiled=True)  15.4 us
    all_to_all x2, starting transfers between devices, exchange(): lax.all_to_all(blocks, AXES, split_axis=0, concat_axis=0, tiled=True)  9.99 us
    pallas_call x1, Pallas kernels, local(): pl.pallas_call(functools.partial(cloud_kernel, devices, carry, nl), out_s...  8.99 us
    pallas_call x1, Pallas kernels, local(): pl.pallas_call(functools.partial(pack_kernel, devices, carry), out_shape=...  2.12 us
    pallas_call x1, Pallas kernels, local(): pl.pallas_call(functools.partial(prep_kernel, carry), out_shape=(jax.Shap...  1.64 us
    pallas_call x1, Pallas kernels, local(): pl.pallas_call(functools.partial(finish_kernel, devices), out_shape=(fiel...  1.23 us
    pallas_call x1, Pallas kernels, local(): pl.pallas_call(functools.partial(base_kernel, devices, carry), out_shape=...  1.04 us
    unnamed x17, local copies, waits for them, and re-layouts  0.88 us
  transfers between devices with their start and end apart: 2, of which 2 were waited for; matrix products, arithmetic and copies ran while one was open for 0% of the time, Pallas kernels for 6%

profile of v4, /device:TPU:0, one launch (start us, length us, event | category | flops | bytes accessed | tf_op | source)
XLA Modules:
  0.0 42.1 jit_solution(1023827028773731245)
XLA Ops:
  0.6 0.0 copy-start.3
  0.6 2.1 %pack.1 = (f32[256,256]{1,0:T(8,128)}, s32[1,256]{1,0:T(1,128)S(1)}) custom-call(f32[72,256]{1,0:T(8,128)} %refs_0_.3, f32[72,256]{1,0:T(8,128)} %refs_1_.3, f32[72,256]{1,0:T(8,128)} %refs_2_.3, s32[1,256]{1,0:T(1,128)} %bitcast.8), custom_call_target="tpu_custom_call" | custom-call | tf_op jit(solution)/shard_map/pack/pallas_call | solution.py:526
  2.8 7.3 %all-to-all-start = ((f32[32,8,256]{2,1,0:T(8,128)}), f32[32,8,256]{2,1,0:T(8,128)S(1)}, u32[]{:S(2)}, u32[]{:S(2)}) async-start(f32[32,8,256]{2,1,0:T(8,128)} %bitcast.1), calls=%async_computation | async-start | bytes 524288 | tf_op jit(solution)/shard_map/all_to_all | solution.py:549
  10.1 0.0 copy-start.4
  10.1 0.7 %copy-done.4 = f32[50,72]{1,0:T(8,128)S(1)} copy-done((f32[50,72]{1,0:T(8,128)S(1)}, f32[50,72]{1,0:T(8,128)}, u32[]{:S(2)}) %copy-start.4) | copy-done | bytes 14424
  10.9 1.6 %prep.1 = (f32[2,50,32,128]{3,2,1,0:T(8,128)S(1)}, f32[56,256]{1,0:T(8,128)S(1)}, f32[280,256]{1,0:T(8,128)S(1)}, f32[8,128]{1,0:T(8,128)S(1)}) custom-call(f32[50,32,256]{2,1,0:T(8,128)} %td_ref.1, f32[50,72]{1,0:T(8,128)S(1)} %copy-done.4, f32[256,256]{1,0:T(8,128)} %get-tuple-element.15.after_ref), custom_call_target="tpu_custom_call" | custom-call | flops 100000000 | bytes 4000000 | tf_op jit(solution)/shard_map/prep/pallas_call | solution.py:568
  12.5 0.0 copy-start.7
  12.5 0.0 copy-start
  12.5 0.0 copy-start.1
  12.6 0.0 copy-start.2
  12.6 0.0 copy-start.5
  12.6 0.0 copy-start.6
  12.6 7.8 %all-to-all-done = f32[32,8,256]{2,1,0:T(8,128)S(1)} async-done(((f32[32,8,256]{2,1,0:T(8,128)}), f32[32,8,256]{2,1,0:T(8,128)S(1)}, u32[]{:S(2)}, u32[]{:S(2)}) %all-to-all-start) | async-done | bytes 262176 | tf_op jit(solution)/shard_map/all_to_all | solution.py:549
  20.3 0.0 copy-done.3
  20.3 9.0 %cloud.1.refs_7_ = f32[320,128]{1,0:T(8,128)} custom-call(f32[256,256]{1,0:T(8,128)S(1)} %bitcast.5, f32[2,50,32,128]{3,2,1,0:T(8,128)S(1)} %get-tuple-element.16.start_ref, f32[56,256]{1,0:T(8,128)S(1)} %get-tuple-element.17.td_mean_ref, f32[280,256]{1,0:T(8,128)S(1)} %get-tuple-element.18.g_ref, f32[8,128]{1,0:T(8,128)S(1)} %get-tuple-element.19.most_ref, ...), custom_call_target="tpu_custom_call" | custom-call | tf_op jit(solution)/shard_map/cloud/pallas_call | solution.py:587
  29.3 2.7 %all-to-all-start.1 = ((f32[32,1,1280]{2,1,0:T(1,128)}), f32[32,1,1280]{2,1,0:T(1,128)S(1)}, u32[]{:S(2)}, u32[]{:S(2)}) async-start(f32[32,1,1280]{2,1,0:T(1,128)} %bitcast.3), calls=%async_computation.1 | async-start | bytes 327680 | tf_op jit(solution)/shard_map/all_to_all | solution.py:549
  32.0 0.0 copy-done.7
  32.0 0.1 copy.14.refs_4_
  32.1 0.0 copy-done
  32.1 0.0 copy-done.1
  32.1 0.0 copy-done.2
  32.1 0.0 copy-done.5
  32.1 0.0 copy-done.6
  32.1 1.0 %base.1 = (f32[72,256]{1,0:T(8,128)S(1)}, f32[72,256]{1,0:T(8,128)S(1)}, f32[216,128]{1,0:T(8,128)S(1)}, f32[72,128]{1,0:T(8,128)S(1)}, bf16[256,256]{1,0:T(8,128)(2,1)S(1)}, /*index=5*/bf16[64,256]{1,0:T(8,128)(2,1)S(1)}) custom-call(f32[72,256]{1,0:T(8,128)S(1)} %copy-done, f32[72,256]{1,0:T(8,128)S(1)} %copy-done.1, f32[72,256]{1,0:T(8,128)S(1)} %copy-done.2, ...), custom_call_target="tpu_custom_call" | custom-call | flops 100000000 | bytes 1000000 | tf_op jit(solution)/shard_map/base/pallas_call | solution.py:608
  33.2 7.7 %all-to-all-done.1 = f32[32,1,1280]{2,1,0:T(1,128)S(1)} async-done(((f32[32,1,1280]{2,1,0:T(1,128)}), f32[32,1,1280]{2,1,0:T(1,128)S(1)}, u32[]{:S(2)}, u32[]{:S(2)}) %all-to-all-start.1) | async-done | bytes 163872 | tf_op jit(solution)/shard_map/all_to_all | solution.py:549
  40.8 1.2 %finish.1 = (f32[72,256]{1,0:T(8,128)}, f32[72,256]{1,0:T(8,128)}, f32[72,256]{1,0:T(8,128)}) custom-call(f32[320,128]{1,0:T(8,128)S(1)} %bitcast.7, s32[1,256]{1,0:T(1,128)S(1)} %get-tuple-element.20.refs_6_.pos_ref, f32[72,256]{1,0:T(8,128)S(1)} %get-tuple-element.21.tb_ref, f32[72,256]{1,0:T(8,128)S(1)} %get-tuple-element.22.qb_ref, ...), custom_call_target="tpu_custom_call" | custom-call | tf_op jit(solution)/shard_map/finish/pallas_call | solution.py:624
Async XLA Ops:
  0.6 19.7 %copy-start.3 = (f32[248,128]{1,0:T(8,128)S(1)}, f32[248,128]{1,0:T(8,128)}, u32[]{:S(2)}) copy-start(f32[248,128]{1,0:T(8,128)} %constant.4.clone.mean_ref) | copy-start | bytes 380932
  2.8 17.6 %all-to-all-start = ((f32[32,8,256]{2,1,0:T(8,128)}), f32[32,8,256]{2,1,0:T(8,128)S(1)}, u32[]{:S(2)}, u32[]{:S(2)}) async-start(f32[32,8,256]{2,1,0:T(8,128)} %bitcast.1), calls=%async_computation | async-start | bytes 524288 | tf_op jit(solution)/shard_map/all_to_all | solution.py:549
  10.1 0.8 %copy-start.4 = (f32[50,72]{1,0:T(8,128)S(1)}, f32[50,72]{1,0:T(8,128)}, u32[]{:S(2)}) copy-start(f32[50,72]{1,0:T(8,128)} %refs_3_.1) | copy-start | bytes 43204
  12.5 19.5 %copy-start.7 = (f32[72,50]{0,1:T(8,128)S(1)}, f32[72,50]{0,1:T(8,128)}, u32[]{:S(2)}) copy-start(f32[72,50]{0,1:T(8,128)} %param.15) | copy-start | bytes 43204
  12.5 19.6 %copy-start = (f32[72,256]{1,0:T(8,128)S(1)}, f32[72,256]{1,0:T(8,128)}, u32[]{:S(2)}) copy-start(f32[72,256]{1,0:T(8,128)} %refs_0_.3) | copy-start | bytes 221188
  12.5 19.6 %copy-start.1 = (f32[72,256]{1,0:T(8,128)S(1)}, f32[72,256]{1,0:T(8,128)}, u32[]{:S(2)}) copy-start(f32[72,256]{1,0:T(8,128)} %refs_1_.3) | copy-start | bytes 221188
  12.6 19.6 %copy-start.2 = (f32[72,256]{1,0:T(8,128)S(1)}, f32[72,256]{1,0:T(8,128)}, u32[]{:S(2)}) copy-start(f32[72,256]{1,0:T(8,128)} %refs_2_.3) | copy-start | bytes 221188
  12.6 19.6 %copy-start.5 = (f32[50,72]{1,0:T(8,128)S(1)}, f32[50,72]{1,0:T(8,128)}, u32[]{:S(2)}) copy-start(f32[50,72]{1,0:T(8,128)} %refs_3_.1) | copy-start | bytes 43204
  12.6 19.6 %copy-start.6 = (f32[2,50,50]{2,1,0:T(8,128)S(1)}, f32[2,50,50]{2,1,0:T(8,128)}, u32[]{:S(2)}) copy-start(f32[2,50,50]{2,1,0:T(8,128)} %constant.5.clone.refs_5_) | copy-start | bytes 60004
  29.3 11.5 %all-to-all-start.1 = ((f32[32,1,1280]{2,1,0:T(1,128)}), f32[32,1,1280]{2,1,0:T(1,128)S(1)}, u32[]{:S(2)}, u32[]{:S(2)}) async-start(f32[32,1,1280]{2,1,0:T(1,128)} %bitcast.3), calls=%async_computation.1 | async-start | bytes 327680 | tf_op jit(solution)/shard_map/all_to_all | solution.py:549

commit v5 on v4

--- a/solution.py
+++ b/solution.py
@@ -283,8 +283,9 @@
     most_ref[...] = functools.reduce(jnp.maximum, most)
 
 
-def cloud_kernel(devices, carry, nl, r_ref, start_ref, td_mean_ref, g_ref, most_ref, mean_ref,
+def cloud_kernel(devices, carry, nl, r_ref, start_ref, td_mean_ref, g_ref, most_ref, mean_ref, after_ref,
                  out_ref, d_ref, base_ref, east_ref, west_ref, force_ref, val_ref, part_ref):
+    del after_ref
     tiles, cz, cx, _ = start_ref.shape
     zp, cols = td_mean_ref.shape
     per = cols // devices
@@ -423,10 +424,9 @@
 
 
 def base_kernel(devices, carry, *refs):
-    t_ref, q_ref, v_ref, down_ref, up_ref, lin_ref, pos_ref, after_ref, r_ref = refs[:9]
-    high_ref = None if carry else refs[9]
-    to_ref, qo_ref, level_ref, rest_ref, sel_ref, pick_ref = refs[-6:]
-    del after_ref
+    t_ref, q_ref, v_ref, down_ref, up_ref, lin_ref, pos_ref = refs[:7]
+    low_ref, high_ref = (None, None) if carry else refs[7:9]
+    to_ref, qo_ref, level_ref, rest_ref, sel_ref, pick_ref, gain_ref = refs[-7:]
     nl, cols = t_ref.shape
     cz = up_ref.shape[1]
     per = cols // devices
@@ -441,29 +441,9 @@
     sel_ref[...] = onehot(pos_ref[...], cols)
     pick_ref[...] = slot_onehot(pos_ref[...], devices, per, cols)
     if carry:
-        first, second = halves(nl)
-        me = lax.axis_index(AXES)
-
-        def ends(device, end):
-            start = pl.multiple_of(device * per, SUB)
-            block = r_ref[pl.ds(start, SUB), :]
-            block = pltpu.roll(block, block.shape[1] - 3 * nl, 1)[:, :LANE].T
-            x, t = [
-                jnp.concatenate(
-                    [
-                        block[:first, row_of(field, 0, end):row_of(field, 0, end) + 1],
-                        block[:second, row_of(field, 1, end):row_of(field, 1, end) + 1],
-                    ],
-                    axis=0,
-                )
-                for field in (0, 1)
-            ]
-            return t, x + 0.5 * t
-
-        low = ends(lax.rem(me + devices - 1, devices), 1)
-        high = ends(lax.rem(me + 1, devices), 0)
+        low = high = (jnp.zeros((nl, 1), jnp.float32),) * 2
     else:
-        low = (r_ref[0], r_ref[1])
+        low = (low_ref[0], low_ref[1])
         high = (high_ref[0], high_ref[1])
     v = v_ref[...]
     t = t_ref[...]
@@ -476,13 +456,70 @@
     gain = dot(up, gain, 1, 0, HI)
     to_ref[...] = t + advt + gain[:, :cols]
     qo_ref[...] = q + advq + gain[:, cols:]
-
-
-def finish_kernel(devices, r_ref, pos_ref, tb_ref, qb_ref, level_ref, rest_ref, sel_ref, pick_ref,
-                  to_ref, qo_ref, co_ref):
+    gain_ref[...] = dot(up, dot(lin[1], down_ref[...], 1, 0, HI), 1, 0, HI)
+
+
+def ends_pick():
+    pick = np.zeros((2 * SUB, 2 * LANE))
+    for r, (field, half, end) in enumerate(CARRIED):
+        row = r + (0 if end else SUB)
+        place = half * LANE + (0 if end else 1)
+        if field:
+            pick[row, place] = 1.0
+        pick[row, place + 2] = 0.5 if field else 1.0
+    return pick
+
+
+def halo_part(devices, r_ref, ends_ref, v_ref):
+    nl, cols = v_ref.shape
+    per = cols // devices
+    first, second = halves(nl)
+    me = lax.axis_index(AXES)
+
+    def block(device):
+        start = pl.multiple_of(device * per, SUB)
+        return r_ref[pl.ds(start, SUB), :]
+
+    rows = jnp.concatenate(
+        [block(lax.rem(me + devices - 1, devices)), block(lax.rem(me + 1, devices))], axis=0
+    )
+    rows = pltpu.roll(rows, rows.shape[1] - 3 * nl, 1)[:, :LANE]
+    a, b = split(rows)
+    pick = ends_ref[...]
+    part = dot(a, pick, 0, 0) + dot(b, pick, 0, 0)
+    ends = jnp.concatenate([part[:first, :LANE], part[:second, LANE:]], axis=0)
+    lane = lax.broadcasted_iota(jnp.int32, ends.shape, 1)
+    low = v_ref[:, :LANE]
+    high = v_ref[:, cols - LANE:]
+    v = jnp.where(
+        lane == 0, low, jnp.where(lane == 2, pltpu.roll(low, 2, 1), jnp.where(
+            lane == 1, -pltpu.roll(high, 2, 1), -pltpu.roll(high, 4, 1)))
+    )
+    return (loop_diff + 0.5 * v) * ends
+
+
+def add_ends(field_ref, out_ref, extra, halo, place):
+    cols = field_ref.shape[1]
+    lane = lax.broadcasted_iota(jnp.int32, halo.shape, 1)
+    start = pltpu.roll(halo, LANE - place, 1) if place else halo
+    stop = pltpu.roll(halo, LANE - 2 - place, 1)
+    parts = [extra[:, k:k + LANE] for k in range(0, cols, LANE)]
+    parts[0] = parts[0] + jnp.where(lane == 0, start, 0.0)
+    parts[-1] = parts[-1] + jnp.where(lane == LANE - 1, stop, 0.0)
+    for k, part in enumerate(parts):
+        out_ref[:, lanes(k)] = field_ref[:, lanes(k)] + part
+
+
+def finish_kernel(devices, carry, *refs):
+    r_ref, pos_ref, tb_ref, qb_ref, level_ref, rest_ref, sel_ref, pick_ref = refs[:8]
+    gain_ref, r1_ref, v_ref, ends_ref = refs[8:12] if carry else (None,) * 4
+    to_ref, qo_ref, co_ref = refs[-3:]
     nl, cols = tb_ref.shape
     per = cols // devices
     rows = r_ref.shape[0] // devices
+    if carry:
+        halo = halo_part(devices, r1_ref, ends_ref, v_ref)
+        halo = halo + dot(gain_ref[...], halo, 1, 0, HI)
     main = jnp.concatenate([r_ref[pl.ds(h * rows, per), :] for h in range(devices)], axis=0)
     extra = jnp.concatenate(
         [r_ref[pl.ds(per + i, devices, stride=rows), :] for i in range(rows - per)], axis=0
@@ -496,8 +533,12 @@
     rest = dot(rest_ref[:, 0:SLOT], left, 1, 0, HI)
     a, b = split(dot(level_ref[...], main, 1, 1, HI))
     out = dot(a, sel_ref[...], 1, 0) + dot(b, sel_ref[...], 1, 0)
-    to_ref[...] = tb_ref[...] + out[0:nl]
-    qo_ref[...] = qb_ref[...] + out[nl:2 * nl]
+    if carry:
+        add_ends(tb_ref, to_ref, out[0:nl], halo, 0)
+        add_ends(qb_ref, qo_ref, out[nl:2 * nl], halo, 2)
+    else:
+        to_ref[...] = tb_ref[...] + out[0:nl]
+        qo_ref[...] = qb_ref[...] + out[nl:2 * nl]
     co_ref[...] = out[2 * nl:3 * nl] + rest
 
 
@@ -573,7 +614,7 @@
             jax.ShapeDtypeStruct((level_rows, width), f32),
             jax.ShapeDtypeStruct((SUB, LANE), f32),
         ),
-        in_specs=[HBM, VMEM, HBM],
+        in_specs=[HBM, VMEM, VMEM],
         out_specs=(VMEM,) * 4,
         scratch_shapes=[
             pltpu.VMEM((tiles, cz, cx, LANE), f32),
@@ -583,11 +624,29 @@
         compiler_params=pltpu.CompilerParams(vmem_limit_bytes=VMEM_PACK),
         cost_estimate=pl.CostEstimate(flops=10**8, bytes_accessed=4 * 10**6, transcendentals=0),
         name="prep",
-    )(in_hbm(thermal_disturbance), layer_index_downscale, in_hbm(out))
+    )(in_hbm(thermal_disturbance), layer_index_downscale, pos)
+    lin = np.stack([power - np.eye(cz), total])
+    *base, gain = pl.pallas_call(
+        functools.partial(base_kernel, devices, carry),
+        out_shape=(
+            field,
+            field,
+            jax.ShapeDtypeStruct((3 * nl, LANE), f32),
+            jax.ShapeDtypeStruct((nl, LANE), f32),
+            jax.ShapeDtypeStruct((cols, cols), jnp.bfloat16),
+            jax.ShapeDtypeStruct((devices * (rows - per), cols), jnp.bfloat16),
+            jax.ShapeDtypeStruct((nl, nl), f32),
+        ),
+        in_specs=[VMEM] * (7 + len(ends)),
+        out_specs=(VMEM,) * 7,
+        compiler_params=pltpu.CompilerParams(vmem_limit_bytes=VMEM_PACK),
+        cost_estimate=pl.CostEstimate(flops=10**8, bytes_accessed=10**6, transcendentals=0),
+        name="base",
+    )(*fields, layer_index_downscale, layer_index_upscale, jnp.asarray(lin, f32), pos, *ends)
     vals = pl.pallas_call(
         functools.partial(cloud_kernel, devices, carry, nl),
         out_shape=jax.ShapeDtypeStruct((devices * rows, LANE), f32),
-        in_specs=[VMEM] * 6,
+        in_specs=[VMEM] * 7,
         out_specs=VMEM,
         scratch_shapes=[
             pltpu.VMEM((tiles, cz, SUB * (groups + 2), LANE), f32),
@@ -600,35 +659,19 @@
         ],
         compiler_params=pltpu.CompilerParams(vmem_limit_bytes=VMEM_CLOUD),
         name="cloud",
-    )(r1, *prep, jnp.asarray(mean, f32))
+    )(r1, *prep, jnp.asarray(mean, f32), gain)
     r2 = exchange(vals, 1, rows * LANE)
-
-    lin = np.stack([power - np.eye(cz), total])
-    halo = (r1,) if carry else ends
-    base = pl.pallas_call(
-        functools.partial(base_kernel, devices, carry),
-        out_shape=(
-            field,
-            field,
-            jax.ShapeDtypeStruct((3 * nl, LANE), f32),
-            jax.ShapeDtypeStruct((nl, LANE), f32),
-            jax.ShapeDtypeStruct((cols, cols), jnp.bfloat16),
-            jax.ShapeDtypeStruct((devices * (rows - per), cols), jnp.bfloat16),
-        ),
-        in_specs=[VMEM] * 7 + [HBM] + [VMEM] * len(halo),
-        out_specs=(VMEM,) * 6,
-        compiler_params=pltpu.CompilerParams(vmem_limit_bytes=VMEM_PACK),
-        cost_estimate=pl.CostEstimate(flops=10**8, bytes_accessed=10**6, transcendentals=0),
-        name="base",
-    )(*fields, layer_index_downscale, layer_index_upscale, jnp.asarray(lin, f32), pos, in_hbm(vals), *halo)
+    halo = ()
+    if carry:
+        halo = (gain, r1, periodic_flow_velocity, jnp.asarray(ends_pick(), jnp.bfloat16))
     return pl.pallas_call(
-        functools.partial(finish_kernel, devices),
+        functools.partial(finish_kernel, devices, carry),
         out_shape=(field,) * 3,
-        in_specs=[VMEM] * 8,
+        in_specs=[VMEM] * (8 + len(halo)),
         out_specs=(VMEM,) * 3,
         compiler_params=pltpu.CompilerParams(vmem_limit_bytes=VMEM_PACK),
         name="finish",
-    )(r2, pos, *base)
+    )(r2, pos, *base, *halo)
 
 
 VMEM_PACK = 16 * 2**20

time: 42.4 us -> 42 us (level)
  blocking collectives: 0 us -> 11.3 us
  waiting for transfers between devices: 15.4 us -> 6.03 us
  starting transfers between devices: 9.99 us -> 7.33 us
  local copies, waits for them, and re-layouts: 0.88 us -> 1.62 us
  Pallas kernels: 15 us -> 14.5 us
    all_to_all x0 -> x1, blocking collectives: none -> 11.3 us  [exchange(): lax.all_to_all(blocks, AXES, split_axis=0, concat_axis=0, tiled=True)]
    all_to_all x2 -> x1, waiting for transfers between devices: 15.4 us -> 6.03 us  [exchange(): lax.all_to_all(blocks, AXES, split_axis=0, concat_axis=0, tiled=True)]
    all_to_all x2 -> x1, starting transfers between devices: 9.99 us -> 7.33 us  [exchange(): lax.all_to_all(blocks, AXES, split_axis=0, concat_axis=0, tiled=True)]
    unnamed x17, local copies, waits for them, and re-layouts: 0.88 us -> 1.62 us
    pallas_call x1, Pallas kernels: 8.99 us -> 8.32 us  [local(): pl.pallas_call(functools.partial(cloud_kernel, devices, carry, nl), out_s...]
  transfers between devices with their start and end apart: 2 -> 1, of which waited for: 2 -> 1; matrix products, arithmetic and copies ran while one was open for 0% -> 2% of each run, Pallas kernels for 6% -> 6%
where the time goes in v5:
time: 42 us; the launch traced here: 41.6 us
  Pallas kernels  14.5 us (35%)
  blocking collectives  11.3 us (27%)
  starting transfers between devices  7.33 us (17%)
  waiting for transfers between devices  6.03 us (14%)
  local copies, waits for them, and re-layouts  1.62 us (4%)
  between operations  0.77 us (2%)
    all_to_all x1, blocking collectives, exchange(): lax.all_to_all(blocks, AXES, split_axis=0, concat_axis=0, tiled=True)  11.3 us
    pallas_call x1, Pallas kernels, local(): pl.pallas_call(functools.partial(cloud_kernel, devices, carry, nl), out_s...  8.32 us
    all_to_all x1, starting transfers between devices, exchange(): lax.all_to_all(blocks, AXES, split_axis=0, concat_axis=0, tiled=True)  7.33 us
    all_to_all x1, waiting for transfers between devices, exchange(): lax.all_to_all(blocks, AXES, split_axis=0, concat_axis=0, tiled=True)  6.03 us
    pallas_call x1, Pallas kernels, local(): pl.pallas_call(functools.partial(pack_kernel, devices, carry), out_shape=...  2.18 us
    pallas_call x1, Pallas kernels, local(): pl.pallas_call(functools.partial(prep_kernel, carry), out_shape=(jax.Shap...  1.64 us
    unnamed x17, local copies, waits for them, and re-layouts  1.62 us
    pallas_call x1, Pallas kernels, local(): pl.pallas_call(functools.partial(finish_kernel, devices, carry), out_shap...  1.52 us
  transfers between devices with their start and end apart: 1, of which 1 were waited for; matrix products, arithmetic and copies ran while one was open for 2% of the time, Pallas kernels for 6%

profile of v5, /device:TPU:0, one launch (start us, length us, event | category | flops | bytes accessed | tf_op | source)
XLA Modules:
  0.0 41.6 jit_solution(3699317408502165443)
XLA Ops:
  0.6 0.0 copy-start.7
  0.6 0.0 copy-start.1
  0.7 0.0 copy-start
  0.7 0.0 copy-start.3
  0.7 0.0 copy-start.2
  0.7 0.0 copy-start.5
  0.7 2.2 %pack.1 = (f32[256,256]{1,0:T(8,128)}, s32[1,256]{1,0:T(1,128)S(1)}) custom-call(f32[72,256]{1,0:T(8,128)} %refs_0_.3, f32[72,256]{1,0:T(8,128)} %refs_1_.3, f32[72,256]{1,0:T(8,128)} %refs_10_.1, s32[1,256]{1,0:T(1,128)} %bitcast.9), custom_call_target="tpu_custom_call" | custom-call | tf_op jit(solution)/shard_map/pack/pallas_call | solution.py:567
  2.9 7.3 %all-to-all-start = ((f32[32,8,256]{2,1,0:T(8,128)}), f32[32,8,256]{2,1,0:T(8,128)S(1)}, u32[]{:S(2)}, u32[]{:S(2)}) async-start(f32[32,8,256]{2,1,0:T(8,128)} %bitcast.1), calls=%async_computation | async-start | bytes 524288 | tf_op jit(solution)/shard_map/all_to_all | solution.py:590
  10.2 0.8 %copy.14.refs_4_ = f32[72,50]{1,0:T(8,128)S(1)} copy(f32[72,50]{0,1:T(8,128)} %param.16) | data formatting | bytes 28800 | tf_op args[6]
  11.1 0.0 copy-start.4
  11.1 0.7 %copy-done.4 = f32[50,72]{1,0:T(8,128)S(1)} copy-done((f32[50,72]{1,0:T(8,128)S(1)}, f32[50,72]{1,0:T(8,128)}, u32[]{:S(2)}) %copy-start.4) | copy-done | bytes 14424
  11.8 1.6 %prep.1 = (f32[2,50,32,128]{3,2,1,0:T(8,128)S(1)}, f32[56,256]{1,0:T(8,128)S(1)}, f32[280,256]{1,0:T(8,128)S(1)}, f32[8,128]{1,0:T(8,128)S(1)}) custom-call(f32[50,32,256]{2,1,0:T(8,128)} %td_ref.1, f32[50,72]{1,0:T(8,128)S(1)} %copy-done.4, s32[1,256]{1,0:T(1,128)S(1)} %get-tuple-element.17.after_ref.refs_6_.refs_1_), custom_call_target="tpu_custom_call" | custom-call | flops 100000000 | bytes 4000000 | tf_op jit(solution)/shard_map/prep/pallas_call | solution.py:609
  13.5 0.0 copy-done.7
  13.5 0.0 copy-done
  13.5 0.0 copy-done.3
  13.5 0.0 copy-done.2
  13.5 0.0 copy-done.5
  13.5 0.0 copy-start.6
  13.5 0.9 %base.1 = (f32[72,256]{1,0:T(8,128)S(1)}, f32[72,256]{1,0:T(8,128)S(1)}, f32[216,128]{1,0:T(8,128)S(1)}, f32[72,128]{1,0:T(8,128)S(1)}, bf16[256,256]{1,0:T(8,12...) custom-call(f32[72,256]{1,0:T(8,128)S(1)} %copy-done.2, f32[72,256]{1,0:T(8,128)S(1)} %copy-done.3, ...), custom_call_target="tpu_custom_call" | custom-call | flops 100000000 | bytes 1000000 | tf_op jit(solution)/shard_map/base/pallas_call | solution.py:629
  14.4 6.0 %all-to-all-done = f32[32,8,256]{2,1,0:T(8,128)S(1)} async-done(((f32[32,8,256]{2,1,0:T(8,128)}), f32[32,8,256]{2,1,0:T(8,128)S(1)}, u32[]{:S(2)}, u32[]{:S(2)}) %all-to-all-start) | async-done | bytes 262176 | tf_op jit(solution)/shard_map/all_to_all | solution.py:590
  20.4 0.0 copy-done.1
  20.5 8.3 %cloud.1 = f32[320,128]{1,0:T(8,128)S(1)} custom-call(f32[256,256]{1,0:T(8,128)S(1)} %bitcast.5, f32[2,50,32,128]{3,2,1,0:T(8,128)S(1)} %get-tuple-element.18.start_ref, f32[56,256]{1,0:T(8,128)S(1)} %get-tuple-element.19.td_mean_ref, f32[280,256]{1,0:T(8,128)S(1)} %get-tuple-element.20.g_ref, f32[8,128]{1,0:T(8,128)S(1)} %get-tuple-element.21.most_ref, ...), custom_call_target="tpu_custom_call" | custom-call | tf_op jit(solution)/shard_map/cloud/pallas_call | solution.py:646
  28.8 11.3 %all_to_all.10 = f32[32,1,1280]{2,1,0:T(1,128)S(1)} all-to-all(f32[32,1,1280]{2,1,0:T(1,128)S(1)} %bitcast.7), channel_id=1, replica_groups=mesh['tile'=8,'crm'=4] {'tile','crm'}, dimensions={0} | all-to-all | bytes 327680 | tf_op jit(solution)/shard_map/all_to_all | solution.py:590
  40.1 0.0 copy-done.6
  40.1 1.5 %finish.1 = (f32[72,256]{1,0:T(8,128)}, f32[72,256]{1,0:T(8,128)}, f32[72,256]{1,0:T(8,128)}) custom-call(f32[320,128]{1,0:T(8,128)S(1)} %bitcast.8, s32[1,256]{1,0:T(1,128)S(1)} %get-tuple-element.17.after_ref.refs_6_.refs_1_, f32[72,256]{1,0:T(8,128)S(1)} %get-tuple-element.23.refs_2_, f32[72,256]{1,0:T(8,128)S(1)} %get-tuple-element.24.refs_3_, ...), custom_call_target="tpu_custom_call" | custom-call | tf_op jit(solution)/shard_map/finish/pallas_call | solution.py:667
Async XLA Ops:
  0.6 12.8 %copy-start.7 = (f32[2,50,50]{2,1,0:T(8,128)S(1)}, f32[2,50,50]{2,1,0:T(8,128)}, u32[]{:S(2)}) copy-start(f32[2,50,50]{2,1,0:T(8,128)} %constant.6.clone.refs_5_) | copy-start | bytes 60004
  0.6 19.8 %copy-start.1 = (f32[248,128]{1,0:T(8,128)S(1)}, f32[248,128]{1,0:T(8,128)}, u32[]{:S(2)}) copy-start(f32[248,128]{1,0:T(8,128)} %constant.7.clone.mean_ref) | copy-start | bytes 380932
  0.7 12.8 %copy-start = (f32[72,256]{1,0:T(8,128)S(1)}, f32[72,256]{1,0:T(8,128)}, u32[]{:S(2)}) copy-start(f32[72,256]{1,0:T(8,128)} %refs_10_.1) | copy-start | bytes 221188
  0.7 12.8 %copy-start.3 = (f32[72,256]{1,0:T(8,128)S(1)}, f32[72,256]{1,0:T(8,128)}, u32[]{:S(2)}) copy-start(f32[72,256]{1,0:T(8,128)} %refs_1_.3) | copy-start | bytes 221188
  0.7 12.8 %copy-start.2 = (f32[72,256]{1,0:T(8,128)S(1)}, f32[72,256]{1,0:T(8,128)}, u32[]{:S(2)}) copy-start(f32[72,256]{1,0:T(8,128)} %refs_0_.3) | copy-start | bytes 221188
  0.7 12.8 %copy-start.5 = (f32[50,72]{1,0:T(8,128)S(1)}, f32[50,72]{1,0:T(8,128)}, u32[]{:S(2)}) copy-start(f32[50,72]{1,0:T(8,128)} %refs_3_.1) | copy-start | bytes 43204
  2.9 17.6 %all-to-all-start = ((f32[32,8,256]{2,1,0:T(8,128)}), f32[32,8,256]{2,1,0:T(8,128)S(1)}, u32[]{:S(2)}, u32[]{:S(2)}) async-start(f32[32,8,256]{2,1,0:T(8,128)} %bitcast.1), calls=%async_computation | async-start | bytes 524288 | tf_op jit(solution)/shard_map/all_to_all | solution.py:590
  11.1 0.8 %copy-start.4 = (f32[50,72]{1,0:T(8,128)S(1)}, f32[50,72]{1,0:T(8,128)}, u32[]{:S(2)}) copy-start(f32[50,72]{1,0:T(8,128)} %refs_3_.1) | copy-start | bytes 43204
  13.5 26.6 %copy-start.6 = (bf16[16,256]{1,0:T(8,128)(2,1)S(1)}, bf16[16,256]{1,0:T(8,128)(2,1)}, u32[]{:S(2)}) copy-start(bf16[16,256]{1,0:T(8,128)(2,1)} %constant.8.clone.refs_11_) | copy-start | bytes 24580

commit v6 on v5

--- a/solution.py
+++ b/solution.py
@@ -67,9 +67,26 @@
     return power, total / SUBSTEPS
 
 
+def shift_operators(levels):
+    drain = cond_rate * (1.0 + 0.5 * latent_heat)
+    rest = (1.0 + drain) * np.eye(levels) - ring_mean_operator(levels)
+    scale = LOG2E / SUBSTEPS
+    return -np.linalg.inv(rest) * scale, -rest / scale
+
+
+def halved(x):
+    a = np.asarray(x, jnp.bfloat16)
+    b = np.asarray(x - a.astype(np.float64), jnp.bfloat16)
+    return jnp.asarray(a), jnp.asarray(b)
+
+
 def split(x):
     a = x.astype(jnp.bfloat16)
     return a, (x - a.astype(jnp.float32)).astype(jnp.bfloat16)
+
+
+def dot3(a, b, ca, cb):
+    return dot(a[0], b[0], ca, cb) + dot(a[0], b[1], ca, cb) + dot(a[1], b[0], ca, cb)
 
 
 def dot(a, b, ca, cb, precision=None):
@@ -204,8 +221,10 @@
 LARGEST = 120.0
 
 
-def small_softplus2(f):
-    return jnp.log2(1.0 + jnp.exp2(f))
+def moved_softplus2(small, g, move):
+    if small:
+        return jnp.log2(move + jnp.exp2(g))
+    return move + softplus2(g - move)
 
 
 def softplus2(f):
@@ -230,13 +249,13 @@
             part_ref[n, pl.ds(z, SUB), :] = jnp.zeros((SUB, LANE), jnp.float32)
 
 
-def prep_kernel(carry, td_ref, down_ref, after_ref, start_ref, mean_ref, g_ref, most_ref,
-                raw_ref, part_ref, td_sem):
+def prep_kernel(carry, td_ref, down_ref, shift_ref, after_ref, start_ref, mean_ref, most_ref,
+                high_ref, low_ref, shift_high_ref, shift_low_ref, raw_ref, part_ref, td_sem):
     del after_ref
     cz, cx, cols = td_ref.shape
     nl = down_ref.shape[1]
     zp = mean_ref.shape[0]
-    width = g_ref.shape[1]
+    width = high_ref.shape[1]
     groups = cx // SUB
     tiles = cols // LANE
     chunk = -(-cz // td_sem.shape[1])
@@ -251,19 +270,28 @@
         for c in range(td_sem.shape[1]):
             td_copy(k, c).start()
 
-    down = jnp.concatenate(
-        [down_ref[...], jnp.zeros((cz, width - nl), jnp.float32)], axis=1
-    )
-    down = jnp.concatenate([down, jnp.zeros((zp - cz, width), jnp.float32)], axis=0)
-    for n in range(3):
-        g_ref[n * zp:(n + 1) * zp, :] = down if n == 0 else pltpu.roll(down, n * nl, 1)
+    def wide(rows):
+        rows = jnp.concatenate(
+            [rows, jnp.zeros((rows.shape[0], width - nl), jnp.float32)], axis=1
+        )
+        return jnp.concatenate([rows, jnp.zeros((zp - cz, width), jnp.float32)], axis=0)
+
+    down = wide(down_ref[...])
+    shift = wide(dot(shift_ref[...], down_ref[...], 1, 0, lax.Precision.HIGHEST))
+    blocks = jnp.concatenate(
+        [down, pltpu.roll(down, nl, 1), pltpu.roll(shift, 2 * nl, 1)], axis=0
+    )
+    a, low_ref[...] = split(blocks)
+    offset = high_ref.shape[0] - 3 * zp
     if carry:
-        shape = (g_ref.shape[0] - 3 * zp, width)
+        shape = (offset, width)
         row = lax.broadcasted_iota(jnp.int32, shape, 0)
         to = jnp.where(row < nl, row + nl, row + 2 * nl)
-        g_ref[3 * zp:, :] = jnp.where(
+        high_ref[0:offset, :] = jnp.where(
             lax.broadcasted_iota(jnp.int32, shape, 1) == to, 1.0, 0.0
-        )
+        ).astype(jnp.bfloat16)
+    high_ref[offset:, :] = a
+    shift_high_ref[...], shift_low_ref[...] = split(shift[:, :nl])
 
     clear_tail(part_ref, cz)
     most = [jnp.zeros((SUB, LANE), jnp.float32)] * groups
@@ -283,22 +311,25 @@
     most_ref[...] = functools.reduce(jnp.maximum, most)
 
 
-def cloud_kernel(devices, carry, nl, r_ref, start_ref, td_mean_ref, g_ref, most_ref, mean_ref, after_ref,
-                 out_ref, d_ref, base_ref, east_ref, west_ref, force_ref, val_ref, part_ref):
-    del after_ref
+def cloud_kernel(devices, carry, nl, r_ref, start_ref, td_mean_ref, most_ref, g_high_ref, g_low_ref,
+                 shift_high_ref, shift_low_ref, mean_high_ref, mean_low_ref, after_ref, *refs):
+    gain_ref, v_ref, ends_ref = (after_ref, *refs[:2]) if carry else (None,) * 3
+    out_ref, halo_ref = refs[2:4] if carry else (refs[0], None)
+    d_ref, base_ref, east_ref, west_ref, shift_ref, scale_ref, val_ref, part_ref = refs[-8:]
     tiles, cz, cx, _ = start_ref.shape
     zp, cols = td_mean_ref.shape
     per = cols // devices
     groups = cx // SUB
 
-    prof = dot(g_ref[...], r_ref[...], 1, 1, HI)
-    d0 = prof[0:zp]
-    speed = max_speed * jnp.tanh(prof[zp:2 * zp])
-    fd = prof[2 * zp:3 * zp]
+    r = split(r_ref[...])
+    offset = g_high_ref.shape[0] - 3 * zp
+    prof = dot(g_high_ref[...], r[0], 1, 1) + dot(g_high_ref[...], r[1], 1, 1)
+    fine = dot(g_low_ref[...], r[0], 1, 1)
+    shift = prof[offset + 2 * zp:] + fine[2 * zp:]
     if carry:
         first, second = halves(nl)
-        v = prof[3 * zp:3 * zp + nl]
-        ends = prof[3 * zp + nl:3 * zp + nl + first]
+        v = prof[0:nl]
+        ends = prof[nl:offset]
         flag = ends[second:second + 1] > 0.5
         place = lax.rem(lax.broadcasted_iota(jnp.int32, (1, cols), 1), per)
 
@@ -314,22 +345,25 @@
         halo = jnp.where(flag & (place == 0), behind, 0.0) + jnp.where(
             flag & (place == per - 1), ahead, 0.0
         )
-        fd = fd + dot(g_ref[0:zp, 0:nl], halo, 1, 0, HI)
-    base_ref[...] = d0 * LOG2E
+        shift = shift + dot3((shift_high_ref[...], shift_low_ref[...]), split(halo), 1, 0)
+    d0 = prof[offset:offset + zp] + fine[0:zp]
+    speed = max_speed * jnp.tanh(prof[offset + zp:offset + 2 * zp] + fine[zp:2 * zp])
+    base = d0 * LOG2E + shift
+    base_ref[...] = base
     east_ref[...] = mix_along - 0.5 * speed
     west_ref[...] = mix_along + 0.5 * speed
-    force = fd * (LOG2E / SUBSTEPS)
-    force_ref[...] = force
+    shift_ref[...] = shift
+    scale_ref[...] = jnp.exp2(shift)
     drain = cond_rate * (1.0 + 0.5 * latent_heat)
     rate = 1.0 - 2.0 * mix_along + max(2.0 * mix_along, max_speed)
     growth = rate**SUBSTEPS
     series = sum(rate**n for n in range(SUBSTEPS))
-    bound = growth * (jnp.max(jnp.abs(d0)) * LOG2E + jnp.max(most_ref[...])) + series * (
-        jnp.max(jnp.abs(force)) + drain
+    bound = growth * (jnp.max(jnp.abs(base)) + jnp.max(most_ref[...])) + series * drain * (
+        jnp.max(jnp.abs(shift)) + 1.0
     )
     val_ref[0:zp, :] = td_mean_ref[...]
     val_ref[zp:2 * zp, :] = d0 - 0.5 * td_mean_ref[...]
-    val_ref[2 * zp:3 * zp, :] = fd
+    val_ref[2 * zp:3 * zp, :] = shift
     clear_tail(part_ref, cz)
 
     def row_at(ref, z, k):
@@ -354,7 +388,7 @@
             for i in range(groups):
                 put(k, z, i, base + start_ref[k, z, pl.ds(SUB * i, SUB), :])
 
-    def step(softplus, _, carry):
+    def step(small, _, carry):
         for k in range(tiles):
             below = cur = get(k, 0)
             pair = None
@@ -368,7 +402,7 @@
                     pair = None
                 ea = row_at(east_ref, z, k)
                 we = row_at(west_ref, z, k)
-                fo = row_at(force_ref, z, k)
+                move = row_at(scale_ref if small else shift_ref, z, k)
                 ring = [d_ref[k, z, pl.ds(last + SUB - 1, SUB), :]] + cur
                 ring = ring + [d_ref[k, z, pl.ds(1, SUB), :]]
                 for i in range(groups):
@@ -376,8 +410,7 @@
                         mix_vertical * column[i]
                         + ea * ring[i + 2]
                         + we * ring[i]
-                        + fo
-                        - drain * softplus(cur[i])
+                        - drain * moved_softplus2(small, cur[i], move)
                     )
                     put(k, z, i, new)
                 below, cur = cur, above
@@ -385,18 +418,24 @@
 
     @pl.when(bound < LARGEST)
     def _():
-        lax.fori_loop(0, SUBSTEPS, functools.partial(step, small_softplus2), 0)
+        lax.fori_loop(0, SUBSTEPS, functools.partial(step, True), 0)
 
     @pl.when(jnp.logical_not(bound < LARGEST))
     def _():
-        lax.fori_loop(0, SUBSTEPS, functools.partial(step, softplus2), 0)
+        lax.fori_loop(0, SUBSTEPS, functools.partial(step, False), 0)
+
+    if carry:
+        halo = halo_part(devices, r_ref, ends_ref, v_ref)
+        halo_ref[...] = halo + dot(gain_ref[...], halo, 1, 0, HI)
 
     head, rows = return_shape(cz, per)
     cloud_ref = east_ref
     for k in range(tiles):
         for z in range(cz):
             total = cloud = None
+            move = row_at(shift_ref, z, k)
             for f in get(k, z):
+                f = f - move
                 c = softplus2(f)
                 total = f if total is None else total + f
                 cloud = c if cloud is None else cloud + c
@@ -405,7 +444,7 @@
         fold(part_ref.at[2 * k], val_ref.at[pl.ds(3 * zp, zp)], k, LN2 / cx)
         fold(part_ref.at[2 * k + 1], cloud_ref, k, LN2 / cx)
         val_ref[4 * zp:, lanes(k)] = cloud_ref[0:head, lanes(k)]
-        main = dot(val_ref[:, lanes(k)], mean_ref[...], 0, 0, HI)
+        main = dot3(split(val_ref[:, lanes(k)]), (mean_high_ref[...], mean_low_ref[...]), 0, 0)
         for h in range(LANE // per):
             out_ref[pl.ds((k * (LANE // per) + h) * rows, per), :] = main[h * per:(h + 1) * per]
     left = cloud_ref[head:, :]
@@ -426,7 +465,8 @@
 def base_kernel(devices, carry, *refs):
     t_ref, q_ref, v_ref, down_ref, up_ref, lin_ref, pos_ref = refs[:7]
     low_ref, high_ref = (None, None) if carry else refs[7:9]
-    to_ref, qo_ref, level_ref, rest_ref, sel_ref, pick_ref, gain_ref = refs[-7:]
+    to_ref, qo_ref, level_high_ref, level_low_ref, rest_high_ref, rest_low_ref = refs[-9:-3]
+    sel_ref, pick_ref, gain_ref = refs[-3:]
     nl, cols = t_ref.shape
     cz = up_ref.shape[1]
     per = cols // devices
@@ -434,10 +474,17 @@
     up = up_ref[...]
     wide = jnp.concatenate([up, jnp.zeros((nl, LANE - cz), jnp.float32)], axis=1)
     lane = lax.broadcasted_iota(jnp.int32, wide.shape, 1)
-    level_ref[0:nl, :] = wide
-    level_ref[nl:2 * nl, :] = -pltpu.roll(wide, cz, 1)
-    level_ref[2 * nl:3 * nl, :] = pltpu.roll(jnp.where(lane < head, wide, 0.0), 2 * cz, 1)
-    rest_ref[...] = jnp.where(lane < SLOT, pltpu.roll(wide, LANE - head, 1), 0.0)
+    level = jnp.concatenate(
+        [
+            wide,
+            -pltpu.roll(wide, cz, 1),
+            pltpu.roll(jnp.where(lane < head, wide, 0.0), 2 * cz, 1),
+        ],
+        axis=0,
+    )
+    level_high_ref[...], level_low_ref[...] = split(level)
+    rest = jnp.where(lane < SLOT, pltpu.roll(wide, LANE - head, 1), 0.0)
+    rest_high_ref[...], rest_low_ref[...] = split(rest[:, 0:SLOT])
     sel_ref[...] = onehot(pos_ref[...], cols)
     pick_ref[...] = slot_onehot(pos_ref[...], devices, per, cols)
     if carry:
@@ -511,15 +558,12 @@
 
 
 def finish_kernel(devices, carry, *refs):
-    r_ref, pos_ref, tb_ref, qb_ref, level_ref, rest_ref, sel_ref, pick_ref = refs[:8]
-    gain_ref, r1_ref, v_ref, ends_ref = refs[8:12] if carry else (None,) * 4
+    r_ref, pos_ref, tb_ref, qb_ref = refs[:4]
+    level_high_ref, level_low_ref, rest_high_ref, rest_low_ref, sel_ref, pick_ref = refs[4:10]
     to_ref, qo_ref, co_ref = refs[-3:]
     nl, cols = tb_ref.shape
     per = cols // devices
     rows = r_ref.shape[0] // devices
-    if carry:
-        halo = halo_part(devices, r1_ref, ends_ref, v_ref)
-        halo = halo + dot(gain_ref[...], halo, 1, 0, HI)
     main = jnp.concatenate([r_ref[pl.ds(h * rows, per), :] for h in range(devices)], axis=0)
     extra = jnp.concatenate(
         [r_ref[pl.ds(per + i, devices, stride=rows), :] for i in range(rows - per)], axis=0
@@ -530,10 +574,11 @@
     left = jnp.where(part == 0, extra[:SLOT], 0.0)
     for j in range(1, SLOTS):
         left = left + jnp.where(part == j, extra[j * SLOT:(j + 1) * SLOT], 0.0)
-    rest = dot(rest_ref[:, 0:SLOT], left, 1, 0, HI)
-    a, b = split(dot(level_ref[...], main, 1, 1, HI))
+    rest = dot3((rest_high_ref[...], rest_low_ref[...]), split(left), 1, 0)
+    a, b = split(dot3((level_high_ref[...], level_low_ref[...]), split(main), 1, 1))
     out = dot(a, sel_ref[...], 1, 0) + dot(b, sel_ref[...], 1, 0)
     if carry:
+        halo = refs[10][...]
         add_ends(tb_ref, to_ref, out[0:nl], halo, 0)
         add_ends(qb_ref, qo_ref, out[nl:2 * nl], halo, 2)
     else:
@@ -593,10 +638,11 @@
 
     power, total = mean_operators(cz)
     release = 1.0 + 0.5 * latent_heat
+    shift, unshift = shift_operators(cz)
     mean = np.zeros((4 * zp + head, LANE))
     z_part = np.zeros((4 * zp + head, cz))
     z_part[zp:zp + cz] = power.T / release
-    z_part[2 * zp:2 * zp + cz] = total.T / release
+    z_part[2 * zp:2 * zp + cz] = (total @ unshift).T / release
     z_part[3 * zp:3 * zp + cz] = -np.eye(cz) / release
     mean[0:cz, 0:cz] = power.T
     mean[:, 0:cz] += latent_heat * z_part
@@ -606,16 +652,20 @@
     tiles = cols // LANE
     groups = cx // SUB
     level_rows = 3 * zp + (nl + halves(nl)[0] if carry else 0)
+    bf16 = jnp.bfloat16
     prep = pl.pallas_call(
         functools.partial(prep_kernel, carry),
         out_shape=(
             jax.ShapeDtypeStruct((tiles, cz, cx, LANE), f32),
             jax.ShapeDtypeStruct((zp, cols), f32),
-            jax.ShapeDtypeStruct((level_rows, width), f32),
             jax.ShapeDtypeStruct((SUB, LANE), f32),
+            jax.ShapeDtypeStruct((level_rows, width), bf16),
+            jax.ShapeDtypeStruct((3 * zp, width), bf16),
+            jax.ShapeDtypeStruct((zp, nl), bf16),
+            jax.ShapeDtypeStruct((zp, nl), bf16),
         ),
-        in_specs=[HBM, VMEM, VMEM],
-        out_specs=(VMEM,) * 4,
+        in_specs=[HBM, VMEM, VMEM, VMEM],
+        out_specs=(VMEM,) * 7,
         scratch_shapes=[
             pltpu.VMEM((tiles, cz, cx, LANE), f32),
             pltpu.VMEM((tiles, zp * SUB, LANE), f32),
@@ -624,32 +674,37 @@
         compiler_params=pltpu.CompilerParams(vmem_limit_bytes=VMEM_PACK),
         cost_estimate=pl.CostEstimate(flops=10**8, bytes_accessed=4 * 10**6, transcendentals=0),
         name="prep",
-    )(in_hbm(thermal_disturbance), layer_index_downscale, pos)
+    )(in_hbm(thermal_disturbance), layer_index_downscale, jnp.asarray(shift, f32), pos)
     lin = np.stack([power - np.eye(cz), total])
     *base, gain = pl.pallas_call(
         functools.partial(base_kernel, devices, carry),
         out_shape=(
             field,
             field,
-            jax.ShapeDtypeStruct((3 * nl, LANE), f32),
-            jax.ShapeDtypeStruct((nl, LANE), f32),
-            jax.ShapeDtypeStruct((cols, cols), jnp.bfloat16),
-            jax.ShapeDtypeStruct((devices * (rows - per), cols), jnp.bfloat16),
+            jax.ShapeDtypeStruct((3 * nl, LANE), bf16),
+            jax.ShapeDtypeStruct((3 * nl, LANE), bf16),
+            jax.ShapeDtypeStruct((nl, SLOT), bf16),
+            jax.ShapeDtypeStruct((nl, SLOT), bf16),
+            jax.ShapeDtypeStruct((cols, cols), bf16),
+            jax.ShapeDtypeStruct((devices * (rows - per), cols), bf16),
             jax.ShapeDtypeStruct((nl, nl), f32),
         ),
         in_specs=[VMEM] * (7 + len(ends)),
-        out_specs=(VMEM,) * 7,
+        out_specs=(VMEM,) * 9,
         compiler_params=pltpu.CompilerParams(vmem_limit_bytes=VMEM_PACK),
         cost_estimate=pl.CostEstimate(flops=10**8, bytes_accessed=10**6, transcendentals=0),
         name="base",
     )(*fields, layer_index_downscale, layer_index_upscale, jnp.asarray(lin, f32), pos, *ends)
-    vals = pl.pallas_call(
+    halo = (periodic_flow_velocity, jnp.asarray(ends_pick(), bf16)) if carry else ()
+    vals, *halo = pl.pallas_call(
         functools.partial(cloud_kernel, devices, carry, nl),
-        out_shape=jax.ShapeDtypeStruct((devices * rows, LANE), f32),
-        in_specs=[VMEM] * 7,
-        out_specs=VMEM,
+        out_shape=(jax.ShapeDtypeStruct((devices * rows, LANE), f32),)
+        + ((jax.ShapeDtypeStruct((nl, LANE), f32),) if carry else ()),
+        in_specs=[VMEM] * (11 + len(halo)),
+        out_specs=(VMEM,) * (2 if carry else 1),
         scratch_shapes=[
             pltpu.VMEM((tiles, cz, SUB * (groups + 2), LANE), f32),
+            pltpu.VMEM((zp, cols), f32),
             pltpu.VMEM((zp, cols), f32),
             pltpu.VMEM((zp, cols), f32),
             pltpu.VMEM((zp, cols), f32),
@@ -659,15 +714,12 @@
         ],
         compiler_params=pltpu.CompilerParams(vmem_limit_bytes=VMEM_CLOUD),
         name="cloud",
-    )(r1, *prep, jnp.asarray(mean, f32), gain)
+    )(r1, *prep, *halved(mean), gain, *halo)
     r2 = exchange(vals, 1, rows * LANE)
-    halo = ()
-    if carry:
-        halo = (gain, r1, periodic_flow_velocity, jnp.asarray(ends_pick(), jnp.bfloat16))
     return pl.pallas_call(
         functools.partial(finish_kernel, devices, carry),
         out_shape=(field,) * 3,
-        in_specs=[VMEM] * (8 + len(halo)),
+        in_specs=[VMEM] * (10 + len(halo)),
         out_specs=(VMEM,) * 3,
         compiler_params=pltpu.CompilerParams(vmem_limit_bytes=VMEM_PACK),
         name="finish",

time: 42 us -> 43.1 us (1.026)
  waiting for transfers between devices: 6.03 us -> 1.7 us
  local copies, waits for them, and re-layouts: 1.62 us -> 5.82 us
  blocking collectives: 11.3 us -> 12.8 us
    all_to_all x1, waiting for transfers between devices: 6.03 us -> 1.7 us  [exchange(): lax.all_to_all(blocks, AXES, split_axis=0, concat_axis=0, tiled=True)]
    unnamed x17 -> x21, local copies, waits for them, and re-layouts: 1.62 us -> 5.82 us
    all_to_all x1, blocking collectives: 11.3 us -> 12.8 us  [exchange(): lax.all_to_all(blocks, AXES, split_axis=0, concat_axis=0, tiled=True)]
where the time goes in v6:
time: 43.1 us; the launch traced here: 42.5 us
  Pallas kernels  14.1 us (33%)
  blocking collectives  12.8 us (30%)
  starting transfers between devices  7.33 us (17%)
  local copies, waits for them, and re-layouts  5.82 us (14%)
  waiting for transfers between devices  1.7 us (4%)
  between operations  0.73 us (2%)
    all_to_all x1, blocking collectives, exchange(): lax.all_to_all(blocks, AXES, split_axis=0, concat_axis=0, tiled=True)  12.8 us
    pallas_call x1, Pallas kernels, local(): pl.pallas_call(functools.partial(cloud_kernel, devices, carry, nl), out_s...  8.01 us
    all_to_all x1, starting transfers between devices, exchange(): lax.all_to_all(blocks, AXES, split_axis=0, concat_axis=0, tiled=True)  7.33 us
    unnamed x21, local copies, waits for them, and re-layouts  5.82 us
    pallas_call x1, Pallas kernels, local(): pl.pallas_call(functools.partial(pack_kernel, devices, carry), out_shape=...  2.14 us
    pallas_call x1, Pallas kernels, local(): pl.pallas_call(functools.partial(prep_kernel, carry), out_shape=(jax.Shap...  1.82 us
    all_to_all x1, waiting for transfers between devices, exchange(): lax.all_to_all(blocks, AXES, split_axis=0, concat_axis=0, tiled=True)  1.7 us
    pallas_call x1, Pallas kernels, local(): pl.pallas_call(functools.partial(finish_kernel, devices, carry), out_shap...  1.24 us
  transfers between devices with their start and end apart: 1, of which 1 were waited for; matrix products, arithmetic and copies ran while one was open for 2% of the time, Pallas kernels for 6%

profile of v6, /device:TPU:0, one launch (start us, length us, event | category | flops | bytes accessed | tf_op | source)
XLA Modules:
  0.0 42.5 jit_solution(12890689417334712484)
XLA Ops:
  0.6 0.0 copy-start.4
  0.6 0.0 copy-start.5
  0.7 0.0 copy-start.8
  0.7 0.0 copy-start.1
  0.7 2.1 %pack.1 = (f32[256,256]{1,0:T(8,128)}, s32[1,256]{1,0:T(1,128)S(1)}) custom-call(f32[72,256]{1,0:T(8,128)} %refs_0_.4, f32[72,256]{1,0:T(8,128)} %refs_1_.4, f32[72,256]{1,0:T(8,128)} %refs_0_.5, s32[1,256]{1,0:T(1,128)} %bitcast.8), custom_call_target="tpu_custom_call" | custom-call | tf_op jit(solution)/shard_map/pack/pallas_call | solution.py:612
  2.8 7.3 %all-to-all-start = ((f32[32,8,256]{2,1,0:T(8,128)}), f32[32,8,256]{2,1,0:T(8,128)S(1)}, u32[]{:S(2)}, u32[]{:S(2)}) async-start(f32[32,8,256]{2,1,0:T(8,128)} %bitcast.1), calls=%async_computation | async-start | bytes 524288 | tf_op jit(solution)/shard_map/all_to_all | solution.py:635
  10.2 0.8 %copy.16.refs_4_ = f32[72,50]{1,0:T(8,128)S(1)} copy(f32[72,50]{0,1:T(8,128)} %param.18) | data formatting | bytes 28800 | tf_op args[6]
  11.0 0.0 copy-start
  11.0 0.9 %copy-done = f32[72,256]{1,0:T(8,128)S(1)} copy-done((f32[72,256]{1,0:T(8,128)S(1)}, f32[72,256]{1,0:T(8,128)}, u32[]{:S(2)}) %copy-start) | copy-done | bytes 73752
  11.9 0.0 copy-start.2
  11.9 0.9 %copy-done.2 = f32[72,256]{1,0:T(8,128)S(1)} copy-done((f32[72,256]{1,0:T(8,128)S(1)}, f32[72,256]{1,0:T(8,128)}, u32[]{:S(2)}) %copy-start.2) | copy-done | bytes 73752
  12.8 0.0 copy-start.3
  12.8 0.9 %copy-done.3 = f32[72,256]{1,0:T(8,128)S(1)} copy-done((f32[72,256]{1,0:T(8,128)S(1)}, f32[72,256]{1,0:T(8,128)}, u32[]{:S(2)}) %copy-start.3) | copy-done | bytes 73752
  13.7 0.0 copy-start.6
  13.7 0.7 %copy-done.6 = f32[50,72]{1,0:T(8,128)S(1)} copy-done((f32[50,72]{1,0:T(8,128)S(1)}, f32[50,72]{1,0:T(8,128)}, u32[]{:S(2)}) %copy-start.6) | copy-done | bytes 14424
  14.4 0.0 copy-start.9
  14.4 0.8 %copy-done.9 = f32[2,50,50]{2,1,0:T(8,128)S(1)} copy-done((f32[2,50,50]{2,1,0:T(8,128)S(1)}, f32[2,50,50]{2,1,0:T(8,128)}, u32[]{:S(2)}) %copy-start.9) | copy-done | bytes 20024
  15.2 0.9 %base.1 = (f32[72,256]{1,0:T(8,128)S(1)}, f32[72,256]{1,0:T(8,128)S(1)}, bf16[216,128]{1,0:T(8,128)(2,1)S(1)}, bf16[216,128]{1,0:T(8,128)(2,1)S(1)}, bf16[72,32]...) custom-call(f32[72,256]{1,0:T(8,128)S(1)} %copy-done.2, ...), custom_call_target="tpu_custom_call" | custom-call | flops 100000000 | bytes 1000000 | tf_op jit(solution)/shard_map/base/pallas_call | solution.py:679
  16.1 0.0 copy-start.7
  16.1 0.7 %copy-done.7 = f32[50,50]{1,0:T(8,128)S(1)} copy-done((f32[50,50]{1,0:T(8,128)S(1)}, f32[50,50]{1,0:T(8,128)}, u32[]{:S(2)}) %copy-start.7) | copy-done | bytes 10024
  16.9 1.8 %prep.1 = (f32[2,50,32,128]{3,2,1,0:T(8,128)S(1)}, f32[56,256]{1,0:T(8,128)S(1)}, f32[8,128]{1,0:T(8,128)S(1)}, bf16[280,256]{1,0:T(8,128)(2,1)S(1)}, bf16[168,2...) custom-call(f32[50,32,256]{2,1,0:T(8,128)} %td_ref.1, f32[50,72]{1,0:T(8,128)S(1)} %copy-done.6, ...), custom_call_target="tpu_custom_call" | custom-call | flops 100000000 | bytes 4000000 | tf_op jit(solution)/shard_map/prep/pallas_call | solution.py:656
  18.7 1.7 %all-to-all-done = f32[32,8,256]{2,1,0:T(8,128)S(1)} async-done(((f32[32,8,256]{2,1,0:T(8,128)}), f32[32,8,256]{2,1,0:T(8,128)S(1)}, u32[]{:S(2)}, u32[]{:S(2)}) %all-to-all-start) | async-done | bytes 262176 | tf_op jit(solution)/shard_map/all_to_all | solution.py:635
  20.4 0.0 copy-done.4
  20.4 0.0 copy-done.5
  20.4 0.0 copy-done.8
  20.4 0.0 copy-done.1
  20.4 8.0 %cloud.1 = (f32[320,128]{1,0:T(8,128)S(1)}, f32[72,128]{1,0:T(8,128)S(1)}) custom-call(f32[256,256]{1,0:T(8,128)S(1)} %bitcast.5, f32[2,50,32,128]{3,2,1,0:T(8,128)S(1)} %get-tuple-element.25.start_ref, f32[56,256]{1,0:T(8,128)S(1)} %get-tuple-element.26.td_mean_ref, f32[8,128]{1,0:T(8,128)S(1)} %get-tuple-element.27.most_ref, ...), custom_call_target="tpu_custom_call" | custom-call | tf_op jit(solution)/shard_map/cloud/pallas_call | solution.py:699
  28.4 12.8 %all_to_all.10 = f32[32,1,1280]{2,1,0:T(1,128)S(1)} all-to-all(f32[32,1,1280]{2,1,0:T(1,128)S(1)} %bitcast.7), channel_id=1, replica_groups=mesh['tile'=8,'crm'=4] {'tile','crm'}, dimensions={0} | all-to-all | bytes 327680 | tf_op jit(solution)/shard_map/all_to_all | solution.py:635
  41.2 1.2 %finish.1 = (f32[72,256]{1,0:T(8,128)}, f32[72,256]{1,0:T(8,128)}, f32[72,256]{1,0:T(8,128)}) custom-call(f32[320,128]{1,0:T(8,128)S(1)} %bitcast.6, s32[1,256]{1,0:T(1,128)S(1)} %get-tuple-element.24.after_ref.refs_6_.refs_1_, f32[72,256]{1,0:T(8,128)S(1)} %get-tuple-element.34.refs_2_, f32[72,256]{1,0:T(8,128)S(1)} %get-tuple-element.35.refs_3_, ...), custom_call_target="tpu_custom_call" | custom-call | tf_op jit(solution)/shard_map/finish/pallas_call | solution.py:719
Async XLA Ops:
  0.6 19.8 %copy-start.4 = (bf16[248,128]{1,0:T(8,128)(2,1)S(1)}, bf16[248,128]{1,0:T(8,128)(2,1)}, u32[]{:S(2)}) copy-start(bf16[248,128]{1,0:T(8,128)(2,1)} %constant.14.clone.mean_low_ref) | copy-start | bytes 190468
  0.6 19.8 %copy-start.5 = (bf16[248,128]{1,0:T(8,128)(2,1)S(1)}, bf16[248,128]{1,0:T(8,128)(2,1)}, u32[]{:S(2)}) copy-start(bf16[248,128]{1,0:T(8,128)(2,1)} %constant.13.clone.mean_high_ref) | copy-start | bytes 190468
  0.7 19.7 %copy-start.8 = (bf16[16,256]{1,0:T(8,128)(2,1)S(1)}, bf16[16,256]{1,0:T(8,128)(2,1)}, u32[]{:S(2)}) copy-start(bf16[16,256]{1,0:T(8,128)(2,1)} %constant.12.clone.refs_1_) | copy-start | bytes 24580
  0.7 19.7 %copy-start.1 = (f32[72,256]{1,0:T(8,128)S(1)}, f32[72,256]{1,0:T(8,128)}, u32[]{:S(2)}) copy-start(f32[72,256]{1,0:T(8,128)} %refs_0_.5) | copy-start | bytes 221188
  2.8 17.6 %all-to-all-start = ((f32[32,8,256]{2,1,0:T(8,128)}), f32[32,8,256]{2,1,0:T(8,128)S(1)}, u32[]{:S(2)}, u32[]{:S(2)}) async-start(f32[32,8,256]{2,1,0:T(8,128)} %bitcast.1), calls=%async_computation | async-start | bytes 524288 | tf_op jit(solution)/shard_map/all_to_all | solution.py:635
  11.0 0.9 %copy-start = (f32[72,256]{1,0:T(8,128)S(1)}, f32[72,256]{1,0:T(8,128)}, u32[]{:S(2)}) copy-start(f32[72,256]{1,0:T(8,128)} %refs_0_.5) | copy-start | bytes 221188
  11.9 0.9 %copy-start.2 = (f32[72,256]{1,0:T(8,128)S(1)}, f32[72,256]{1,0:T(8,128)}, u32[]{:S(2)}) copy-start(f32[72,256]{1,0:T(8,128)} %refs_0_.4) | copy-start | bytes 221188
  12.8 0.9 %copy-start.3 = (f32[72,256]{1,0:T(8,128)S(1)}, f32[72,256]{1,0:T(8,128)}, u32[]{:S(2)}) copy-start(f32[72,256]{1,0:T(8,128)} %refs_1_.4) | copy-start | bytes 221188
  13.7 0.7 %copy-start.6 = (f32[50,72]{1,0:T(8,128)S(1)}, f32[50,72]{1,0:T(8,128)}, u32[]{:S(2)}) copy-start(f32[50,72]{1,0:T(8,128)} %refs_3_.1) | copy-start | bytes 43204
  14.4 0.8 %copy-start.9 = (f32[2,50,50]{2,1,0:T(8,128)S(1)}, f32[2,50,50]{2,1,0:T(8,128)}, u32[]{:S(2)}) copy-start(f32[2,50,50]{2,1,0:T(8,128)} %constant.11.clone.refs_5_) | copy-start | bytes 60004
  16.1 0.8 %copy-start.7 = (f32[50,50]{1,0:T(8,128)S(1)}, f32[50,50]{1,0:T(8,128)}, u32[]{:S(2)}) copy-start(f32[50,50]{1,0:T(8,128)} %constant.10.clone.shift_ref) | copy-start | bytes 30004

commit v7 on v6

--- a/solution.py
+++ b/solution.py
@@ -30,6 +30,15 @@
 
 def in_hbm(x):
     return pltpu.with_memory_space_constraint(x, pltpu.HBM)
+
+
+def fetch(sources, targets, sem):
+    copies = [
+        pltpu.make_async_copy(a, b, sem.at[n]) for n, (a, b) in enumerate(zip(sources, targets))
+    ]
+    for copy in copies:
+        copy.start()
+    return copies
 
 
 def up_to(n, m):
@@ -235,12 +244,11 @@
     return pl.ds(k * LANE, LANE)
 
 
-def fold(part_ref, out_ref, k, scale):
-    levels = out_ref.shape[0]
+def fold(part_ref, levels, scale):
     total = part_ref[pl.ds(0, levels, stride=SUB), :]
     for s in range(1, SUB):
         total = total + part_ref[pl.ds(s, levels, stride=SUB), :]
-    out_ref[:, lanes(k)] = total * scale
+    return total * scale
 
 
 def clear_tail(part_ref, cz):
@@ -249,8 +257,9 @@
             part_ref[n, pl.ds(z, SUB), :] = jnp.zeros((SUB, LANE), jnp.float32)
 
 
-def prep_kernel(carry, td_ref, down_ref, shift_ref, after_ref, start_ref, mean_ref, most_ref,
-                high_ref, low_ref, shift_high_ref, shift_low_ref, raw_ref, part_ref, td_sem):
+def prep_kernel(carry, td_ref, down_hbm, shift_hbm, after_ref, start_ref, mean_ref, most_ref,
+                high_ref, low_ref, shift_high_ref, shift_low_ref, raw_ref, part_ref, down_ref,
+                shift_ref, td_sem, sem):
     del after_ref
     cz, cx, cols = td_ref.shape
     nl = down_ref.shape[1]
@@ -266,9 +275,12 @@
             td_ref.at[levels, :, lanes(k)], raw_ref.at[k, levels], td_sem.at[k, c]
         )
 
+    copies = fetch((down_hbm, shift_hbm), (down_ref, shift_ref), sem)
     for k in range(tiles):
         for c in range(td_sem.shape[1]):
             td_copy(k, c).start()
+    for copy in copies:
+        copy.wait()
 
     def wide(rows):
         rows = jnp.concatenate(
@@ -307,15 +319,18 @@
                 start_ref[k, z, pl.ds(SUB * i, SUB), :] = first
                 most[i] = jnp.maximum(most[i], jnp.abs(first))
             part_ref[k, pl.ds(z * SUB, SUB), :] = total
-        fold(part_ref.at[k], mean_ref, k, 1.0 / cx)
+        mean_ref[:, lanes(k)] = fold(part_ref.at[k], zp, 1.0 / cx)
     most_ref[...] = functools.reduce(jnp.maximum, most)
 
 
 def cloud_kernel(devices, carry, nl, r_ref, start_ref, td_mean_ref, most_ref, g_high_ref, g_low_ref,
-                 shift_high_ref, shift_low_ref, mean_high_ref, mean_low_ref, after_ref, *refs):
+                 shift_high_ref, shift_low_ref, early_high_ref, early_low_ref,
+                 late_high_ref, late_low_ref, after_ref, *refs):
     gain_ref, v_ref, ends_ref = (after_ref, *refs[:2]) if carry else (None,) * 3
     out_ref, halo_ref = refs[2:4] if carry else (refs[0], None)
-    d_ref, base_ref, east_ref, west_ref, shift_ref, scale_ref, val_ref, part_ref = refs[-8:]
+    d_ref, base_ref, east_ref, west_ref, shift_ref, scale_ref, late_ref, value_ref, part_ref = (
+        refs[-9:]
+    )
     tiles, cz, cx, _ = start_ref.shape
     zp, cols = td_mean_ref.shape
     per = cols // devices
@@ -361,9 +376,9 @@
     bound = growth * (jnp.max(jnp.abs(base)) + jnp.max(most_ref[...])) + series * drain * (
         jnp.max(jnp.abs(shift)) + 1.0
     )
-    val_ref[0:zp, :] = td_mean_ref[...]
-    val_ref[zp:2 * zp, :] = d0 - 0.5 * td_mean_ref[...]
-    val_ref[2 * zp:3 * zp, :] = shift
+    value_ref[0:zp, :] = td_mean_ref[...]
+    value_ref[zp:2 * zp, :] = d0 - 0.5 * td_mean_ref[...]
+    value_ref[2 * zp:, :] = shift
     clear_tail(part_ref, cz)
 
     def row_at(ref, z, k):
@@ -416,62 +431,75 @@
                 below, cur = cur, above
         return carry
 
+    def finish(small):
+        lax.fori_loop(0, SUBSTEPS, functools.partial(step, small), 0)
+        head, rows = return_shape(cz, per)
+        cloud_ref = east_ref
+        for k in range(tiles):
+            for z in range(cz):
+                total = cloud = None
+                move = row_at(scale_ref if small else shift_ref, z, k)
+                for f in get(k, z):
+                    c = moved_softplus2(small, f, move)
+                    total = f if total is None else total + f
+                    cloud = c if cloud is None else cloud + c
+                part_ref[2 * k, pl.ds(z * SUB, SUB), :] = total
+                part_ref[2 * k + 1, pl.ds(z * SUB, SUB), :] = cloud
+            early = dot3(
+                split(value_ref[:, lanes(k)]), (early_high_ref[...], early_low_ref[...]), 0, 0
+            )
+            if carry and k == 0:
+                halo = halo_part(devices, r_ref, ends_ref, v_ref)
+                halo_ref[...] = halo + dot(gain_ref[...], halo, 1, 0, HI)
+            moved = LN2 * shift_ref[:, lanes(k)]
+            end = fold(part_ref.at[2 * k], zp, LN2 / cx) - moved
+            cloud = fold(part_ref.at[2 * k + 1], zp, LN2 / cx) - moved
+            late_ref[0:zp, lanes(k)] = end
+            late_ref[zp:, lanes(k)] = cloud[0:head]
+            cloud_ref[:, lanes(k)] = cloud
+            late = dot3(split(late_ref[:, lanes(k)]), (late_high_ref[...], late_low_ref[...]), 0, 0)
+            main = early + late
+            for h in range(LANE // per):
+                out_ref[pl.ds((k * (LANE // per) + h) * rows, per), :] = main[h * per:(h + 1) * per]
+        left = cloud_ref[head:, :]
+        left = jnp.concatenate([left, jnp.zeros((SLOT - left.shape[0], cols), jnp.float32)], axis=0) \
+            if left.shape[0] < SLOT else left
+        place = lax.broadcasted_iota(jnp.int32, (1, cols), 1)
+        part = place % SLOTS
+        spread = jnp.concatenate(
+            [jnp.where(part == j, left, 0.0) for j in range(SLOTS)], axis=0
+        )
+        pick = slot_onehot(place, devices, per, cols)
+        a, b = split(spread)
+        extra = dot(pick, a, 1, 1) + dot(pick, b, 1, 1)
+        for i in range(rows - per):
+            out_ref[pl.ds(per + i, devices, stride=rows), :] = extra[i * devices:(i + 1) * devices]
+
     @pl.when(bound < LARGEST)
     def _():
-        lax.fori_loop(0, SUBSTEPS, functools.partial(step, True), 0)
+        finish(True)
 
     @pl.when(jnp.logical_not(bound < LARGEST))
     def _():
-        lax.fori_loop(0, SUBSTEPS, functools.partial(step, False), 0)
-
-    if carry:
-        halo = halo_part(devices, r_ref, ends_ref, v_ref)
-        halo_ref[...] = halo + dot(gain_ref[...], halo, 1, 0, HI)
-
-    head, rows = return_shape(cz, per)
-    cloud_ref = east_ref
-    for k in range(tiles):
-        for z in range(cz):
-            total = cloud = None
-            move = row_at(shift_ref, z, k)
-            for f in get(k, z):
-                f = f - move
-                c = softplus2(f)
-                total = f if total is None else total + f
-                cloud = c if cloud is None else cloud + c
-            part_ref[2 * k, pl.ds(z * SUB, SUB), :] = total
-            part_ref[2 * k + 1, pl.ds(z * SUB, SUB), :] = cloud
-        fold(part_ref.at[2 * k], val_ref.at[pl.ds(3 * zp, zp)], k, LN2 / cx)
-        fold(part_ref.at[2 * k + 1], cloud_ref, k, LN2 / cx)
-        val_ref[4 * zp:, lanes(k)] = cloud_ref[0:head, lanes(k)]
-        main = dot3(split(val_ref[:, lanes(k)]), (mean_high_ref[...], mean_low_ref[...]), 0, 0)
-        for h in range(LANE // per):
-            out_ref[pl.ds((k * (LANE // per) + h) * rows, per), :] = main[h * per:(h + 1) * per]
-    left = cloud_ref[head:, :]
-    left = jnp.concatenate([left, jnp.zeros((SLOT - left.shape[0], cols), jnp.float32)], axis=0) \
-        if left.shape[0] < SLOT else left
-    place = lax.broadcasted_iota(jnp.int32, (1, cols), 1)
-    part = place % SLOTS
-    spread = jnp.concatenate(
-        [jnp.where(part == j, left, 0.0) for j in range(SLOTS)], axis=0
-    )
-    pick = slot_onehot(place, devices, per, cols)
-    a, b = split(spread)
-    extra = dot(pick, a, 1, 1) + dot(pick, b, 1, 1)
-    for i in range(rows - per):
-        out_ref[pl.ds(per + i, devices, stride=rows), :] = extra[i * devices:(i + 1) * devices]
+        finish(False)
 
 
 def base_kernel(devices, carry, *refs):
-    t_ref, q_ref, v_ref, down_ref, up_ref, lin_ref, pos_ref = refs[:7]
+    pos_ref = refs[6]
     low_ref, high_ref = (None, None) if carry else refs[7:9]
-    to_ref, qo_ref, level_high_ref, level_low_ref, rest_high_ref, rest_low_ref = refs[-9:-3]
-    sel_ref, pick_ref, gain_ref = refs[-3:]
+    to_ref, qo_ref, level_high_ref, level_low_ref, rest_high_ref, rest_low_ref = refs[-16:-10]
+    sel_ref, pick_ref, gain_ref = refs[-10:-7]
+    t_ref, q_ref, v_ref, down_ref, up_ref, lin_ref, sem = refs[-7:]
+    copies = fetch(refs[:6], refs[-7:-1], sem)
     nl, cols = t_ref.shape
-    cz = up_ref.shape[1]
+    cz = up_ref.shape[0]
     per = cols // devices
     head, _ = return_shape(cz, per)
-    up = up_ref[...]
+    sel_ref[...] = onehot(pos_ref[...], cols)
+    pick_ref[...] = slot_onehot(pos_ref[...], devices, per, cols)
+    for copy in copies:
+        copy.wait()
+    up = up_ref[...].T
     wide = jnp.concatenate([up, jnp.zeros((nl, LANE - cz), jnp.float32)], axis=1)
     lane = lax.broadcasted_iota(jnp.int32, wide.shape, 1)
     level = jnp.concatenate(
@@ -485,8 +513,6 @@
     level_high_ref[...], level_low_ref[...] = split(level)
     rest = jnp.where(lane < SLOT, pltpu.roll(wide, LANE - head, 1), 0.0)
     rest_high_ref[...], rest_low_ref[...] = split(rest[:, 0:SLOT])
-    sel_ref[...] = onehot(pos_ref[...], cols)
-    pick_ref[...] = slot_onehot(pos_ref[...], devices, per, cols)
     if carry:
         low = high = (jnp.zeros((nl, 1), jnp.float32),) * 2
     else:
@@ -664,17 +690,25 @@
             jax.ShapeDtypeStruct((zp, nl), bf16),
             jax.ShapeDtypeStruct((zp, nl), bf16),
         ),
-        in_specs=[HBM, VMEM, VMEM, VMEM],
+        in_specs=[HBM, HBM, HBM, VMEM],
         out_specs=(VMEM,) * 7,
         scratch_shapes=[
             pltpu.VMEM((tiles, cz, cx, LANE), f32),
             pltpu.VMEM((tiles, zp * SUB, LANE), f32),
+            pltpu.VMEM((cz, nl), f32),
+            pltpu.VMEM((cz, cz), f32),
             pltpu.SemaphoreType.DMA((tiles, 5)),
+            pltpu.SemaphoreType.DMA((2,)),
         ],
         compiler_params=pltpu.CompilerParams(vmem_limit_bytes=VMEM_PACK),
         cost_estimate=pl.CostEstimate(flops=10**8, bytes_accessed=4 * 10**6, transcendentals=0),
         name="prep",
-    )(in_hbm(thermal_disturbance), layer_index_downscale, jnp.asarray(shift, f32), pos)
+    )(
+        in_hbm(thermal_disturbance),
+        in_hbm(layer_index_downscale),
+        in_hbm(jnp.asarray(shift, f32)),
+        pos,
+    )
     lin = np.stack([power - np.eye(cz), total])
     *base, gain = pl.pallas_call(
         functools.partial(base_kernel, devices, carry),
@@ -689,18 +723,39 @@
             jax.ShapeDtypeStruct((devices * (rows - per), cols), bf16),
             jax.ShapeDtypeStruct((nl, nl), f32),
         ),
-        in_specs=[VMEM] * (7 + len(ends)),
+        in_specs=[HBM] * 6 + [VMEM] * (1 + len(ends)),
         out_specs=(VMEM,) * 9,
+        scratch_shapes=[
+            pltpu.VMEM((nl, cols), f32),
+            pltpu.VMEM((nl, cols), f32),
+            pltpu.VMEM((nl, cols), f32),
+            pltpu.VMEM((cz, nl), f32),
+            pltpu.VMEM((cz, nl), f32),
+            pltpu.VMEM((2, cz, cz), f32),
+            pltpu.SemaphoreType.DMA((6,)),
+        ],
         compiler_params=pltpu.CompilerParams(vmem_limit_bytes=VMEM_PACK),
         cost_estimate=pl.CostEstimate(flops=10**8, bytes_accessed=10**6, transcendentals=0),
         name="base",
-    )(*fields, layer_index_downscale, layer_index_upscale, jnp.asarray(lin, f32), pos, *ends)
+    )(
+        *[
+            in_hbm(x)
+            for x in (
+                *fields,
+                layer_index_downscale,
+                layer_index_upscale.T,
+                jnp.asarray(lin, f32),
+            )
+        ],
+        pos,
+        *ends,
+    )
     halo = (periodic_flow_velocity, jnp.asarray(ends_pick(), bf16)) if carry else ()
     vals, *halo = pl.pallas_call(
         functools.partial(cloud_kernel, devices, carry, nl),
         out_shape=(jax.ShapeDtypeStruct((devices * rows, LANE), f32),)
         + ((jax.ShapeDtypeStruct((nl, LANE), f32),) if carry else ()),
-        in_specs=[VMEM] * (11 + len(halo)),
+        in_specs=[VMEM] * (13 + len(halo)),
         out_specs=(VMEM,) * (2 if carry else 1),
         scratch_shapes=[
             pltpu.VMEM((tiles, cz, SUB * (groups + 2), LANE), f32),
@@ -709,12 +764,13 @@
             pltpu.VMEM((zp, cols), f32),
             pltpu.VMEM((zp, cols), f32),
             pltpu.VMEM((zp, cols), f32),
-            pltpu.VMEM((4 * zp + head, cols), f32),
+            pltpu.VMEM((zp + head, cols), f32),
+            pltpu.VMEM((3 * zp, cols), f32),
             pltpu.VMEM((2 * tiles, zp * SUB, LANE), f32),
         ],
         compiler_params=pltpu.CompilerParams(vmem_limit_bytes=VMEM_CLOUD),
         name="cloud",
-    )(r1, *prep, *halved(mean), gain, *halo)
+    )(r1, *prep, *halved(mean[:3 * zp]), *halved(mean[3 * zp:]), gain, *halo)
     r2 = exchange(vals, 1, rows * LANE)
     return pl.pallas_call(
         functools.partial(finish_kernel, devices, carry),

time: 43.1 us -> 41.1 us (0.954)
  local copies, waits for them, and re-layouts: 5.82 us -> 0.04 us
  waiting for transfers between devices: 1.7 us -> 6.26 us
  blocking collectives: 12.8 us -> 11.3 us
  Pallas kernels: 14.1 us -> 15.1 us
    unnamed x21 -> x12, local copies, waits for them, and re-layouts: 5.82 us -> 0.04 us
    all_to_all x1, waiting for transfers between devices: 1.7 us -> 6.26 us  [exchange(): lax.all_to_all(blocks, AXES, split_axis=0, concat_axis=0, tiled=True)]
    all_to_all x1, blocking collectives: 12.8 us -> 11.3 us  [exchange(): lax.all_to_all(blocks, AXES, split_axis=0, concat_axis=0, tiled=True)]
    pallas_call x1, Pallas kernels: 0.88 us -> 1.9 us  [local(): pl.pallas_call(functools.partial(base_kernel, devices, carry), out_shape=...]
  transfers between devices with their start and end apart: 1 -> 1, of which waited for: 1 -> 1; matrix products, arithmetic and copies ran while one was open for 2% -> 0% of each run, Pallas kernels for 6% -> 10%
where the time goes in v7:
time: 41.1 us; the launch traced here: 40.8 us
  Pallas kernels  15.1 us (37%)
  blocking collectives  11.3 us (27%)
  starting transfers between devices  7.33 us (18%)
  waiting for transfers between devices  6.26 us (15%)
  between operations  0.75 us (2%)
    all_to_all x1, blocking collectives, exchange(): lax.all_to_all(blocks, AXES, split_axis=0, concat_axis=0, tiled=True)  11.3 us
    pallas_call x1, Pallas kernels, local(): pl.pallas_call(functools.partial(cloud_kernel, devices, carry, nl), out_s...  7.78 us
    all_to_all x1, starting transfers between devices, exchange(): lax.all_to_all(blocks, AXES, split_axis=0, concat_axis=0, tiled=True)  7.33 us
    all_to_all x1, waiting for transfers between devices, exchange(): lax.all_to_all(blocks, AXES, split_axis=0, concat_axis=0, tiled=True)  6.26 us
    pallas_call x1, Pallas kernels, local(): pl.pallas_call(functools.partial(pack_kernel, devices, carry), out_shape=...  2.14 us
    pallas_call x1, Pallas kernels, local(): pl.pallas_call(functools.partial(prep_kernel, carry), out_shape=(jax.Shap...  2.05 us
    pallas_call x1, Pallas kernels, local(): pl.pallas_call(functools.partial(base_kernel, devices, carry), out_shape=...  1.9 us
    pallas_call x1, Pallas kernels, local(): pl.pallas_call(functools.partial(finish_kernel, devices, carry), out_shap...  1.24 us
  transfers between devices with their start and end apart: 1, of which 1 were waited for; matrix products, arithmetic and copies ran while one was open for 0% of the time, Pallas kernels for 10%

profile of v7, /device:TPU:0, one launch (start us, length us, event | category | flops | bytes accessed | tf_op | source)
XLA Modules:
  0.0 40.8 jit_solution(1938539149394239595)
XLA Ops:
  0.6 0.0 copy-start.3
  0.6 0.0 copy-start.4
  0.7 0.0 copy-start.1
  0.7 0.0 copy-start.2
  0.7 0.0 copy-start.5
  0.7 0.0 copy-start
  0.7 2.1 %pack.1 = (f32[256,256]{1,0:T(8,128)}, s32[1,256]{1,0:T(1,128)S(1)}) custom-call(f32[72,256]{1,0:T(8,128)} %refs_0_.4, f32[72,256]{1,0:T(8,128)} %refs_1_.4, f32[72,256]{1,0:T(8,128)} %refs_0_.5, s32[1,256]{1,0:T(1,128)} %bitcast.9), custom_call_target="tpu_custom_call" | custom-call | tf_op jit(solution)/shard_map/pack/pallas_call | solution.py:638
  2.8 7.3 %all-to-all-start = ((f32[32,8,256]{2,1,0:T(8,128)}), f32[32,8,256]{2,1,0:T(8,128)S(1)}, u32[]{:S(2)}, u32[]{:S(2)}) async-start(f32[32,8,256]{2,1,0:T(8,128)} %bitcast.1), calls=%async_computation | async-start | bytes 524288 | tf_op jit(solution)/shard_map/all_to_all | solution.py:661
  10.2 1.9 %base.1 = (f32[72,256]{1,0:T(8,128)S(1)}, f32[72,256]{1,0:T(8,128)S(1)}, bf16[216,128]{1,0:T(8,128)(2,1)S(1)}, bf16[216,128]{1,0:T(8,128)(2,1)S(1)}, bf16[72,32]...) custom-call(f32[72,256]{1,0:T(8,128)} %refs_0_.4, ...), custom_call_target="tpu_custom_call" | custom-call | flops 100000000 | bytes 1000000 | tf_op jit(solution)/shard_map/base/pallas_call | solution.py:713
  12.1 2.1 %prep.1 = (f32[2,50,32,128]{3,2,1,0:T(8,128)S(1)}, f32[56,256]{1,0:T(8,128)S(1)}, f32[8,128]{1,0:T(8,128)S(1)}, bf16[280,256]{1,0:T(8,128)(2,1)S(1)}, bf16[168,2...) custom-call(f32[50,32,256]{2,1,0:T(8,128)} %td_ref.1, f32[50,72]{1,0:T(8,128)} %refs_3_.1, ...), custom_call_target="tpu_custom_call" | custom-call | flops 100000000 | bytes 4000000 | tf_op jit(solution)/shard_map/prep/pallas_call | solution.py:682
  14.2 6.3 %all-to-all-done = f32[32,8,256]{2,1,0:T(8,128)S(1)} async-done(((f32[32,8,256]{2,1,0:T(8,128)}), f32[32,8,256]{2,1,0:T(8,128)S(1)}, u32[]{:S(2)}, u32[]{:S(2)}) %all-to-all-start) | async-done | bytes 262176 | tf_op jit(solution)/shard_map/all_to_all | solution.py:661
  20.4 0.0 copy-done.3
  20.4 0.0 copy-done.4
  20.4 0.0 copy-done.1
  20.4 0.0 copy-done.2
  20.4 0.0 copy-done.5
  20.4 0.0 copy-done
  20.5 7.8 %cloud.1 = (f32[320,128]{1,0:T(8,128)S(1)}, f32[72,128]{1,0:T(8,128)S(1)}) custom-call(f32[256,256]{1,0:T(8,128)S(1)} %bitcast.6, f32[2,50,32,128]{3,2,1,0:T(8,128)S(1)} %get-tuple-element.25.start_ref, f32[56,256]{1,0:T(8,128)S(1)} %get-tuple-element.26.td_mean_ref, f32[8,128]{1,0:T(8,128)S(1)} %get-tuple-element.27.most_ref, ...), custom_call_target="tpu_custom_call" | custom-call | tf_op jit(solution)/shard_map/cloud/pallas_call | solution.py:754
  28.2 11.3 %all_to_all.10 = f32[32,1,1280]{2,1,0:T(1,128)S(1)} all-to-all(f32[32,1,1280]{2,1,0:T(1,128)S(1)} %bitcast.8), channel_id=1, replica_groups=mesh['tile'=8,'crm'=4] {'tile','crm'}, dimensions={0} | all-to-all | bytes 327680 | tf_op jit(solution)/shard_map/all_to_all | solution.py:661
  39.6 1.2 %finish.1 = (f32[72,256]{1,0:T(8,128)}, f32[72,256]{1,0:T(8,128)}, f32[72,256]{1,0:T(8,128)}) custom-call(f32[320,128]{1,0:T(8,128)S(1)} %bitcast.7, s32[1,256]{1,0:T(1,128)S(1)} %get-tuple-element.24.after_ref.refs_6_.refs_1_, f32[72,256]{1,0:T(8,128)S(1)} %get-tuple-element.34.refs_2_, f32[72,256]{1,0:T(8,128)S(1)} %get-tuple-element.35.refs_3_, ...), custom_call_target="tpu_custom_call" | custom-call | tf_op jit(solution)/shard_map/finish/pallas_call | solution.py:775
Async XLA Ops:
  0.6 19.8 %copy-start.3 = (bf16[80,128]{1,0:T(8,128)(2,1)S(1)}, bf16[80,128]{1,0:T(8,128)(2,1)}, u32[]{:S(2)}) copy-start(bf16[80,128]{1,0:T(8,128)(2,1)} %constant.20.clone.late_low_ref) | copy-start | bytes 61444
  0.6 19.8 %copy-start.4 = (bf16[80,128]{1,0:T(8,128)(2,1)S(1)}, bf16[80,128]{1,0:T(8,128)(2,1)}, u32[]{:S(2)}) copy-start(bf16[80,128]{1,0:T(8,128)(2,1)} %constant.19.clone.late_high_ref) | copy-start | bytes 61444
  0.7 19.8 %copy-start.1 = (bf16[168,128]{1,0:T(8,128)(2,1)S(1)}, bf16[168,128]{1,0:T(8,128)(2,1)}, u32[]{:S(2)}) copy-start(bf16[168,128]{1,0:T(8,128)(2,1)} %constant.18.clone.early_low_ref) | copy-start | bytes 129028
  0.7 19.8 %copy-start.2 = (bf16[168,128]{1,0:T(8,128)(2,1)S(1)}, bf16[168,128]{1,0:T(8,128)(2,1)}, u32[]{:S(2)}) copy-start(bf16[168,128]{1,0:T(8,128)(2,1)} %constant.17.clone.early_high_ref) | copy-start | bytes 129028
  0.7 19.8 %copy-start.5 = (bf16[16,256]{1,0:T(8,128)(2,1)S(1)}, bf16[16,256]{1,0:T(8,128)(2,1)}, u32[]{:S(2)}) copy-start(bf16[16,256]{1,0:T(8,128)(2,1)} %constant.16.clone.refs_1_) | copy-start | bytes 24580
  0.7 19.8 %copy-start = (f32[72,256]{1,0:T(8,128)S(1)}, f32[72,256]{1,0:T(8,128)}, u32[]{:S(2)}) copy-start(f32[72,256]{1,0:T(8,128)} %refs_0_.5) | copy-start | bytes 221188
  2.8 17.6 %all-to-all-start = ((f32[32,8,256]{2,1,0:T(8,128)}), f32[32,8,256]{2,1,0:T(8,128)S(1)}, u32[]{:S(2)}, u32[]{:S(2)}) async-start(f32[32,8,256]{2,1,0:T(8,128)} %bitcast.1), calls=%async_computation | async-start | bytes 524288 | tf_op jit(solution)/shard_map/all_to_all | solution.py:661

commit v8 on v7

--- a/solution.py
+++ b/solution.py
@@ -227,13 +227,21 @@
     out_ref[...] = out
 
 
-LARGEST = 120.0
+LARGEST = 60.0
 
 
 def moved_softplus2(small, g, move):
     if small:
         return jnp.log2(move + jnp.exp2(g))
     return move + softplus2(g - move)
+
+
+def moved_sum(small, parts, move):
+    if not small:
+        return [moved_softplus2(small, g, move) for g in parts]
+    powers = [move + jnp.exp2(g) for g in parts]
+    pairs = [a * b for a, b in zip(powers[::2], powers[1::2])] + powers[len(powers) // 2 * 2:]
+    return [jnp.log2(p) for p in pairs]
 
 
 def softplus2(f):
@@ -435,22 +443,30 @@
         lax.fori_loop(0, SUBSTEPS, functools.partial(step, small), 0)
         head, rows = return_shape(cz, per)
         cloud_ref = east_ref
-        for k in range(tiles):
+        early = [None] * tiles
+
+        def sums(k):
             for z in range(cz):
                 total = cloud = None
                 move = row_at(scale_ref if small else shift_ref, z, k)
+                for c in moved_sum(small, get(k, z), move):
+                    cloud = c if cloud is None else cloud + c
                 for f in get(k, z):
-                    c = moved_softplus2(small, f, move)
                     total = f if total is None else total + f
-                    cloud = c if cloud is None else cloud + c
                 part_ref[2 * k, pl.ds(z * SUB, SUB), :] = total
                 part_ref[2 * k + 1, pl.ds(z * SUB, SUB), :] = cloud
-            early = dot3(
+
+        def known(k):
+            early[k] = dot3(
                 split(value_ref[:, lanes(k)]), (early_high_ref[...], early_low_ref[...]), 0, 0
             )
-            if carry and k == 0:
+
+        def ends_part():
+            if carry:
                 halo = halo_part(devices, r_ref, ends_ref, v_ref)
                 halo_ref[...] = halo + dot(gain_ref[...], halo, 1, 0, HI)
+
+        def close(k):
             moved = LN2 * shift_ref[:, lanes(k)]
             end = fold(part_ref.at[2 * k], zp, LN2 / cx) - moved
             cloud = fold(part_ref.at[2 * k + 1], zp, LN2 / cx) - moved
@@ -458,14 +474,23 @@
             late_ref[zp:, lanes(k)] = cloud[0:head]
             cloud_ref[:, lanes(k)] = cloud
             late = dot3(split(late_ref[:, lanes(k)]), (late_high_ref[...], late_low_ref[...]), 0, 0)
-            main = early + late
+            main = early[k] + late
             for h in range(LANE // per):
                 out_ref[pl.ds((k * (LANE // per) + h) * rows, per), :] = main[h * per:(h + 1) * per]
+
+        for k in range(tiles):
+            sums(k)
+            if k == 0:
+                for n in range(tiles):
+                    known(n)
+            if k == 1:
+                ends_part()
+            close(k)
         left = cloud_ref[head:, :]
         left = jnp.concatenate([left, jnp.zeros((SLOT - left.shape[0], cols), jnp.float32)], axis=0) \
             if left.shape[0] < SLOT else left
         place = lax.broadcasted_iota(jnp.int32, (1, cols), 1)
-        part = place % SLOTS
+        part = place % per % SLOTS
         spread = jnp.concatenate(
             [jnp.where(part == j, left, 0.0) for j in range(SLOTS)], axis=0
         )

time: 41.1 us -> 41.9 us (1.019); the launches traced: 40.8 us -> 42.4 us
  blocking collectives: 11.3 us -> 13 us
    all_to_all x1, blocking collectives: 11.3 us -> 13 us  [exchange(): lax.all_to_all(blocks, AXES, split_axis=0, concat_axis=0, tiled=True)]
  transfers between devices with their start and end apart: 1 -> 1, of which waited for: 1 -> 1; matrix products, arithmetic and copies ran while one was open for 0% -> 0% of each run, Pallas kernels for 10% -> 9%
where the time goes in v8:
time: 41.9 us; the launch traced here: 42.4 us
  Pallas kernels  15 us (36%)
  blocking collectives  13 us (31%)
  starting transfers between devices  7.33 us (17%)
  waiting for transfers between devices  6.26 us (15%)
  between operations  0.75 us (2%)
    all_to_all x1, blocking collectives, exchange(): lax.all_to_all(blocks, AXES, split_axis=0, concat_axis=0, tiled=True)  13 us
    pallas_call x1, Pallas kernels, local(): pl.pallas_call(functools.partial(cloud_kernel, devices, carry, nl), out_s...  7.7 us
    all_to_all x1, starting transfers between devices, exchange(): lax.all_to_all(blocks, AXES, split_axis=0, concat_axis=0, tiled=True)  7.33 us
    all_to_all x1, waiting for transfers between devices, exchange(): lax.all_to_all(blocks, AXES, split_axis=0, concat_axis=0, tiled=True)  6.26 us
    pallas_call x1, Pallas kernels, local(): pl.pallas_call(functools.partial(pack_kernel, devices, carry), out_shape=...  2.14 us
    pallas_call x1, Pallas kernels, local(): pl.pallas_call(functools.partial(prep_kernel, carry), out_shape=(jax.Shap...  2.05 us
    pallas_call x1, Pallas kernels, local(): pl.pallas_call(functools.partial(base_kernel, devices, carry), out_shape=...  1.9 us
    pallas_call x1, Pallas kernels, local(): pl.pallas_call(functools.partial(finish_kernel, devices, carry), out_shap...  1.24 us
  transfers between devices with their start and end apart: 1, of which 1 were waited for; matrix products, arithmetic and copies ran while one was open for 0% of the time, Pallas kernels for 9%

profile of v8, /device:TPU:0, one launch (start us, length us, event | category | flops | bytes accessed | tf_op | source)
XLA Modules:
  0.0 42.4 jit_solution(2305233141833891456)
XLA Ops:
  0.6 0.0 copy-start.3
  0.6 0.0 copy-start.4
  0.7 0.0 copy-start.1
  0.7 0.0 copy-start.2
  0.7 0.0 copy-start.5
  0.7 0.0 copy-start
  0.7 2.1 %pack.1 = (f32[256,256]{1,0:T(8,128)}, s32[1,256]{1,0:T(1,128)S(1)}) custom-call(f32[72,256]{1,0:T(8,128)} %refs_0_.4, f32[72,256]{1,0:T(8,128)} %refs_1_.4, f32[72,256]{1,0:T(8,128)} %refs_0_.5, s32[1,256]{1,0:T(1,128)} %bitcast.9), custom_call_target="tpu_custom_call" | custom-call | tf_op jit(solution)/shard_map/pack/pallas_call | solution.py:663
  2.8 7.3 %all-to-all-start = ((f32[32,8,256]{2,1,0:T(8,128)}), f32[32,8,256]{2,1,0:T(8,128)S(1)}, u32[]{:S(2)}, u32[]{:S(2)}) async-start(f32[32,8,256]{2,1,0:T(8,128)} %bitcast.1), calls=%async_computation | async-start | bytes 524288 | tf_op jit(solution)/shard_map/all_to_all | solution.py:686
  10.2 1.9 %base.1 = (f32[72,256]{1,0:T(8,128)S(1)}, f32[72,256]{1,0:T(8,128)S(1)}, bf16[216,128]{1,0:T(8,128)(2,1)S(1)}, bf16[216,128]{1,0:T(8,128)(2,1)S(1)}, bf16[72,32]...) custom-call(f32[72,256]{1,0:T(8,128)} %refs_0_.4, ...), custom_call_target="tpu_custom_call" | custom-call | flops 100000000 | bytes 1000000 | tf_op jit(solution)/shard_map/base/pallas_call | solution.py:738
  12.1 2.1 %prep.1 = (f32[2,50,32,128]{3,2,1,0:T(8,128)S(1)}, f32[56,256]{1,0:T(8,128)S(1)}, f32[8,128]{1,0:T(8,128)S(1)}, bf16[280,256]{1,0:T(8,128)(2,1)S(1)}, bf16[168,2...) custom-call(f32[50,32,256]{2,1,0:T(8,128)} %td_ref.1, f32[50,72]{1,0:T(8,128)} %refs_3_.1, ...), custom_call_target="tpu_custom_call" | custom-call | flops 100000000 | bytes 4000000 | tf_op jit(solution)/shard_map/prep/pallas_call | solution.py:707
  14.2 6.3 %all-to-all-done = f32[32,8,256]{2,1,0:T(8,128)S(1)} async-done(((f32[32,8,256]{2,1,0:T(8,128)}), f32[32,8,256]{2,1,0:T(8,128)S(1)}, u32[]{:S(2)}, u32[]{:S(2)}) %all-to-all-start) | async-done | bytes 262176 | tf_op jit(solution)/shard_map/all_to_all | solution.py:686
  20.4 0.0 copy-done.3
  20.4 0.0 copy-done.4
  20.4 0.0 copy-done.1
  20.4 0.0 copy-done.2
  20.4 0.0 copy-done.5
  20.4 0.0 copy-done
  20.5 7.7 %cloud.1 = (f32[320,128]{1,0:T(8,128)S(1)}, f32[72,128]{1,0:T(8,128)S(1)}) custom-call(f32[256,256]{1,0:T(8,128)S(1)} %bitcast.6, f32[2,50,32,128]{3,2,1,0:T(8,128)S(1)} %get-tuple-element.25.start_ref, f32[56,256]{1,0:T(8,128)S(1)} %get-tuple-element.26.td_mean_ref, f32[8,128]{1,0:T(8,128)S(1)} %get-tuple-element.27.most_ref, ...), custom_call_target="tpu_custom_call" | custom-call | tf_op jit(solution)/shard_map/cloud/pallas_call | solution.py:779
  28.2 13.0 %all_to_all.10 = f32[32,1,1280]{2,1,0:T(1,128)S(1)} all-to-all(f32[32,1,1280]{2,1,0:T(1,128)S(1)} %bitcast.8), channel_id=1, replica_groups=mesh['tile'=8,'crm'=4] {'tile','crm'}, dimensions={0} | all-to-all | bytes 327680 | tf_op jit(solution)/shard_map/all_to_all | solution.py:686
  41.2 1.2 %finish.1 = (f32[72,256]{1,0:T(8,128)}, f32[72,256]{1,0:T(8,128)}, f32[72,256]{1,0:T(8,128)}) custom-call(f32[320,128]{1,0:T(8,128)S(1)} %bitcast.7, s32[1,256]{1,0:T(1,128)S(1)} %get-tuple-element.24.after_ref.refs_6_.refs_1_, f32[72,256]{1,0:T(8,128)S(1)} %get-tuple-element.34.refs_2_, f32[72,256]{1,0:T(8,128)S(1)} %get-tuple-element.35.refs_3_, ...), custom_call_target="tpu_custom_call" | custom-call | tf_op jit(solution)/shard_map/finish/pallas_call | solution.py:800
Async XLA Ops:
  0.6 19.8 %copy-start.3 = (bf16[80,128]{1,0:T(8,128)(2,1)S(1)}, bf16[80,128]{1,0:T(8,128)(2,1)}, u32[]{:S(2)}) copy-start(bf16[80,128]{1,0:T(8,128)(2,1)} %constant.20.clone.late_low_ref) | copy-start | bytes 61444
  0.6 19.8 %copy-start.4 = (bf16[80,128]{1,0:T(8,128)(2,1)S(1)}, bf16[80,128]{1,0:T(8,128)(2,1)}, u32[]{:S(2)}) copy-start(bf16[80,128]{1,0:T(8,128)(2,1)} %constant.19.clone.late_high_ref) | copy-start | bytes 61444
  0.7 19.8 %copy-start.1 = (bf16[168,128]{1,0:T(8,128)(2,1)S(1)}, bf16[168,128]{1,0:T(8,128)(2,1)}, u32[]{:S(2)}) copy-start(bf16[168,128]{1,0:T(8,128)(2,1)} %constant.18.clone.early_low_ref) | copy-start | bytes 129028
  0.7 19.8 %copy-start.2 = (bf16[168,128]{1,0:T(8,128)(2,1)S(1)}, bf16[168,128]{1,0:T(8,128)(2,1)}, u32[]{:S(2)}) copy-start(bf16[168,128]{1,0:T(8,128)(2,1)} %constant.17.clone.early_high_ref) | copy-start | bytes 129028
  0.7 19.8 %copy-start.5 = (bf16[16,256]{1,0:T(8,128)(2,1)S(1)}, bf16[16,256]{1,0:T(8,128)(2,1)}, u32[]{:S(2)}) copy-start(bf16[16,256]{1,0:T(8,128)(2,1)} %constant.16.clone.refs_1_) | copy-start | bytes 24580
  0.7 19.8 %copy-start = (f32[72,256]{1,0:T(8,128)S(1)}, f32[72,256]{1,0:T(8,128)}, u32[]{:S(2)}) copy-start(f32[72,256]{1,0:T(8,128)} %refs_0_.5) | copy-start | bytes 221188
  2.8 17.6 %all-to-all-start = ((f32[32,8,256]{2,1,0:T(8,128)}), f32[32,8,256]{2,1,0:T(8,128)S(1)}, u32[]{:S(2)}, u32[]{:S(2)}) async-start(f32[32,8,256]{2,1,0:T(8,128)} %bitcast.1), calls=%async_computation | async-start | bytes 524288 | tf_op jit(solution)/shard_map/all_to_all | solution.py:686

commit v9 on v8

--- a/solution.py
+++ b/solution.py
@@ -512,7 +512,7 @@
 def base_kernel(devices, carry, *refs):
     pos_ref = refs[6]
     low_ref, high_ref = (None, None) if carry else refs[7:9]
-    to_ref, qo_ref, level_high_ref, level_low_ref, rest_high_ref, rest_low_ref = refs[-16:-10]
+    to_ref, qo_ref, level_high_ref, level_low_ref = refs[-14:-10]
     sel_ref, pick_ref, gain_ref = refs[-10:-7]
     t_ref, q_ref, v_ref, down_ref, up_ref, lin_ref, sem = refs[-7:]
     copies = fetch(refs[:6], refs[-7:-1], sem)
@@ -535,9 +535,9 @@
         ],
         axis=0,
     )
-    level_high_ref[...], level_low_ref[...] = split(level)
-    rest = jnp.where(lane < SLOT, pltpu.roll(wide, LANE - head, 1), 0.0)
-    rest_high_ref[...], rest_low_ref[...] = split(rest[:, 0:SLOT])
+    rest = jnp.where(lane < SLOT, pltpu.roll(wide, LANE - head, 1), 0.0)[:, 0:SLOT]
+    rest = jnp.concatenate([jnp.zeros((2 * nl, SLOT), jnp.float32), rest], axis=0)
+    level_high_ref[...], level_low_ref[...] = split(jnp.concatenate([level, rest], axis=1))
     if carry:
         low = high = (jnp.zeros((nl, 1), jnp.float32),) * 2
     else:
@@ -610,12 +610,14 @@
 
 def finish_kernel(devices, carry, *refs):
     r_ref, pos_ref, tb_ref, qb_ref = refs[:4]
-    level_high_ref, level_low_ref, rest_high_ref, rest_low_ref, sel_ref, pick_ref = refs[4:10]
+    level_high_ref, level_low_ref, sel_ref, pick_ref = refs[4:8]
     to_ref, qo_ref, co_ref = refs[-3:]
     nl, cols = tb_ref.shape
     per = cols // devices
     rows = r_ref.shape[0] // devices
     main = jnp.concatenate([r_ref[pl.ds(h * rows, per), :] for h in range(devices)], axis=0)
+    a, b = split(main)
+    values = dot(a, sel_ref[...], 0, 0) + dot(b, sel_ref[...], 0, 0)
     extra = jnp.concatenate(
         [r_ref[pl.ds(per + i, devices, stride=rows), :] for i in range(rows - per)], axis=0
     )
@@ -625,17 +627,16 @@
     left = jnp.where(part == 0, extra[:SLOT], 0.0)
     for j in range(1, SLOTS):
         left = left + jnp.where(part == j, extra[j * SLOT:(j + 1) * SLOT], 0.0)
-    rest = dot3((rest_high_ref[...], rest_low_ref[...]), split(left), 1, 0)
-    a, b = split(dot3((level_high_ref[...], level_low_ref[...]), split(main), 1, 1))
-    out = dot(a, sel_ref[...], 1, 0) + dot(b, sel_ref[...], 1, 0)
+    values = split(jnp.concatenate([values, left], axis=0))
+    out = dot3((level_high_ref[...], level_low_ref[...]), values, 1, 0)
     if carry:
-        halo = refs[10][...]
+        halo = refs[8][...]
         add_ends(tb_ref, to_ref, out[0:nl], halo, 0)
         add_ends(qb_ref, qo_ref, out[nl:2 * nl], halo, 2)
     else:
         to_ref[...] = tb_ref[...] + out[0:nl]
         qo_ref[...] = qb_ref[...] + out[nl:2 * nl]
-    co_ref[...] = out[2 * nl:3 * nl] + rest
+    co_ref[...] = out[2 * nl:3 * nl]
 
 
 def local(
@@ -740,16 +741,14 @@
         out_shape=(
             field,
             field,
-            jax.ShapeDtypeStruct((3 * nl, LANE), bf16),
-            jax.ShapeDtypeStruct((3 * nl, LANE), bf16),
-            jax.ShapeDtypeStruct((nl, SLOT), bf16),
-            jax.ShapeDtypeStruct((nl, SLOT), bf16),
+            jax.ShapeDtypeStruct((3 * nl, LANE + SLOT), bf16),
+            jax.ShapeDtypeStruct((3 * nl, LANE + SLOT), bf16),
             jax.ShapeDtypeStruct((cols, cols), bf16),
             jax.ShapeDtypeStruct((devices * (rows - per), cols), bf16),
             jax.ShapeDtypeStruct((nl, nl), f32),
         ),
         in_specs=[HBM] * 6 + [VMEM] * (1 + len(ends)),
-        out_specs=(VMEM,) * 9,
+        out_specs=(VMEM,) * 7,
         scratch_shapes=[
             pltpu.VMEM((nl, cols), f32),
             pltpu.VMEM((nl, cols), f32),
@@ -800,7 +799,7 @@
     return pl.pallas_call(
         functools.partial(finish_kernel, devices, carry),
         out_shape=(field,) * 3,
-        in_specs=[VMEM] * (10 + len(halo)),
+        in_specs=[VMEM] * (8 + len(halo)),
         out_specs=(VMEM,) * 3,
         compiler_params=pltpu.CompilerParams(vmem_limit_bytes=VMEM_PACK),
         name="finish",

time: 41.9 us -> 42.8 us (1.021); the launches traced: 42.4 us -> 42.1 us
  no operation moved by 1% of the time
where the time goes in v9:
time: 42.8 us; the launch traced here: 42.1 us
  Pallas kernels  15 us (35%)
  blocking collectives  12.8 us (30%)
  starting transfers between devices  7.33 us (17%)
  waiting for transfers between devices  6.26 us (15%)
  between operations  0.75 us (2%)
    all_to_all x1, blocking collectives, exchange(): lax.all_to_all(blocks, AXES, split_axis=0, concat_axis=0, tiled=True)  12.8 us
    pallas_call x1, Pallas kernels, local(): pl.pallas_call(functools.partial(cloud_kernel, devices, carry, nl), out_s...  7.7 us
    all_to_all x1, starting transfers between devices, exchange(): lax.all_to_all(blocks, AXES, split_axis=0, concat_axis=0, tiled=True)  7.33 us
    all_to_all x1, waiting for transfers between devices, exchange(): lax.all_to_all(blocks, AXES, split_axis=0, concat_axis=0, tiled=True)  6.26 us
    pallas_call x1, Pallas kernels, local(): pl.pallas_call(functools.partial(pack_kernel, devices, carry), out_shape=...  2.14 us
    pallas_call x1, Pallas kernels, local(): pl.pallas_call(functools.partial(prep_kernel, carry), out_shape=(jax.Shap...  2.05 us
    pallas_call x1, Pallas kernels, local(): pl.pallas_call(functools.partial(base_kernel, devices, carry), out_shape=...  1.9 us
    pallas_call x1, Pallas kernels, local(): pl.pallas_call(functools.partial(finish_kernel, devices, carry), out_shap...  1.17 us
  transfers between devices with their start and end apart: 1, of which 1 were waited for; matrix products, arithmetic and copies ran while one was open for 0% of the time, Pallas kernels for 9%

profile of v9, /device:TPU:0, one launch (start us, length us, event | category | flops | bytes accessed | tf_op | source)
XLA Modules:
  0.0 42.1 jit_solution(3138242431814711486)
XLA Ops:
  0.6 0.0 copy-start.3
  0.6 0.0 copy-start.4
  0.7 0.0 copy-start.1
  0.7 0.0 copy-start.2
  0.7 0.0 copy-start.5
  0.7 0.0 copy-start
  0.7 2.1 %pack.1 = (f32[256,256]{1,0:T(8,128)}, s32[1,256]{1,0:T(1,128)S(1)}) custom-call(f32[72,256]{1,0:T(8,128)} %refs_0_.4, f32[72,256]{1,0:T(8,128)} %refs_1_.4, f32[72,256]{1,0:T(8,128)} %refs_0_.5, s32[1,256]{1,0:T(1,128)} %bitcast.9), custom_call_target="tpu_custom_call" | custom-call | tf_op jit(solution)/shard_map/pack/pallas_call | solution.py:664
  2.8 7.3 %all-to-all-start = ((f32[32,8,256]{2,1,0:T(8,128)}), f32[32,8,256]{2,1,0:T(8,128)S(1)}, u32[]{:S(2)}, u32[]{:S(2)}) async-start(f32[32,8,256]{2,1,0:T(8,128)} %bitcast.1), calls=%async_computation | async-start | bytes 524288 | tf_op jit(solution)/shard_map/all_to_all | solution.py:687
  10.2 1.9 %base.1 = (f32[72,256]{1,0:T(8,128)S(1)}, f32[72,256]{1,0:T(8,128)S(1)}, bf16[216,160]{1,0:T(8,128)(2,1)S(1)}, bf16[216,160]{1,0:T(8,128)(2,1)S(1)}, bf16[256,25...) custom-call(f32[72,256]{1,0:T(8,128)} %refs_0_.4, f32[72,256]{1,0:T(8,128)} %refs_1_.4, ...), custom_call_target="tpu_custom_call" | custom-call | flops 100000000 | bytes 1000000 | tf_op jit(solution)/shard_map/base/pallas_call | solution.py:739
  12.1 2.1 %prep.1 = (f32[2,50,32,128]{3,2,1,0:T(8,128)S(1)}, f32[56,256]{1,0:T(8,128)S(1)}, f32[8,128]{1,0:T(8,128)S(1)}, bf16[280,256]{1,0:T(8,128)(2,1)S(1)}, bf16[168,2...) custom-call(f32[50,32,256]{2,1,0:T(8,128)} %td_ref.1, f32[50,72]{1,0:T(8,128)} %refs_3_.1, ...), custom_call_target="tpu_custom_call" | custom-call | flops 100000000 | bytes 4000000 | tf_op jit(solution)/shard_map/prep/pallas_call | solution.py:708
  14.2 6.3 %all-to-all-done = f32[32,8,256]{2,1,0:T(8,128)S(1)} async-done(((f32[32,8,256]{2,1,0:T(8,128)}), f32[32,8,256]{2,1,0:T(8,128)S(1)}, u32[]{:S(2)}, u32[]{:S(2)}) %all-to-all-start) | async-done | bytes 262176 | tf_op jit(solution)/shard_map/all_to_all | solution.py:687
  20.4 0.0 copy-done.3
  20.4 0.0 copy-done.4
  20.4 0.0 copy-done.1
  20.4 0.0 copy-done.2
  20.4 0.0 copy-done.5
  20.4 0.0 copy-done
  20.5 7.7 %cloud.1 = (f32[320,128]{1,0:T(8,128)S(1)}, f32[72,128]{1,0:T(8,128)S(1)}) custom-call(f32[256,256]{1,0:T(8,128)S(1)} %bitcast.6, f32[2,50,32,128]{3,2,1,0:T(8,128)S(1)} %get-tuple-element.23.start_ref, f32[56,256]{1,0:T(8,128)S(1)} %get-tuple-element.24.td_mean_ref, f32[8,128]{1,0:T(8,128)S(1)} %get-tuple-element.25.most_ref, ...), custom_call_target="tpu_custom_call" | custom-call | tf_op jit(solution)/shard_map/cloud/pallas_call | solution.py:778
  28.2 12.8 %all_to_all.10 = f32[32,1,1280]{2,1,0:T(1,128)S(1)} all-to-all(f32[32,1,1280]{2,1,0:T(1,128)S(1)} %bitcast.8), channel_id=1, replica_groups=mesh['tile'=8,'crm'=4] {'tile','crm'}, dimensions={0} | all-to-all | bytes 327680 | tf_op jit(solution)/shard_map/all_to_all | solution.py:687
  40.9 1.2 %finish.1 = (f32[72,256]{1,0:T(8,128)}, f32[72,256]{1,0:T(8,128)}, f32[72,256]{1,0:T(8,128)}) custom-call(f32[320,128]{1,0:T(8,128)S(1)} %bitcast.7, s32[1,256]{1,0:T(1,128)S(1)} %get-tuple-element.22.after_ref.refs_6_.refs_1_, f32[72,256]{1,0:T(8,128)S(1)} %get-tuple-element.32.refs_2_, f32[72,256]{1,0:T(8,128)S(1)} %get-tuple-element.33.refs_3_, ...), custom_call_target="tpu_custom_call" | custom-call | tf_op jit(solution)/shard_map/finish/pallas_call | solution.py:799
Async XLA Ops:
  0.6 19.8 %copy-start.3 = (bf16[80,128]{1,0:T(8,128)(2,1)S(1)}, bf16[80,128]{1,0:T(8,128)(2,1)}, u32[]{:S(2)}) copy-start(bf16[80,128]{1,0:T(8,128)(2,1)} %constant.20.clone.late_low_ref) | copy-start | bytes 61444
  0.6 19.8 %copy-start.4 = (bf16[80,128]{1,0:T(8,128)(2,1)S(1)}, bf16[80,128]{1,0:T(8,128)(2,1)}, u32[]{:S(2)}) copy-start(bf16[80,128]{1,0:T(8,128)(2,1)} %constant.19.clone.late_high_ref) | copy-start | bytes 61444
  0.7 19.8 %copy-start.1 = (bf16[168,128]{1,0:T(8,128)(2,1)S(1)}, bf16[168,128]{1,0:T(8,128)(2,1)}, u32[]{:S(2)}) copy-start(bf16[168,128]{1,0:T(8,128)(2,1)} %constant.18.clone.early_low_ref) | copy-start | bytes 129028
  0.7 19.8 %copy-start.2 = (bf16[168,128]{1,0:T(8,128)(2,1)S(1)}, bf16[168,128]{1,0:T(8,128)(2,1)}, u32[]{:S(2)}) copy-start(bf16[168,128]{1,0:T(8,128)(2,1)} %constant.17.clone.early_high_ref) | copy-start | bytes 129028
  0.7 19.8 %copy-start.5 = (bf16[16,256]{1,0:T(8,128)(2,1)S(1)}, bf16[16,256]{1,0:T(8,128)(2,1)}, u32[]{:S(2)}) copy-start(bf16[16,256]{1,0:T(8,128)(2,1)} %constant.16.clone.refs_1_) | copy-start | bytes 24580
  0.7 19.8 %copy-start = (f32[72,256]{1,0:T(8,128)S(1)}, f32[72,256]{1,0:T(8,128)}, u32[]{:S(2)}) copy-start(f32[72,256]{1,0:T(8,128)} %refs_0_.5) | copy-start | bytes 221188
  2.8 17.6 %all-to-all-start = ((f32[32,8,256]{2,1,0:T(8,128)}), f32[32,8,256]{2,1,0:T(8,128)S(1)}, u32[]{:S(2)}, u32[]{:S(2)}) async-start(f32[32,8,256]{2,1,0:T(8,128)} %bitcast.1), calls=%async_computation | async-start | bytes 524288 | tf_op jit(solution)/shard_map/all_to_all | solution.py:687

commit v10 on v9

--- a/solution.py
+++ b/solution.py
@@ -204,25 +204,30 @@
             (lane == 0) | (lane == cols - 1), 1.0, 0.0
         )
     a, b = split(s_ref[...])
-    out = dot(sel, a, 1, 1) + dot(sel, b, 1, 1)
     if carry:
-        fill = jnp.zeros((first - second, cols), jnp.float32)
-        parts = []
-        for f in (x, t):
-            parts += [f[:first], jnp.concatenate([f[first:], fill], axis=0)]
-        parts = jnp.concatenate(parts, axis=1)
-        shape = (SUB, parts.shape[1])
-        want = jnp.full(shape, -1, jnp.int32)
+        shape = (SUB, cols)
         row = lax.broadcasted_iota(jnp.int32, shape, 0)
-        for r, (field, half, end) in enumerate(CARRIED):
-            want = jnp.where(row == r, (2 * field + half) * cols + end * (cols - 1), want)
+        want = jnp.zeros(shape, jnp.int32)
+        for r, (_, _, end) in enumerate(CARRIED):
+            want = jnp.where(row == r, end * (cols - 1), want)
         pick = jnp.where(lax.broadcasted_iota(jnp.int32, shape, 1) == want, 1.0, 0.0).astype(
             jnp.bfloat16
         )
-        a, b = split(parts)
-        ends = dot(pick, a, 1, 1) + dot(pick, b, 1, 1)
-        ends = jnp.concatenate([ends, jnp.zeros((SUB, width - first), jnp.float32)], axis=1)
-        ends = pltpu.roll(ends, 3 * nl, 1)
+        row = lax.broadcasted_iota(jnp.int32, (SUB, width), 0)
+        lane = lax.broadcasted_iota(jnp.int32, (SUB, width), 1)
+        ends = jnp.zeros((SUB, width), jnp.float32)
+        for field, terms in enumerate(((a[:nl], b[:nl]), split(t))):
+            found = dot(pick, terms[0], 1, 1) + dot(pick, terms[1], 1, 1)
+            found = jnp.concatenate([found, jnp.zeros((SUB, width - nl), jnp.float32)], axis=1)
+            for half, (start, size) in enumerate(((0, first), (first, second))):
+                mine = functools.reduce(
+                    jnp.logical_or,
+                    [row == r for r, c in enumerate(CARRIED) if c[:2] == (field, half)],
+                )
+                mine = mine & (lane >= 3 * nl) & (lane < 3 * nl + size)
+                ends = jnp.where(mine, pltpu.roll(found, 3 * nl - start, 1), ends)
+    out = dot(sel, a, 1, 1) + dot(sel, b, 1, 1)
+    if carry:
         out = (out.reshape(devices, per, width) + ends[None]).reshape(cols, width)
     out_ref[...] = out
 

time: 42.8 us -> 42.7 us (level)
  no operation moved by 1% of the time
where the time goes in v10:
time: 42.7 us; the launch traced here: 41.8 us
  Pallas kernels  14.9 us (35%)
  blocking collectives  12.5 us (29%)
  starting transfers between devices  7.33 us (17%)
  waiting for transfers between devices  6.26 us (15%)
  between operations  0.75 us (2%)
    all_to_all x1, blocking collectives, exchange(): lax.all_to_all(blocks, AXES, split_axis=0, concat_axis=0, tiled=True)  12.5 us
    pallas_call x1, Pallas kernels, local(): pl.pallas_call(functools.partial(cloud_kernel, devices, carry, nl), out_s...  7.7 us
    all_to_all x1, starting transfers between devices, exchange(): lax.all_to_all(blocks, AXES, split_axis=0, concat_axis=0, tiled=True)  7.33 us
    all_to_all x1, waiting for transfers between devices, exchange(): lax.all_to_all(blocks, AXES, split_axis=0, concat_axis=0, tiled=True)  6.26 us
    pallas_call x1, Pallas kernels, local(): pl.pallas_call(functools.partial(pack_kernel, devices, carry), out_shape=...  2.1 us
    pallas_call x1, Pallas kernels, local(): pl.pallas_call(functools.partial(prep_kernel, carry), out_shape=(jax.Shap...  2.05 us
    pallas_call x1, Pallas kernels, local(): pl.pallas_call(functools.partial(base_kernel, devices, carry), out_shape=...  1.89 us
    pallas_call x1, Pallas kernels, local(): pl.pallas_call(functools.partial(finish_kernel, devices, carry), out_shap...  1.17 us
  transfers between devices with their start and end apart: 1, of which 1 were waited for; matrix products, arithmetic and copies ran while one was open for 0% of the time, Pallas kernels for 9%

profile of v10, /device:TPU:0, one launch (start us, length us, event | category | flops | bytes accessed | tf_op | source)
XLA Modules:
  0.0 41.8 jit_solution(9015729019075843595)
XLA Ops:
  0.6 0.0 copy-start.3
  0.6 0.0 copy-start.4
  0.7 0.0 copy-start.1
  0.7 0.0 copy-start.2
  0.7 0.0 copy-start.5
  0.7 0.0 copy-start
  0.7 2.1 %pack.1 = (f32[256,256]{1,0:T(8,128)}, s32[1,256]{1,0:T(1,128)S(1)}) custom-call(f32[72,256]{1,0:T(8,128)} %refs_0_.4, f32[72,256]{1,0:T(8,128)} %refs_1_.4, f32[72,256]{1,0:T(8,128)} %refs_0_.5, s32[1,256]{1,0:T(1,128)} %bitcast.9), custom_call_target="tpu_custom_call" | custom-call | tf_op jit(solution)/shard_map/pack/pallas_call | solution.py:669
  2.8 7.3 %all-to-all-start = ((f32[32,8,256]{2,1,0:T(8,128)}), f32[32,8,256]{2,1,0:T(8,128)S(1)}, u32[]{:S(2)}, u32[]{:S(2)}) async-start(f32[32,8,256]{2,1,0:T(8,128)} %bitcast.1), calls=%async_computation | async-start | bytes 524288 | tf_op jit(solution)/shard_map/all_to_all | solution.py:692
  10.2 1.9 %base.1 = (f32[72,256]{1,0:T(8,128)S(1)}, f32[72,256]{1,0:T(8,128)S(1)}, bf16[216,160]{1,0:T(8,128)(2,1)S(1)}, bf16[216,160]{1,0:T(8,128)(2,1)S(1)}, bf16[256,25...) custom-call(f32[72,256]{1,0:T(8,128)} %refs_0_.4, f32[72,256]{1,0:T(8,128)} %refs_1_.4, ...), custom_call_target="tpu_custom_call" | custom-call | flops 100000000 | bytes 1000000 | tf_op jit(solution)/shard_map/base/pallas_call | solution.py:744
  12.1 2.1 %prep.1 = (f32[2,50,32,128]{3,2,1,0:T(8,128)S(1)}, f32[56,256]{1,0:T(8,128)S(1)}, f32[8,128]{1,0:T(8,128)S(1)}, bf16[280,256]{1,0:T(8,128)(2,1)S(1)}, bf16[168,2...) custom-call(f32[50,32,256]{2,1,0:T(8,128)} %td_ref.1, f32[50,72]{1,0:T(8,128)} %refs_3_.1, ...), custom_call_target="tpu_custom_call" | custom-call | flops 100000000 | bytes 4000000 | tf_op jit(solution)/shard_map/prep/pallas_call | solution.py:713
  14.1 6.3 %all-to-all-done = f32[32,8,256]{2,1,0:T(8,128)S(1)} async-done(((f32[32,8,256]{2,1,0:T(8,128)}), f32[32,8,256]{2,1,0:T(8,128)S(1)}, u32[]{:S(2)}, u32[]{:S(2)}) %all-to-all-start) | async-done | bytes 262176 | tf_op jit(solution)/shard_map/all_to_all | solution.py:692
  20.4 0.0 copy-done.3
  20.4 0.0 copy-done.4
  20.4 0.0 copy-done.1
  20.4 0.0 copy-done.2
  20.4 0.0 copy-done.5
  20.4 0.0 copy-done
  20.4 7.7 %cloud.1 = (f32[320,128]{1,0:T(8,128)S(1)}, f32[72,128]{1,0:T(8,128)S(1)}) custom-call(f32[256,256]{1,0:T(8,128)S(1)} %bitcast.6, f32[2,50,32,128]{3,2,1,0:T(8,128)S(1)} %get-tuple-element.23.start_ref, f32[56,256]{1,0:T(8,128)S(1)} %get-tuple-element.24.td_mean_ref, f32[8,128]{1,0:T(8,128)S(1)} %get-tuple-element.25.most_ref, ...), custom_call_target="tpu_custom_call" | custom-call | tf_op jit(solution)/shard_map/cloud/pallas_call | solution.py:783
  28.1 12.5 %all_to_all.10 = f32[32,1,1280]{2,1,0:T(1,128)S(1)} all-to-all(f32[32,1,1280]{2,1,0:T(1,128)S(1)} %bitcast.8), channel_id=1, replica_groups=mesh['tile'=8,'crm'=4] {'tile','crm'}, dimensions={0} | all-to-all | bytes 327680 | tf_op jit(solution)/shard_map/all_to_all | solution.py:692
  40.7 1.2 %finish.1 = (f32[72,256]{1,0:T(8,128)}, f32[72,256]{1,0:T(8,128)}, f32[72,256]{1,0:T(8,128)}) custom-call(f32[320,128]{1,0:T(8,128)S(1)} %bitcast.7, s32[1,256]{1,0:T(1,128)S(1)} %get-tuple-element.22.after_ref.refs_6_.refs_1_, f32[72,256]{1,0:T(8,128)S(1)} %get-tuple-element.32.refs_2_, f32[72,256]{1,0:T(8,128)S(1)} %get-tuple-element.33.refs_3_, ...), custom_call_target="tpu_custom_call" | custom-call | tf_op jit(solution)/shard_map/finish/pallas_call | solution.py:804
Async XLA Ops:
  0.6 19.8 %copy-start.3 = (bf16[80,128]{1,0:T(8,128)(2,1)S(1)}, bf16[80,128]{1,0:T(8,128)(2,1)}, u32[]{:S(2)}) copy-start(bf16[80,128]{1,0:T(8,128)(2,1)} %constant.20.clone.late_low_ref) | copy-start | bytes 61444
  0.6 19.7 %copy-start.4 = (bf16[80,128]{1,0:T(8,128)(2,1)S(1)}, bf16[80,128]{1,0:T(8,128)(2,1)}, u32[]{:S(2)}) copy-start(bf16[80,128]{1,0:T(8,128)(2,1)} %constant.19.clone.late_high_ref) | copy-start | bytes 61444
  0.7 19.7 %copy-start.1 = (bf16[168,128]{1,0:T(8,128)(2,1)S(1)}, bf16[168,128]{1,0:T(8,128)(2,1)}, u32[]{:S(2)}) copy-start(bf16[168,128]{1,0:T(8,128)(2,1)} %constant.18.clone.early_low_ref) | copy-start | bytes 129028
  0.7 19.7 %copy-start.2 = (bf16[168,128]{1,0:T(8,128)(2,1)S(1)}, bf16[168,128]{1,0:T(8,128)(2,1)}, u32[]{:S(2)}) copy-start(bf16[168,128]{1,0:T(8,128)(2,1)} %constant.17.clone.early_high_ref) | copy-start | bytes 129028
  0.7 19.7 %copy-start.5 = (bf16[16,256]{1,0:T(8,128)(2,1)S(1)}, bf16[16,256]{1,0:T(8,128)(2,1)}, u32[]{:S(2)}) copy-start(bf16[16,256]{1,0:T(8,128)(2,1)} %constant.16.clone.refs_1_) | copy-start | bytes 24580
  0.7 19.7 %copy-start = (f32[72,256]{1,0:T(8,128)S(1)}, f32[72,256]{1,0:T(8,128)}, u32[]{:S(2)}) copy-start(f32[72,256]{1,0:T(8,128)} %refs_0_.5) | copy-start | bytes 221188
  2.8 17.6 %all-to-all-start = ((f32[32,8,256]{2,1,0:T(8,128)}), f32[32,8,256]{2,1,0:T(8,128)S(1)}, u32[]{:S(2)}, u32[]{:S(2)}) async-start(f32[32,8,256]{2,1,0:T(8,128)} %bitcast.1), calls=%async_computation | async-start | bytes 524288 | tf_op jit(solution)/shard_map/all_to_all | solution.py:692
